TPU v7x, 32 devices: a whole 2x2x4 slice. The times are simulated.
32 devices in a mesh: groups: 2 (over x), row: 16 (over z, y, core).
Axes of the slice: x: 2, y: 2, z: 4, core: 2. Of those that a mesh axis runs over, the one named last changes fastest.
Arguments:
- obj_field: float32 [2, 2, 8192, 1024], P(None, None, ('groups', 'row')), parts along dimension 2, may hold values from -4.2 to 4.2
- probe_wave: float32 [4, 256, 256], P('groups'), parts along dimension 0, may hold values from -4.2 to 4.2
- prop_phase: float32 [256, 256], replicated, may hold values from -3.140625 to 3.140625
- win_offsets: int32 [128, 2], P(('groups', 'row')), parts along dimension 0, may hold values from 0 to 3840, as said below
- live_counts: int32 [32], P(('groups', 'row')), parts along dimension 0, may hold values from 0 to 4, as said below
- intensity: float32 [128, 256, 256], P(('groups', 'row')), parts along dimension 0, may hold values from 0.1 to 3
Outputs:
- gradient: float32 [2, 2, 8192, 1024], P(None, None, ('groups', 'row')), parts along dimension 2
There are 2 independent parts, one for each index of `groups`. A program takes and returns all parts, laid end to end along the dimension named above; an argument that names none is the same for every part. Nothing has to cross between parts.
Inputs may be any that keep to these rules, and one draw needn't show every extreme that they name: `win_offsets`: slot j belongs to index j div 4 of row; its window's top row lies in that index's block of rows, (j div 4) * 256 to (j div 4) * 256 + 255, and never past 4096 - 256; its left column is at most 768. The used slots of an index of row are its first live_counts ones; some index has all 4 in use.
All inputs are finite; a program needn't handle non-finite values.
Results may differ from a plain program's by a relative error of at most 0.0003.
Values sent between devices are 32-bit elements; how exact they have to be, the bound alone decides.
No kernel may reach another device: no remote copies, remote signals or barrier semaphores. Data moves between devices by JAX's collectives and lax.ppermute only.
A program may use at most 128 MiB of HBM per device.

v0:
```python
import jax
import jax.numpy as jnp
from jax import lax
from jax.sharding import PartitionSpec as P


def from_behind(block, axis, distance):
    devices = range(lax.axis_size(axis))
    route = [(i - distance, i) for i in devices if i - distance in devices]
    return lax.ppermute(block, axis, route)


def dft_tables(extent):
    indices = jnp.arange(extent, dtype=jnp.int32)
    phase_idx = indices[:, None] * indices[None, :] % extent
    angles = phase_idx.astype(jnp.float32) * (2.0 * jnp.pi / extent)
    factor = 1.0 / jnp.sqrt(jnp.float32(extent))
    return jnp.concatenate([jnp.cos(angles) * factor, jnp.sin(angles) * factor], axis=1)


def part_of(wave, which):
    return wave[..., which, :, :]


def right_pass(wave_in, both_tables, direction):
    extent = wave_in.shape[-1]
    flat = wave_in.reshape(-1, extent)
    product = jnp.dot(flat, both_tables, precision=lax.Precision.HIGHEST)
    product = product.reshape(wave_in.shape[:-1] + (2 * extent,))
    cos_part = product[..., :extent]
    sin_part = product[..., extent:]
    return jnp.stack(
        [
            part_of(cos_part, 0) + direction * part_of(sin_part, 1),
            part_of(cos_part, 1) - direction * part_of(sin_part, 0),
        ],
        axis=-3,
    )


def transform(wave_in, both_tables, direction):
    once = right_pass(wave_in, both_tables, direction)
    twice = right_pass(jnp.swapaxes(once, -1, -2), both_tables, direction)
    return jnp.swapaxes(twice, -1, -2)


def complex_mul(left_op, right_op):
    return jnp.stack(
        [
            part_of(left_op, 0) * part_of(right_op, 0) - part_of(left_op, 1) * part_of(right_op, 1),
            part_of(left_op, 0) * part_of(right_op, 1) + part_of(left_op, 1) * part_of(right_op, 0),
        ],
        axis=-3,
    )


def conj_mul(left_op, right_op):
    return jnp.stack(
        [
            part_of(left_op, 0) * part_of(right_op, 0) + part_of(left_op, 1) * part_of(right_op, 1),
            part_of(left_op, 0) * part_of(right_op, 1) - part_of(left_op, 1) * part_of(right_op, 0),
        ],
        axis=-3,
    )


def position_gradient(tiles_at, measured, probe_in, kernel, both_tables):
    layers = tiles_at.shape[1]
    batch = tiles_at.shape[0]
    probe_many = jnp.broadcast_to(probe_in[None], (batch,) + probe_in.shape)
    entering = [probe_many]
    exit_wave = complex_mul(probe_many, tiles_at[:, 0])
    layer_at = 1
    spectrum = complex_mul(kernel[None], transform(exit_wave, both_tables, 1.0))
    entered = transform(spectrum, both_tables, -1.0)
    entering.append(entered)
    exit_wave = complex_mul(entered, tiles_at[:, layer_at])
    far_field = transform(exit_wave, both_tables, 1.0)
    power_now = part_of(far_field, 0) * part_of(far_field, 0) + part_of(far_field, 1) * part_of(
        far_field, 1
    )
    back_wave = transform((power_now - measured)[:, None] * far_field, both_tables, -1.0)
    layer_grads = [None] * layers
    for layer_at in range(layers - 1, -1, -1):
        layer_grads[layer_at] = conj_mul(entering[layer_at], back_wave)
        if layer_at > 0:
            spectrum = transform(conj_mul(tiles_at[:, layer_at], back_wave), both_tables, 1.0)
            back_wave = transform(conj_mul(kernel[None], spectrum), both_tables, -1.0)
    return jnp.stack(layer_grads, axis=1)


def run_slots(
    window, base_row, offsets_in, measures, how_many, accumulated, probe_in, kernel, both_tables
):
    layers = window.shape[0]
    extent = probe_in.shape[-1]
    tile_shape = (layers, 2, extent, extent)
    last_slot = offsets_in.shape[0] - 1
    zero_idx = jnp.int32(0)

    def corner_of(slot_idx):
        top_row = offsets_in[slot_idx, 0] - base_row
        left_col = offsets_in[slot_idx, 1]
        return (zero_idx, zero_idx, top_row, left_col)

    def visit(pair_idx, running):
        wanted = [2 * pair_idx, 2 * pair_idx + 1]
        picked = [jnp.minimum(slot_idx, last_slot) for slot_idx in wanted]
        corners = [corner_of(slot_idx) for slot_idx in picked]
        tiles_at = jnp.stack([lax.dynamic_slice(window, corner, tile_shape) for corner in corners])
        measured = jnp.stack(
            [lax.dynamic_index_in_dim(measures, slot_idx, 0, keepdims=False) for slot_idx in picked]
        )
        contrib = position_gradient(tiles_at, measured, probe_in, kernel, both_tables)
        for member in range(2):
            flag_now = (wanted[member] < how_many).astype(jnp.float32)
            previous = lax.dynamic_slice(running, corners[member], tile_shape)
            running = lax.dynamic_update_slice(
                running, previous + flag_now * contrib[member], corners[member]
            )
        return running

    return lax.fori_loop(0, (how_many + 1) // 2, visit, accumulated)


def shards(obj_field, probe_wave, prop_phase, win_offsets, live_counts, intensity):
    block_rows = obj_field.shape[2]
    extent = probe_wave.shape[-1]
    both_tables = dft_tables(extent)
    kernel = jnp.stack([jnp.cos(prop_phase), jnp.sin(prop_phase)])
    device_row = lax.axis_index("row")
    live_now = live_counts[0]
    following = from_behind(obj_field, "row", -1)
    window = jnp.concatenate([obj_field, following], axis=2)
    accumulated = jnp.zeros(window.shape, jnp.float32)
    accumulated = run_slots(
        window,
        device_row * block_rows,
        win_offsets,
        intensity,
        live_now,
        accumulated,
        probe_wave,
        kernel,
        both_tables,
    )
    spilled = from_behind(accumulated[:, :, block_rows:], "row", 1)
    return accumulated[:, :, :block_rows] + spilled


def solution(mesh):
    in_specs = (
        P(None, None, ("groups", "row"), None),
        P("groups", None, None),
        P(),
        P(("groups", "row"), None),
        P(("groups", "row")),
        P(("groups", "row"), None, None),
    )
    out_specs = P(None, None, ("groups", "row"), None)
    return jax.shard_map(shards, mesh=mesh, in_specs=in_specs, out_specs=out_specs, check_vma=False)
```

profile of v0, /device:TPU:30, one launch (start us, length us, event | category | flops | bytes accessed | tf_op | source)
XLA Modules:
  0.0 248.1 jit_solution(13540463652661266131)
XLA Ops:
  0.0 1.9 collective-permute-start
  7.4 40.8 %collective-permute-done = f32[2,2,256,1024]{3,2,1,0:T(8,128)} collective-permute-done((f32[2,2,256,1024]{3,2,1,0:T(8,128)}, f32[2,2,256,1024]{3,2,1,0:T(8,128)}, u32[]{:S(2)}, u32[]{:S(2)}) %collective-permute-start) | collective-permute-done | bytes 4194336 | tf_op jit(solution)/shard_map/ppermute | solution.py:10
  48.2 8.4 %pad_maximum_fusion.2 = f32[2,2,512,1024]{3,2,1,0:T(8,128)} fusion(f32[2,2,256,1024]{3,2,1,0:T(8,128)} %collective-permute-done, f32[2,2,256,1024]{3,2,1,0:T(8,128)} %param.8), kind=kLoop, calls=%fused_computation.162 | loop fusion | flops 2097152 | bytes 16777216 | tf_op jit(solution)/shard_map/concatenate | solution.py:134
  56.6 4.3 %broadcast_in_dim.8 = f32[2,2,512,1024]{3,2,1,0:T(8,128)} broadcast(f32[]{:T(128)} %constant.54.clone.1), dimensions={} | broadcast | bytes 8388612 | tf_op jit(solution)/shard_map/broadcast_in_dim | solution.py:135
  61.0 131.4 %while.10 = (s32[]{:T(128)}, f32[2,2,512,1024]{3,2,1,0:T(8,128)}, s32[]{:T(128)}, s32[4,2]{0,1:T(2,128)S(1)}, s32[]{:T(128)}, /*index=5*/s32[]{:T(128)}, f32[2,2...) while((s32[]{:T(128)}, f32[2,2,512,1024]{3,2,1,0:T(8,128)}, ...), condition=%wide.region_1.2_spmd, body=%wide.region_0.1_spmd.sunk | while | flops 19345833984 | bytes 154665648 | solution.py:123
  68.3 2.6 %dynamic-slice_bitcast_fusion.6 = (f32[1,2,2,256,256]{4,3,2,0,1:T(8,128)S(1)}, f32[1,2,2,256,256]{4,3,2,0,1:T(8,128)S(1)}) fusion(f32[2,2,512,1024]{3,2,1,0:T(8,128)} %get-tuple-element.377, s32[]{:T(128)S(6)} %select_n.63, s32[]{:T(128)S(6)} %select_n.64, s32[]{:T(128)S(6)} %select_n.65, s32[]{:T(128)S(6)} %select_n.66), kind=kLoop, calls=%fused_computation.71.clone.1 | loop fusion | bytes 4194320 | tf_op jit(solution)/shard_map/while/body/stack | solution.py:110
  75.3 1.9 fusion.157
  83.8 1.9 fusion.164
  85.9 1.9 fusion.166
  97.0 2.8 %fusion.174 = f32[2,2,256,256]{3,2,1,0:T(8,128)} fusion(f32[2,1,2,256,256]{4,3,2,0,1:T(8,128)S(1)} %get-tuple-element.331, f32[2,1,2,256,256]{4,3,2,0,1:T(8,128)S(1)} %get-tuple-element.332, f32[2,2,512,1024]{3,2,1,0:T(8,128)} %get-tuple-element.352, s32[]{:T(128)S(6)} %select_n.65, s32[]{:T(128)S(6)} %select_n.66, f32[]{:T(128)S(6)} %convert_element_type.21), kind=kLoop, calls=%fused_computation.8.clone.1 | loop fusion | flops 786432 | bytes 4194316 | tf_op jit(solution)/shard_map/while/body/add | solution.py:119
  99.7 12.0 %dynamic_update_slice.8 = f32[2,2,512,1024]{3,2,1,0:T(8,128)} dynamic-update-slice(f32[2,2,512,1024]{3,2,1,0:T(8,128)} %get-tuple-element.352, f32[2,2,256,256]{3,2,1,0:T(8,128)} %fusion.174, s32[]{:T(128)} %constant.53.clone.1..sunk, s32[]{:T(128)} %constant.53.clone.1..sunk, s32[]{:T(128)S(6)} %select_n.65, s32[]{:T(128)S(6)} %select_n.66) | dynamic-update-slice | bytes 2097156 | tf_op jit(solution)/shard_map/while/body/dynamic_update_slice | solution.py:118
  111.8 2.8 %fusion.175 = f32[2,2,256,256]{3,2,1,0:T(8,128)} fusion(f32[2,1,2,256,256]{4,3,2,0,1:T(8,128)S(1)} %get-tuple-element.332, f32[2,1,2,256,256]{4,3,2,0,1:T(8,128)S(1)} %get-tuple-element.331, f32[2,2,512,1024]{3,2,1,0:T(8,128)} %dynamic_update_slice.8, s32[]{:T(128)S(6)} %select_n.63, s32[]{:T(128)S(6)} %select_n.64, f32[]{:T(128)S(6)} %convert_element_type.22), kind=kLoop, calls=%fused_computation.14.clone.1 | loop fusion | flops 786432 | bytes 4194316 | tf_op jit(solution)/shard_map/while/body/add | solution.py:119
  114.5 11.9 %dynamic_update_slice.9 = f32[2,2,512,1024]{3,2,1,0:T(8,128)} dynamic-update-slice(f32[2,2,512,1024]{3,2,1,0:T(8,128)} %dynamic_update_slice.8, f32[2,2,256,256]{3,2,1,0:T(8,128)} %fusion.175, s32[]{:T(128)} %constant.53.clone.1..sunk, s32[]{:T(128)} %constant.53.clone.1..sunk, s32[]{:T(128)S(6)} %select_n.63, s32[]{:T(128)S(6)} %select_n.64) | dynamic-update-slice | bytes 2097156 | tf_op jit(solution)/shard_map/while/body/dynamic_update_slice | solution.py:118
  133.7 2.6 %dynamic-slice_bitcast_fusion.6 = (f32[1,2,2,256,256]{4,3,2,0,1:T(8,128)S(1)}, f32[1,2,2,256,256]{4,3,2,0,1:T(8,128)S(1)}) fusion(f32[2,2,512,1024]{3,2,1,0:T(8,128)} %get-tuple-element.377, s32[]{:T(128)S(6)} %select_n.63, s32[]{:T(128)S(6)} %select_n.64, s32[]{:T(128)S(6)} %select_n.65, s32[]{:T(128)S(6)} %select_n.66), kind=kLoop, calls=%fused_computation.71.clone.1 | loop fusion | bytes 4194320 | tf_op jit(solution)/shard_map/while/body/stack | solution.py:110
  140.7 1.9 fusion.157
  149.2 1.9 fusion.164
  162.4 2.8 %fusion.174 = f32[2,2,256,256]{3,2,1,0:T(8,128)} fusion(f32[2,1,2,256,256]{4,3,2,0,1:T(8,128)S(1)} %get-tuple-element.331, f32[2,1,2,256,256]{4,3,2,0,1:T(8,128)S(1)} %get-tuple-element.332, f32[2,2,512,1024]{3,2,1,0:T(8,128)} %get-tuple-element.352, s32[]{:T(128)S(6)} %select_n.65, s32[]{:T(128)S(6)} %select_n.66, f32[]{:T(128)S(6)} %convert_element_type.21), kind=kLoop, calls=%fused_computation.8.clone.1 | loop fusion | flops 786432 | bytes 4194316 | tf_op jit(solution)/shard_map/while/body/add | solution.py:119
  165.1 12.3 %dynamic_update_slice.8 = f32[2,2,512,1024]{3,2,1,0:T(8,128)} dynamic-update-slice(f32[2,2,512,1024]{3,2,1,0:T(8,128)} %get-tuple-element.352, f32[2,2,256,256]{3,2,1,0:T(8,128)} %fusion.174, s32[]{:T(128)} %constant.53.clone.1..sunk, s32[]{:T(128)} %constant.53.clone.1..sunk, s32[]{:T(128)S(6)} %select_n.65, s32[]{:T(128)S(6)} %select_n.66) | dynamic-update-slice | bytes 2097156 | tf_op jit(solution)/shard_map/while/body/dynamic_update_slice | solution.py:118
  177.4 2.8 %fusion.175 = f32[2,2,256,256]{3,2,1,0:T(8,128)} fusion(f32[2,1,2,256,256]{4,3,2,0,1:T(8,128)S(1)} %get-tuple-element.332, f32[2,1,2,256,256]{4,3,2,0,1:T(8,128)S(1)} %get-tuple-element.331, f32[2,2,512,1024]{3,2,1,0:T(8,128)} %dynamic_update_slice.8, s32[]{:T(128)S(6)} %select_n.63, s32[]{:T(128)S(6)} %select_n.64, f32[]{:T(128)S(6)} %convert_element_type.22), kind=kLoop, calls=%fused_computation.14.clone.1 | loop fusion | flops 786432 | bytes 4194316 | tf_op jit(solution)/shard_map/while/body/add | solution.py:119
  180.2 12.1 %dynamic_update_slice.9 = f32[2,2,512,1024]{3,2,1,0:T(8,128)} dynamic-update-slice(f32[2,2,512,1024]{3,2,1,0:T(8,128)} %dynamic_update_slice.8, f32[2,2,256,256]{3,2,1,0:T(8,128)} %fusion.175, s32[]{:T(128)} %constant.53.clone.1..sunk, s32[]{:T(128)} %constant.53.clone.1..sunk, s32[]{:T(128)S(6)} %select_n.63, s32[]{:T(128)S(6)} %select_n.64) | dynamic-update-slice | bytes 2097156 | tf_op jit(solution)/shard_map/while/body/dynamic_update_slice | solution.py:118
  192.3 2.7 %slice.343 = f32[2,2,256,1024]{3,2,1,0:T(8,128)S(1)} slice(f32[2,2,512,1024]{3,2,1,0:T(8,128)} %get-tuple-element.388), slice={[0:2], [0:2], [256:512], [0:1024]} | slice | bytes 8388608 | tf_op jit(solution)/shard_map/slice | solution.py:147
  195.0 2.2 collective-permute-start.1
  197.2 47.9 %collective-permute-done.1 = f32[2,2,256,1024]{3,2,1,0:T(8,128)S(1)} collective-permute-done((f32[2,2,256,1024]{3,2,1,0:T(8,128)S(1)}, f32[2,2,256,1024]{3,2,1,0:T(8,128)S(1)}, u32[]{:S(2)}, u32[]{:S(2)}) %collective-permute-start.1) | collective-permute-done | bytes 4194336 | tf_op jit(solution)/shard_map/ppermute | solution.py:10
  245.1 2.9 %slice_add_fusion.6 = f32[2,2,256,1024]{3,2,1,0:T(8,128)} fusion(f32[2,2,256,1024]{3,2,1,0:T(8,128)S(1)} %collective-permute-done.1, f32[2,2,512,1024]{3,2,1,0:T(8,128)S(1)} %copy-done), kind=kLoop, calls=%fused_computation.163 | loop fusion | flops 1048576 | bytes 12582912 | tf_op jit(solution)/shard_map/add | solution.py:148
  (105 shorter events, 48.4 us)
Async XLA Ops:
  0.0 48.2 %collective-permute-start = (f32[2,2,256,1024]{3,2,1,0:T(8,128)}, f32[2,2,256,1024]{3,2,1,0:T(8,128)}, u32[]{:S(2)}, u32[]{:S(2)}) collective-permute-start(f32[2,2,256,1024]{3,2,1,0:T(8,128)} %param.8), channel_id=1, source_target_pairs={{1,0},{2,1},{3,2},{4,3},{5,4},{6,5},{7,6},{8,7},{9,8},{10,9},{11,1... | collective-permute-start | bytes 12582920 | tf_op jit(solution)/shard_map/ppermute | solution.py:10
  56.6 4.3 %copy-start.1 = (f32[2,256,256]{2,1,0:T(8,128)S(1)}, f32[2,256,256]{2,1,0:T(8,128)}, u32[]{:S(2)}) copy-start(f32[2,256,256]{2,1,0:T(8,128)} %param.9) | copy-start | bytes 1572868
  56.6 4.3 %copy-start.5 = (s32[4,2]{0,1:T(2,128)S(1)}, s32[4,2]{0,1:T(2,128)}, u32[]{:S(2)}) copy-start(s32[4,2]{0,1:T(2,128)} %param.11) | copy-start | bytes 100
  61.0 7.3 %copy-start.3 = (f32[4,256,256]{1,2,0:T(8,128)}, f32[4,256,256]{1,2,0:T(8,128)S(1)}, u32[]{:S(2)}) copy-start(f32[4,256,256]{1,2,0:T(8,128)S(1)} %get-tuple-element.379) | copy-start | bytes 3145732 | tf_op jit(solution)/shard_map/while
  114.5 11.9 %copy-start.2 = (f32[2,256,256]{2,1,0:T(8,128)S(1)}, f32[2,256,256]{2,1,0:T(8,128)}, u32[]{:S(2)}) copy-start(f32[2,256,256]{2,1,0:T(8,128)} %get-tuple-element.405) | copy-start | bytes 1572868 | tf_op jit(solution)/shard_map/while
  114.5 11.9 %copy-start.4 = (f32[4,256,256]{1,2,0:T(8,128)S(1)}, f32[4,256,256]{1,2,0:T(8,128)}, u32[]{:S(2)}) copy-start(f32[4,256,256]{1,2,0:T(8,128)} %copy-done.3) | copy-start | bytes 3145732 | tf_op jit(solution)/shard_map/while
  126.4 7.3 %copy-start.3 = (f32[4,256,256]{1,2,0:T(8,128)}, f32[4,256,256]{1,2,0:T(8,128)S(1)}, u32[]{:S(2)}) copy-start(f32[4,256,256]{1,2,0:T(8,128)S(1)} %get-tuple-element.379) | copy-start | bytes 3145732 | tf_op jit(solution)/shard_map/while
  180.2 12.1 %copy-start.2 = (f32[2,256,256]{2,1,0:T(8,128)S(1)}, f32[2,256,256]{2,1,0:T(8,128)}, u32[]{:S(2)}) copy-start(f32[2,256,256]{2,1,0:T(8,128)} %get-tuple-element.405) | copy-start | bytes 1572868 | tf_op jit(solution)/shard_map/while
  180.2 12.1 %copy-start.4 = (f32[4,256,256]{1,2,0:T(8,128)S(1)}, f32[4,256,256]{1,2,0:T(8,128)}, u32[]{:S(2)}) copy-start(f32[4,256,256]{1,2,0:T(8,128)} %copy-done.3) | copy-start | bytes 3145732 | tf_op jit(solution)/shard_map/while
  192.3 52.8 %copy-start = (f32[2,2,512,1024]{3,2,1,0:T(8,128)S(1)}, f32[2,2,512,1024]{3,2,1,0:T(8,128)}, u32[]{:S(2)}) copy-start(f32[2,2,512,1024]{3,2,1,0:T(8,128)} %get-tuple-element.388) | copy-start | bytes 25165828
  195.0 50.1 %collective-permute-start.1 = (f32[2,2,256,1024]{3,2,1,0:T(8,128)S(1)}, f32[2,2,256,1024]{3,2,1,0:T(8,128)S(1)}, u32[]{:S(2)}, u32[]{:S(2)}) collective-permute-start(f32[2,2,256,1024]{3,2,1,0:T(8,128)S(1)} %slice.343), channel_id=1, source_target_pairs={{0,1},{1,2},{2,3},{3,4},{4,5},{5,6},{6,7},{7,8},{8,9},{9,10},{10,1... | collective-permute-start | bytes 12582920 | tf_op jit(solution)/shard_map/ppermute | solution.py:10
where the time goes:
time: 251 us; the launch traced here: 248 us
  waiting for transfers between devices  88.7 us (35%)
  local copies, waits for them, and re-layouts  65.6 us (26%)
  matrix products  44.6 us (18%)
  other arithmetic  30.5 us (12%)
  loops' own time  13.8 us (5%)
  starting transfers between devices  4.1 us (2%)
    ppermute x2, waiting for transfers between devices, from_behind(): return lax.ppermute(block, axis, route)  88.7 us
    dynamic_update_slice x4, local copies, waits for them, and re-layouts, visit(): lax.dynamic_update_slice(running, previous + flag_now * contrib[member],...  48.3 us
    dot_general x24, matrix products, right_pass(): product = jnp.dot(flat, both_tables, precision=lax.Precision.HIGHEST)  44.6 us
    another operation x1, loops' own time, run_slots(): return lax.fori_loop(0, (how_many + 1) // 2, visit, accumulated)  13.8 us
    add x4, other arithmetic, visit(): previous + flag_now * contrib[member]  11 us
    concatenate x1, other arithmetic, shards(): window = jnp.concatenate([obj_field, following], axis=2)  8.4 us
    another operation x2, local copies, waits for them, and re-layouts, visit(): jnp.stack([lax.dynamic_slice(window, corner, tile_shape) for corner in co...  5.14 us
  transfers between devices with their start and end apart: 2, of which 2 were waited for; matrix products, arithmetic and copies ran while one was open for 2% of the time, Pallas kernels for 0%

commit v1 on v0

v1 whole, which is shorter than its diff:
```python
import functools

import jax
import jax.numpy as jnp
import numpy as np
from jax import lax
from jax.experimental import pallas as pl
from jax.experimental.pallas import tpu as pltpu
from jax.sharding import PartitionSpec as P

WIN = 256
HALF = WIN // 2
LANES = 128
SUB = 8
CAP = 4
GROUPS = WIN // SUB
INT_GROUPS = GROUPS // 4
CAP_FWD = 48
CAP_BACK_A = 48
CAP_BACK_B = 32
DEAD, AT_A, AT_B = 0, 1, 2
FIELDS = 8
f32 = jnp.float32
bf16 = jnp.bfloat16
VM = pltpu.MemorySpace.VMEM
SM = pltpu.MemorySpace.SMEM


def real_tables():
    k = np.arange(HALF)[:, None]
    n = np.arange(HALF)[None, :]
    out = []
    for odd in (0, 1):
        angle = 2.0 * np.pi * (((2 * k + odd) * n) % WIN) / WIN
        c, s = np.cos(angle) / 16.0, np.sin(angle) / 16.0
        out.append(np.block([[c, s], [-s, c]]))
    return out


def high_low(table):
    high = table.astype(np.float32).astype(bf16)
    low = (table - high.astype(np.float64)).astype(np.float32).astype(bf16)
    return high, low


def left_table(table):
    high, low = high_low(table)
    return np.concatenate([high, low, high], axis=1)


def right_table(table):
    high, low = high_low(table)
    return np.concatenate([high, high, low], axis=0)


def make_tables():
    even, odd = real_tables()
    left = np.stack([left_table(m) for m in (even, odd, even.T, odd.T)])
    right = np.stack([right_table(m) for m in (even.T, odd.T, even, odd)])
    order = np.concatenate([np.arange(0, WIN, 2), np.arange(1, WIN, 2)])
    shuffle = np.zeros((WIN, WIN), np.float32)
    shuffle[order, np.arange(WIN)] = 1.0
    return left, right, np.concatenate([shuffle, shuffle], axis=0).astype(bf16)


def split(x):
    high = x.astype(bf16)
    return high, (x - high.astype(f32)).astype(bf16)


def left_mul(table, x):
    high, low = split(x)
    return jnp.dot(table, jnp.concatenate([high, high, low], axis=0), preferred_element_type=f32)


def right_mul(x, table):
    high, low = split(x)
    return jnp.dot(jnp.concatenate([high, low, high], axis=1), table, preferred_element_type=f32)


def rows_forward(re, im, left, cols):
    def halves(x):
        return x[:HALF], x[HALF:]

    tr, br = halves(re)
    ti, bi = halves(im)
    e = left_mul(left[0], jnp.concatenate([tr + br, ti + bi], axis=0))
    o = left_mul(left[1], jnp.concatenate([tr - br, ti - bi], axis=0))
    return e, o


def rows_inverse(xr, xi, left):
    u = left_mul(left[2], jnp.concatenate([xr[:HALF], xi[:HALF]], axis=0))
    v = left_mul(left[3], jnp.concatenate([xr[HALF:], xi[HALF:]], axis=0))
    return u, v


def lanes_forward(re, im, right):
    lr, rr = re[:, :HALF], re[:, HALF:]
    li, ri = im[:, :HALF], im[:, HALF:]
    e = right_mul(jnp.concatenate([lr + rr, li + ri], axis=1), right[0])
    o = right_mul(jnp.concatenate([lr - rr, li - ri], axis=1), right[1])
    return (
        jnp.concatenate([e[:, :HALF], o[:, :HALF]], axis=1),
        jnp.concatenate([e[:, HALF:], o[:, HALF:]], axis=1),
    )


def lanes_inverse(re, im, right):
    u = right_mul(jnp.concatenate([re[:, :HALF], im[:, :HALF]], axis=1), right[2])
    v = right_mul(jnp.concatenate([re[:, HALF:], im[:, HALF:]], axis=1), right[3])
    return (
        jnp.concatenate([u[:, :HALF] + v[:, :HALF], u[:, :HALF] - v[:, :HALF]], axis=1),
        jnp.concatenate([u[:, HALF:] + v[:, HALF:], u[:, HALF:] - v[:, HALF:]], axis=1),
    )


def cmul(ar, ai, br, bi):
    return ar * br - ai * bi, ar * bi + ai * br


def cmul_conj(ar, ai, br, bi):
    return ar * br + ai * bi, ar * bi - ai * br


def decide_kernel(offsets, live, table):
    count = live[0]
    rows = [jnp.bitwise_and(offsets[j, 0], WIN - 1) for j in range(CAP)]
    used = [(j < count).astype(jnp.int32) for j in range(CAP)]
    on_a = [used[j] * ((rows[j] + SUB - 1) // SUB) for j in range(CAP)]
    on_b = [used[j] * (GROUPS - rows[j] // SUB + INT_GROUPS) for j in range(CAP)]
    best, chosen = jnp.int32(10000), jnp.int32(0)
    for mask in range(1 << CAP):
        total_a = jnp.int32(0)
        total_b = jnp.int32(0)
        for j in range(CAP):
            if mask >> j & 1:
                total_b = total_b + on_b[j]
            else:
                total_a = total_a + on_a[j]
        cost = jnp.maximum(total_a, total_b)
        better = cost < best
        best = jnp.where(better, cost, best)
        chosen = jnp.where(better, mask, chosen)
    at_a = jnp.int32(0)
    at_b = jnp.int32(0)
    back = jnp.int32(0)
    for j in range(CAP):
        to_b = jnp.bitwise_and(chosen >> j, 1) * used[j]
        to_b = jnp.where(rows[j] == 0, 0, to_b)
        to_a = used[j] - to_b
        table[FIELDS * j] = to_a * AT_A + to_b * AT_B
        table[FIELDS * j + 1] = rows[j]
        table[FIELDS * j + 2] = offsets[j, 1]
        table[FIELDS * j + 3] = jnp.where(to_b == 1, at_b, at_a)
        table[FIELDS * j + 4] = jnp.where(to_b == 1, back, at_a)
        at_a = at_a + to_a * on_a[j]
        at_b = at_b + to_b * on_b[j]
        back = back + to_b * (on_b[j] - INT_GROUPS)
        table[FIELDS * j + 5] = 0
        table[FIELDS * j + 6] = 0
        table[FIELDS * j + 7] = 0


def slot_of(table, j):
    base = FIELDS * j
    return table[base], table[base + 1], table[base + 2], table[base + 3], table[base + 4]


def lane_blocks(col):
    first = col // LANES
    starts = [jnp.minimum(first + k, 7) * LANES for k in range(3)]
    return [pl.multiple_of(start, LANES) for start in starts], jnp.bitwise_and(col, LANES - 1)


def lane_iota():
    return lax.broadcasted_iota(jnp.int32, (SUB, LANES), 1)


def load_group(field, plane, group, starts, shift):
    rows = pl.ds(pl.multiple_of(group * SUB, SUB), SUB)
    first = field[plane, rows, pl.ds(starts[0], LANES)]
    second = field[plane, rows, pl.ds(starts[1], LANES)]
    third = field[plane, rows, pl.ds(starts[2], LANES)]
    return jnp.where(lane_iota() >= shift, first, third), second


def add_group(total, plane, group, starts, shift, left, right):
    rows = pl.ds(pl.multiple_of(group * SUB, SUB), SUB)
    inside = lane_iota() >= shift
    total[plane, rows, pl.ds(starts[0], LANES)] += jnp.where(inside, left, 0.0)
    total[plane, rows, pl.ds(starts[1], LANES)] += right
    total[plane, rows, pl.ds(starts[2], LANES)] += jnp.where(inside, 0.0, left)


def pack_to_b_kernel(table, field, intensity, out):
    for j in range(CAP):
        state, row, col, start, _ = slot_of(table, j)

        @pl.when(state == AT_B)
        def _():
            starts, shift = lane_blocks(col)
            first = row // SUB

            def body(group, carry):
                at = start + group - first
                for plane in range(4):
                    left, right = load_group(field, plane, group, starts, shift)
                    out[at, plane, :, :LANES] = left
                    out[at, plane, :, LANES:] = right
                return carry

            lax.fori_loop(first, GROUPS, body, 0)
            after = start + GROUPS - first

            def body_int(group, carry):
                for plane in range(4):
                    rows = pl.ds(pl.multiple_of((group * 4 + plane) * SUB, SUB), SUB)
                    out[after + group, plane] = intensity[j, rows, :]
                return carry

            lax.fori_loop(0, INT_GROUPS, body_int, 0)


def pack_to_a_kernel(table, field, out):
    for j in range(CAP):
        state, row, col, start, _ = slot_of(table, j)

        @pl.when(state == AT_A)
        def _():
            starts, shift = lane_blocks(col)

            def body(group, carry):
                for plane in range(4):
                    left, right = load_group(field, plane, group, starts, shift)
                    out[start + group, plane, :, :LANES] = left
                    out[start + group, plane, :, LANES:] = right
                return carry

            lax.fori_loop(0, (row + SUB - 1) // SUB, body, 0)


def slots_kernel(
    first_kind,
    role,
    table,
    field,
    intensity,
    probe,
    kernel,
    left,
    right,
    shuffle,
    from_b,
    from_a,
    total_in,
    total,
    back_a,
    back_b,
    got,
    tile,
    measured,
    twice,
    beam,
    work,
    entered,
    sem,
):
    is_a = role[0] == 0
    mine = jnp.where(is_a, AT_A, AT_B)

    def fetch(source):
        copy = pltpu.make_async_copy(source, got, sem)
        copy.start()
        copy.wait()

    @pl.when(is_a)
    def _():
        fetch(from_b)

    @pl.when(jnp.logical_not(is_a))
    def _():
        fetch(from_a)

    if first_kind:
        total[...] = jnp.zeros_like(total)
    else:
        copy = pltpu.make_async_copy(total_in, total, sem)
        copy.start()
        copy.wait()
    for plane in range(2):
        for part in range(2):
            cut = probe[plane, :, part * LANES : (part + 1) * LANES]
            twice[2 * plane + part, :WIN] = cut
            twice[2 * plane + part, WIN:] = cut

    def slot_body(j, carry):
        state, row, col, start, back = slot_of(table, j)

        @pl.when(state == mine)
        def _():
            starts, shift = lane_blocks(col)
            low = row // SUB
            base = jnp.where(is_a, start, start - low)
            sublane = lax.broadcasted_iota(jnp.int32, (SUB, LANES), 0)

            def own_rows(group):
                below = (group * SUB + sublane < row).astype(jnp.int32)
                return below == jnp.where(is_a, 0, 1)

            def gather(group, carry):
                own = own_rows(group)
                at = jnp.clip(base + group, 0, CAP_FWD - 1)
                rows = pl.ds(pl.multiple_of(group * SUB, SUB), SUB)
                for plane in range(4):
                    lf, rt = load_group(field, plane, group, starts, shift)
                    tile[plane, rows, :LANES] = jnp.where(own, lf, got[at, plane, :, :LANES])
                    tile[plane, rows, LANES:] = jnp.where(own, rt, got[at, plane, :, LANES:])
                return carry

            lax.fori_loop(0, GROUPS, gather, 0)

            @pl.when(is_a)
            def _():
                measured[0] = intensity[j, :, :LANES]
                measured[1] = intensity[j, :, LANES:]

            @pl.when(jnp.logical_not(is_a))
            def _():
                after = start + GROUPS - low

                def unpack(group, carry):
                    for plane in range(4):
                        rows = pl.ds(pl.multiple_of((group * 4 + plane) * SUB, SUB), SUB)
                        measured[0, rows, :] = got[after + group, plane, :, :LANES]
                        measured[1, rows, :] = got[after + group, plane, :, LANES:]
                    return carry

                lax.fori_loop(0, INT_GROUPS, unpack, 0)

            for plane in range(2):
                parts = [twice[2 * plane + part, pl.ds(WIN - row, WIN), :] for part in range(2)]
                beam[plane] = pltpu.roll(jnp.concatenate(parts, axis=1), shift, 1)

            def store_rows(e, o):
                work[0, :HALF], work[1, :HALF] = e[:HALF], e[HALF:]
                work[0, HALF:], work[1, HALF:] = o[:HALF], o[HALF:]

            def middle(pointwise):
                for half in range(2):
                    rows = pl.ds(half * HALF, HALF)
                    re, im = lanes_forward(work[0, rows, :], work[1, rows, :], right)
                    re, im = pointwise(half, rows, re, im)
                    re, im = lanes_inverse(re, im, right)
                    work[0, rows, :], work[1, rows, :] = re, im

            def unstack(u, v):
                return (
                    jnp.concatenate([u[:HALF] + v[:HALF], u[:HALF] - v[:HALF]], axis=0),
                    jnp.concatenate([u[HALF:] + v[HALF:], u[HALF:] - v[HALF:]], axis=0),
                )

            def propagate(half, rows, re, im):
                return cmul(kernel[0, rows, :], kernel[1, rows, :], re, im)

            def propagate_back(half, rows, re, im):
                return cmul_conj(kernel[0, rows, :], kernel[1, rows, :], re, im)

            def residual(half, rows, re, im):
                every = pl.ds(half, HALF, stride=2)
                rows_of = jnp.concatenate([measured[0, every, :], measured[1, every, :]], axis=1)
                high, low_part = split(rows_of)
                wanted = jnp.dot(
                    jnp.concatenate([high, low_part], axis=1), shuffle[...], preferred_element_type=f32
                )
                scale = re * re + im * im - wanted
                return scale * re, scale * im

            re, im = cmul(beam[0], beam[1], tile[0], tile[1])
            store_rows(*rows_forward(re, im, left, None))
            middle(propagate)
            re, im = unstack(*rows_inverse(work[0], work[1], left))
            entered[0], entered[1] = re, im
            re, im = cmul(re, im, tile[2], tile[3])
            store_rows(*rows_forward(re, im, left, None))
            middle(residual)
            br, bi = unstack(*rows_inverse(work[0], work[1], left))
            re, im = cmul_conj(tile[2], tile[3], br, bi)
            tile[2], tile[3] = cmul_conj(entered[0], entered[1], br, bi)
            store_rows(*rows_forward(re, im, left, None))
            middle(propagate_back)
            br, bi = unstack(*rows_inverse(work[0], work[1], left))
            tile[0], tile[1] = cmul_conj(beam[0], beam[1], br, bi)

            def scatter(group, carry):
                own = own_rows(group)
                rows = pl.ds(pl.multiple_of(group * SUB, SUB), SUB)
                for plane in range(4):
                    lf = jnp.where(own, tile[plane, rows, :LANES], 0.0)
                    rt = jnp.where(own, tile[plane, rows, LANES:], 0.0)
                    add_group(total, plane, group, starts, shift, lf, rt)
                return carry

            lax.fori_loop(jnp.where(is_a, low, 0), jnp.where(is_a, GROUPS, (row + SUB - 1) // SUB), scatter, 0)

            def send(out, offset):
                def body(group, carry):
                    rows = pl.ds(pl.multiple_of(group * SUB, SUB), SUB)
                    for plane in range(4):
                        out[offset + group, plane] = tile[plane, rows, :]
                    return carry

                return body

            @pl.when(is_a)
            def _():
                lax.fori_loop(0, (row + SUB - 1) // SUB, send(back_a, back), 0)

            @pl.when(jnp.logical_not(is_a))
            def _():
                lax.fori_loop(low, GROUPS, send(back_b, back - low), 0)

        return carry

    lax.fori_loop(0, CAP, slot_body, 0)


def finish_kernel(
    role_in, table_in, role_out, table_out, total_in, in_a, in_b, out_a, out_b, total, got_in, got_out, sem
):
    def start_copies(role, from_a, from_b, got, at):
        @pl.when(role[0] == 0)
        def _():
            pltpu.make_async_copy(from_b, got.at[pl.ds(0, CAP_BACK_B)], sem.at[at]).start()
            pltpu.make_async_copy(from_b, got.at[pl.ds(0, CAP_BACK_B)], sem.at[at]).wait()

        @pl.when(role[0] == 1)
        def _():
            pltpu.make_async_copy(from_a, got, sem.at[at]).start()
            pltpu.make_async_copy(from_a, got, sem.at[at]).wait()

    start_copies(role_in, in_a, in_b, got_in, 0)
    start_copies(role_out, out_a, out_b, got_out, 1)
    total[...] = total_in[...]
    for role, table, got in ((role_in, table_in, got_in), (role_out, table_out, got_out)):
        is_a = role[0] == 0
        theirs = jnp.where(is_a, AT_B, AT_A)
        for j in range(CAP):
            state, row, col, _, back = slot_of(table, j)

            @pl.when(state == theirs)
            def _():
                starts, shift = lane_blocks(col)
                low = row // SUB
                base = jnp.where(is_a, back - low, back)
                sublane = lax.broadcasted_iota(jnp.int32, (SUB, LANES), 0)

                def body(group, carry):
                    below = (group * SUB + sublane < row).astype(jnp.int32)
                    own = below == jnp.where(is_a, 0, 1)
                    for plane in range(4):
                        lf = jnp.where(own, got[base + group, plane, :, :LANES], 0.0)
                        rt = jnp.where(own, got[base + group, plane, :, LANES:], 0.0)
                        add_group(total, plane, group, starts, shift, lf, rt)
                    return carry

                lax.fori_loop(
                    jnp.where(is_a, low, 0), jnp.where(is_a, GROUPS, (row + SUB - 1) // SUB), body, 0
                )


def spec(space):
    return pl.BlockSpec(memory_space=space)


PARAMS = pltpu.CompilerParams(vmem_limit_bytes=48 << 20)


def packed(groups):
    return jax.ShapeDtypeStruct((groups, 4, SUB, WIN), f32)


def run_slots(first_kind, role, table, field, intensity, probe, kernel, tables, from_b, from_a, total):
    left, right, shuffle = tables
    specs = [spec(SM)] * 2 + [spec(VM)] * 7 + [spec(pl.ANY)] * 3
    return pl.pallas_call(
        functools.partial(slots_kernel, first_kind),
        out_shape=(
            jax.ShapeDtypeStruct(field.shape, f32),
            packed(CAP_BACK_A),
            packed(CAP_BACK_B),
        ),
        in_specs=specs,
        out_specs=(spec(VM),) * 3,
        scratch_shapes=[
            pltpu.VMEM((CAP_FWD, 4, SUB, WIN), f32),
            pltpu.VMEM((4, WIN, WIN), f32),
            pltpu.VMEM((2, WIN, LANES), f32),
            pltpu.VMEM((4, 2 * WIN, LANES), f32),
            pltpu.VMEM((2, WIN, WIN), f32),
            pltpu.VMEM((2, WIN, WIN), f32),
            pltpu.VMEM((2, WIN, WIN), f32),
            pltpu.SemaphoreType.DMA,
        ],
        compiler_params=PARAMS,
    )(role, table, field, intensity, probe, kernel, left, right, shuffle, from_b, from_a, total)


def shards(obj_field, probe_wave, prop_phase, win_offsets, live_counts, intensity):
    field = obj_field.reshape((4,) + obj_field.shape[2:])
    count = lax.axis_size("row")
    within = [(i, i + 1) for i in range(0, count - 1, 2)]
    across = [(i, i + 1) for i in range(1, count - 1, 2)]
    back = lambda pairs: [(b, a) for a, b in pairs]
    move = lambda x, pairs: lax.ppermute(x, "row", pairs)
    odd = jnp.bitwise_and(lax.axis_index("row"), 1)
    role_in = odd.reshape(1)
    role_out = (1 - odd).reshape(1)

    own = pl.pallas_call(
        decide_kernel,
        out_shape=jax.ShapeDtypeStruct((CAP * FIELDS,), jnp.int32),
        in_specs=[spec(SM)] * 2,
        out_specs=spec(SM),
    )(win_offsets, live_counts)
    before = move(own, within + across)
    to_b = pl.pallas_call(
        pack_to_b_kernel,
        out_shape=packed(CAP_FWD),
        in_specs=[spec(SM), spec(VM), spec(VM)],
        out_specs=spec(VM),
        compiler_params=PARAMS,
    )(own, field, intensity)
    in_from_a = move(to_b, within)
    out_from_a = move(to_b, across)
    to_a = pl.pallas_call(
        pack_to_a_kernel,
        out_shape=packed(CAP_FWD),
        in_specs=[spec(SM), spec(VM)],
        out_specs=spec(VM),
        compiler_params=PARAMS,
    )(before, field)
    in_from_b = move(to_a, back(within))
    out_from_b = move(to_a, back(across))
    table_in = jnp.where(odd == 0, own, before)
    table_out = jnp.where(odd == 0, before, own)

    phase = prop_phase.reshape(HALF, 2, HALF, 2).transpose(1, 0, 3, 2).reshape(WIN, WIN)
    kernel = jnp.stack([jnp.cos(phase), jnp.sin(phase)])
    tables = tuple(jnp.asarray(t) for t in make_tables())

    args = (field, intensity, probe_wave, kernel, tables)
    total, in_back_a, in_back_b = run_slots(True, role_in, table_in, *args, in_from_b, in_from_a, field)
    in_a = move(in_back_a, within)
    in_b = move(in_back_b, back(within))
    total, out_back_a, out_back_b = run_slots(False, role_out, table_out, *args, out_from_b, out_from_a, total)
    out_a = move(out_back_a, across)
    out_b = move(out_back_b, back(across))
    grad = pl.pallas_call(
        finish_kernel,
        out_shape=jax.ShapeDtypeStruct(field.shape, f32),
        in_specs=[spec(SM)] * 4 + [spec(VM)] + [spec(pl.ANY)] * 4,
        out_specs=spec(VM),
        scratch_shapes=[
            pltpu.VMEM((CAP_BACK_A, 4, SUB, WIN), f32),
            pltpu.VMEM((CAP_BACK_A, 4, SUB, WIN), f32),
            pltpu.SemaphoreType.DMA((2,)),
        ],
        input_output_aliases={4: 0},
        compiler_params=PARAMS,
    )(role_in, table_in, role_out, table_out, total, in_a, in_b, out_a, out_b)
    return grad.reshape(obj_field.shape)


def solution(mesh):
    in_specs = (
        P(None, None, ("groups", "row"), None),
        P("groups", None, None),
        P(),
        P(("groups", "row"), None),
        P(("groups", "row")),
        P(("groups", "row"), None, None),
    )
    out_specs = P(None, None, ("groups", "row"), None)
    return jax.shard_map(shards, mesh=mesh, in_specs=in_specs, out_specs=out_specs, check_vma=False)
```

time: 251 us -> 166 us (0.66)
  the two profiles are of different devices: /device:TPU:30 before, /device:TPU:20 now
where the time goes in v1:
time: 166 us; the launch traced here: 167 us
  local copies, waits for them, and re-layouts  64.5 us (39%)
  Pallas kernels  51.4 us (31%)
  waiting for transfers between devices  25.9 us (16%)
  starting transfers between devices  24.5 us (15%)
    pallas_call x2, Pallas kernels, run_slots(): pl.pallas_call(functools.partial(slots_kernel, first_kind), out_shape=(ja...  40.3 us
    sin x4, local copies, waits for them, and re-layouts, shards(): kernel = jnp.stack([jnp.cos(phase), jnp.sin(phase)])  30.8 us
    cos x3, local copies, waits for them, and re-layouts, shards(): kernel = jnp.stack([jnp.cos(phase), jnp.sin(phase)])  28.5 us
    ppermute x9, waiting for transfers between devices, shards(): move = lambda x, pairs: lax.ppermute(x, 'row', pairs)  25.9 us
    ppermute x9, starting transfers between devices, shards(): move = lambda x, pairs: lax.ppermute(x, 'row', pairs)  24.5 us
    pallas_call x1, Pallas kernels, shards(): pl.pallas_call(finish_kernel, out_shape=jax.ShapeDtypeStruct(field.shape,...  5.45 us
    unnamed x18, local copies, waits for them, and re-layouts  4.18 us
  transfers between devices with their start and end apart: 9, of which 2 were waited for; matrix products, arithmetic and copies ran while one was open for 37% of the time, Pallas kernels for 27%

profile of v1, /device:TPU:20, one launch (start us, length us, event | category | flops | bytes accessed | tf_op | source)
XLA Modules:
  0.0 167.3 jit_solution(16742669760120786462)
XLA Ops:
  0.0 1.3 copy.14.offsets
  2.0 1.3 shard_map.91.table
  3.3 1.9 %collective-permute-start = (s32[32]{0:T(128)}, s32[32]{0:T(128)S(1)}, u32[]{:S(2)}, u32[]{:S(2)}) collective-permute-start(s32[32]{0:T(128)} %shard_map.91.table), channel_id=1, source_target_pairs={{0,1},{2,3},{4,5},{6,7},{8,9},{10,11},{12,13},{14,15},{1,2},{3,4},... | collective-permute-start | bytes 392 | tf_op jit(solution)/shard_map/ppermute | solution.py:515
  5.2 1.2 copy-done.1
  7.1 2.6 %shard_map.93 = f32[48,4,8,256]{3,2,1,0:T(8,128)S(1)} custom-call(s32[32]{0:T(128)S(1)} %copy-done.5, f32[4,256,1024]{2,1,0:T(8,128)} %bitcast.6, f32[4,256,256]{2,1,0:T(8,128)S(1)} %copy-done.1), custom_call_target="tpu_custom_call" | custom-call | tf_op jit(solution)/shard_map/pallas_call | solution.py:527
  9.7 4.7 %collective-permute-start.4 = (f32[48,4,8,256]{3,2,1,0:T(8,128)S(1)}, f32[48,4,8,256]{3,2,1,0:T(8,128)}, u32[]{:S(2)}, u32[]{:S(2)}) collective-permute-start(f32[48,4,8,256]{3,2,1,0:T(8,128)S(1)} %shard_map.93), channel_id=1, source_target_pairs={{0,1},{2,3},{4,5},{6,7},{8,9},{10,11},{12,13},{14,15},{16,17},{18,... | collective-permute-start | bytes 4718600 | tf_op jit(solution)/shard_map/ppermute | solution.py:515
  14.3 1.8 %shard_map.92 = f32[48,4,8,256]{3,2,1,0:T(8,128)} custom-call(s32[32]{0:T(128)S(1)} %collective-permute-done.table, f32[4,256,1024]{2,1,0:T(8,128)S(1)} %bitcast.10), custom_call_target="tpu_custom_call" | custom-call | tf_op jit(solution)/shard_map/pallas_call | solution.py:536
  16.2 1.3 collective-permute-start.3
  17.4 1.3 collective-permute-start.2
  18.7 6.7 %collective-permute-start.1 = (f32[48,4,8,256]{3,2,1,0:T(8,128)}, f32[48,4,8,256]{3,2,1,0:T(8,128)}, u32[]{:S(2)}, u32[]{:S(2)}) collective-permute-start(f32[48,4,8,256]{3,2,1,0:T(8,128)} %shard_map.92), channel_id=1, source_target_pairs={{2,1},{4,3},{6,5},{8,7},{10,9},{12,11},{14,13},{18,17},{20,19},{22... | collective-permute-start | bytes 4718600 | tf_op jit(solution)/shard_map/ppermute | solution.py:515
  26.4 18.1 %cos.20 = f32[128,2,128,2]{3,2,1,0:T(8,128)} reshape(f32[256,256]{1,0:T(8,128)S(1)} %get-tuple-element.18) | data formatting | bytes 524288 | tf_op jit(solution)/shard_map/cos | solution.py:549
  44.5 9.5 %copy.15 = f32[2,128,2,128]{3,2,1,0:T(2,128)S(1)} copy(f32[2,128,2,128]{2,3,0,1:T(8,128)} %bitcast.11) | data formatting | bytes 524288 | tf_op jit(solution)/shard_map/cos | solution.py:549
  54.9 18.1 %sin.20 = f32[128,2,128,2]{3,2,1,0:T(8,128)} reshape(f32[256,256]{1,0:T(8,128)S(1)} %get-tuple-element.17) | data formatting | bytes 524288 | tf_op jit(solution)/shard_map/sin | solution.py:549
  73.0 9.8 %copy.16 = f32[2,128,2,128]{3,2,1,0:T(2,128)} copy(f32[2,128,2,128]{2,3,0,1:T(8,128)} %bitcast.12) | data formatting | bytes 524288 | tf_op jit(solution)/shard_map/sin | solution.py:549
  82.8 2.0 %sin.22 = f32[1,256,256]{2,1,0:T(8,128)} reshape(f32[2,128,2,128]{3,2,1,0:T(2,128)} %copy.16) | data formatting | bytes 524288 | tf_op jit(solution)/shard_map/sin | solution.py:549
  86.8 25.3 %shard_map.94 = (f32[4,256,1024]{2,1,0:T(8,128)}, f32[48,4,8,256]{3,2,1,0:T(8,128)S(1)}, f32[32,4,8,256]{3,2,1,0:T(8,128)S(1)}) custom-call(s32[1]{0:T(128)} %bitcast.role.role_in, s32[32]{0:T(128)S(1)} %get-tuple-element.20.table.table_in, f32[4,256,1024]{2,1,0:T(8,128)} %bitcast.7, f32[4,256,256]{2,1,0:T(8,128)S(1)} %copy-done.2, ...), custom_call_target="tpu_custom_call" | custom-call | tf_op jit(solution)/shard_map/pallas_call | solution.py:486
  112.1 1.6 collective-permute-start.5
  113.7 15.0 %shard_map.95 = (f32[4,256,1024]{2,1,0:T(8,128)}, f32[48,4,8,256]{3,2,1,0:T(8,128)S(1)}, f32[32,4,8,256]{3,2,1,0:T(8,128)S(1)}) custom-call(s32[1]{0:T(128)} %bitcast.1.role.role_out, s32[32]{0:T(128)S(1)} %get-tuple-element.19.table.table_out, f32[4,256,1024]{2,1,0:T(8,128)} %bitcast.9, f32[4,256,256]{2,1,0:T(8,128)S(1)} %copy-done.2, ...), custom_call_target="tpu_custom_call" | custom-call | tf_op jit(solution)/shard_map/pallas_call | solution.py:486
  128.7 1.3 collective-permute-start.7
  130.0 1.3 collective-permute-start.6
  131.3 4.5 %collective-permute-start.8 = (f32[32,4,8,256]{3,2,1,0:T(8,128)S(1)}, f32[32,4,8,256]{3,2,1,0:T(8,128)S(1)}, u32[]{:S(2)}, u32[]{:S(2)}) collective-permute-start(f32[32,4,8,256]{3,2,1,0:T(8,128)S(1)} %get-tuple-element.16), channel_id=1, source_target_pairs={{2,1},{4,3},{6,5},{8,7},{10,9},{12,11},{14,13},{18,17},{20,19},{22... | collective-permute-start | bytes 3145736 | tf_op jit(solution)/shard_map/ppermute | solution.py:515
  135.8 12.2 %collective-permute-done.8.out_b = f32[32,4,8,256]{3,2,1,0:T(8,128)S(1)} collective-permute-done((f32[32,4,8,256]{3,2,1,0:T(8,128)S(1)}, f32[32,4,8,256]{3,2,1,0:T(8,128)S(1)}, u32[]{:S(2)}, u32[]{:S(2)}) %collective-permute-start.8) | collective-permute-done | bytes 1048608 | tf_op jit(solution)/shard_map/ppermute | solution.py:515
  148.1 13.6 %collective-permute-done.7.out_a = f32[48,4,8,256]{3,2,1,0:T(8,128)S(1)} collective-permute-done((f32[48,4,8,256]{3,2,1,0:T(8,128)S(1)}, f32[48,4,8,256]{3,2,1,0:T(8,128)S(1)}, u32[]{:S(2)}, u32[]{:S(2)}) %collective-permute-start.7) | collective-permute-done | bytes 1572896 | tf_op jit(solution)/shard_map/ppermute | solution.py:515
  161.7 5.5 %shard_map.96 = f32[4,256,1024]{2,1,0:T(8,128)} custom-call(s32[1]{0:T(128)} %bitcast.role.role_in, s32[32]{0:T(128)S(1)} %get-tuple-element.20.table.table_in, s32[1]{0:T(128)} %bitcast.1.role.role_out, s32[32]{0:T(128)S(1)} %get-tuple-element.19.table.table_out, f32[4,256,1024]{2,1,0:T(8,128)} %get-tuple-element.12.total_in, ...), custom_call_target="tpu_custom_call", output_to_operand_aliasing={{}: (4, {})} | custom-call | tf_op jit(solution)/shard_map/pallas_call | solution.py:559
  (27 shorter events, 4.5 us)
Async XLA Ops:
  3.3 11.1 %collective-permute-start = (s32[32]{0:T(128)}, s32[32]{0:T(128)S(1)}, u32[]{:S(2)}, u32[]{:S(2)}) collective-permute-start(s32[32]{0:T(128)} %shard_map.91.table), channel_id=1, source_target_pairs={{0,1},{2,3},{4,5},{6,7},{8,9},{10,11},{12,13},{14,15},{1,2},{3,4},... | collective-permute-start | bytes 392 | tf_op jit(solution)/shard_map/ppermute | solution.py:515
  5.2 1.2 copy-start.1
  6.4 0.6 copy-start.5
  7.1 7.3 %copy-start = (f32[2,2,256,1024]{3,2,1,0:T(8,128)S(1)}, f32[2,2,256,1024]{3,2,1,0:T(8,128)}, u32[]{:S(2)}) copy-start(f32[2,2,256,1024]{3,2,1,0:T(8,128)} %param.9) | copy-start | bytes 12582916
  9.7 15.8 %copy-start.7 = (f32[256,256]{1,0:T(8,128)S(1)}, f32[256,256]{1,0:T(8,128)}, u32[]{:S(2)}) copy-start(f32[256,256]{1,0:T(8,128)} %param.11) | copy-start | bytes 786436
  9.7 77.1 %collective-permute-start.4 = (f32[48,4,8,256]{3,2,1,0:T(8,128)S(1)}, f32[48,4,8,256]{3,2,1,0:T(8,128)}, u32[]{:S(2)}, u32[]{:S(2)}) collective-permute-start(f32[48,4,8,256]{3,2,1,0:T(8,128)S(1)} %shard_map.93), channel_id=1, source_target_pairs={{0,1},{2,3},{4,5},{6,7},{8,9},{10,11},{12,13},{14,15},{16,17},{18,... | collective-permute-start | bytes 4718600 | tf_op jit(solution)/shard_map/ppermute | solution.py:515
  16.2 70.6 %collective-permute-start.3 = (f32[48,4,8,256]{3,2,1,0:T(8,128)}, f32[48,4,8,256]{3,2,1,0:T(8,128)}, u32[]{:S(2)}, u32[]{:S(2)}) collective-permute-start(f32[48,4,8,256]{3,2,1,0:T(8,128)} %shard_map.92), channel_id=1, source_target_pairs={{1,0},{3,2},{5,4},{7,6},{9,8},{11,10},{13,12},{15,14},{17,16},{19,... | collective-permute-start | bytes 4718600 | tf_op jit(solution)/shard_map/ppermute | solution.py:515
  17.4 96.2 %collective-permute-start.2 = (f32[48,4,8,256]{3,2,1,0:T(8,128)S(1)}, f32[48,4,8,256]{3,2,1,0:T(8,128)}, u32[]{:S(2)}, u32[]{:S(2)}) collective-permute-start(f32[48,4,8,256]{3,2,1,0:T(8,128)S(1)} %shard_map.93), channel_id=1, source_target_pairs={{1,2},{3,4},{5,6},{7,8},{9,10},{11,12},{13,14},{17,18},{19,20},{21... | collective-permute-start | bytes 4718600 | tf_op jit(solution)/shard_map/ppermute | solution.py:515
  18.7 94.9 %collective-permute-start.1 = (f32[48,4,8,256]{3,2,1,0:T(8,128)}, f32[48,4,8,256]{3,2,1,0:T(8,128)}, u32[]{:S(2)}, u32[]{:S(2)}) collective-permute-start(f32[48,4,8,256]{3,2,1,0:T(8,128)} %shard_map.92), channel_id=1, source_target_pairs={{2,1},{4,3},{6,5},{8,7},{10,9},{12,11},{14,13},{18,17},{20,19},{22... | collective-permute-start | bytes 4718600 | tf_op jit(solution)/shard_map/ppermute | solution.py:515
  73.0 13.8 %copy-start.6 = (s32[32]{0:T(128)S(1)}, s32[32]{0:T(128)}, u32[]{:S(2)}) copy-start(s32[32]{0:T(128)} %shard_map.91.table) | copy-start | bytes 388
  73.0 13.8 %copy-start.4 = (bf16[512,256]{1,0:T(8,128)(2,1)S(1)}, bf16[512,256]{1,0:T(8,128)(2,1)}, u32[]{:S(2)}) copy-start(bf16[512,256]{1,0:T(8,128)(2,1)} %constant.16.clone.shuffle) | copy-start | bytes 786436
  82.8 4.0 %copy-start.2 = (f32[4,256,256]{2,1,0:T(8,128)S(1)}, f32[4,256,256]{2,1,0:T(8,128)}, u32[]{:S(2)}) copy-start(f32[4,256,256]{2,1,0:T(8,128)} %intensity.5) | copy-start | bytes 3145732
  82.8 4.0 %copy-start.3 = (f32[2,256,256]{2,1,0:T(8,128)S(1)}, f32[2,256,256]{2,1,0:T(8,128)}, u32[]{:S(2)}) copy-start(f32[2,256,256]{2,1,0:T(8,128)} %probe.3) | copy-start | bytes 1572868
  112.1 36.0 %collective-permute-start.5 = (f32[48,4,8,256]{3,2,1,0:T(8,128)S(1)}, f32[48,4,8,256]{3,2,1,0:T(8,128)S(1)}, u32[]{:S(2)}, u32[]{:S(2)}) collective-permute-start(f32[48,4,8,256]{3,2,1,0:T(8,128)S(1)} %get-tuple-element.13), channel_id=1, source_target_pairs={{0,1},{2,3},{4,5},{6,7},{8,9},{10,11},{12,13},{14,15},{16,17},{18,... | collective-permute-start | bytes 4718600 | tf_op jit(solution)/shard_map/ppermute | solution.py:515
  128.7 33.0 %collective-permute-start.7 = (f32[48,4,8,256]{3,2,1,0:T(8,128)S(1)}, f32[48,4,8,256]{3,2,1,0:T(8,128)S(1)}, u32[]{:S(2)}, u32[]{:S(2)}) collective-permute-start(f32[48,4,8,256]{3,2,1,0:T(8,128)S(1)} %get-tuple-element.15), channel_id=1, source_target_pairs={{1,2},{3,4},{5,6},{7,8},{9,10},{11,12},{13,14},{17,18},{19,20},{21... | collective-permute-start | bytes 4718600 | tf_op jit(solution)/shard_map/ppermute | solution.py:515
  130.0 5.8 %collective-permute-start.6 = (f32[32,4,8,256]{3,2,1,0:T(8,128)S(1)}, f32[32,4,8,256]{3,2,1,0:T(8,128)S(1)}, u32[]{:S(2)}, u32[]{:S(2)}) collective-permute-start(f32[32,4,8,256]{3,2,1,0:T(8,128)S(1)} %get-tuple-element.14), channel_id=1, source_target_pairs={{1,0},{3,2},{5,4},{7,6},{9,8},{11,10},{13,12},{15,14},{17,16},{19,... | collective-permute-start | bytes 3145736 | tf_op jit(solution)/shard_map/ppermute | solution.py:515
  131.3 16.7 %collective-permute-start.8 = (f32[32,4,8,256]{3,2,1,0:T(8,128)S(1)}, f32[32,4,8,256]{3,2,1,0:T(8,128)S(1)}, u32[]{:S(2)}, u32[]{:S(2)}) collective-permute-start(f32[32,4,8,256]{3,2,1,0:T(8,128)S(1)} %get-tuple-element.16), channel_id=1, source_target_pairs={{2,1},{4,3},{6,5},{8,7},{10,9},{12,11},{14,13},{18,17},{20,19},{22... | collective-permute-start | bytes 3145736 | tf_op jit(solution)/shard_map/ppermute | solution.py:515

commit v2 on v1

--- a/solution.py
+++ b/solution.py
@@ -43,24 +43,16 @@
     return high, low
 
 
-def left_table(table):
-    high, low = high_low(table)
-    return np.concatenate([high, low, high], axis=1)
-
-
-def right_table(table):
-    high, low = high_low(table)
-    return np.concatenate([high, high, low], axis=0)
-
-
 def make_tables():
     even, odd = real_tables()
-    left = np.stack([left_table(m) for m in (even, odd, even.T, odd.T)])
-    right = np.stack([right_table(m) for m in (even.T, odd.T, even, odd)])
+    forms = np.stack([np.stack(high_low(m)) for m in (even, odd, even.T, odd.T)])
     order = np.concatenate([np.arange(0, WIN, 2), np.arange(1, WIN, 2)])
     shuffle = np.zeros((WIN, WIN), np.float32)
     shuffle[order, np.arange(WIN)] = 1.0
-    return left, right, np.concatenate([shuffle, shuffle], axis=0).astype(bf16)
+    return forms, shuffle.astype(bf16)
+
+
+EVEN, ODD, EVEN_T, ODD_T = range(4)
 
 
 def split(x):
@@ -68,47 +60,46 @@
     return high, (x - high.astype(f32)).astype(bf16)
 
 
-def left_mul(table, x):
+def left_mul(forms, which, x):
     high, low = split(x)
-    return jnp.dot(table, jnp.concatenate([high, high, low], axis=0), preferred_element_type=f32)
-
-
-def right_mul(x, table):
+    t_high, t_low = forms[which, 0], forms[which, 1]
+    wide = jnp.concatenate([t_high, t_low, t_high], axis=1)
+    return jnp.dot(wide, jnp.concatenate([high, high, low], axis=0), preferred_element_type=f32)
+
+
+def right_mul(x, forms, which):
     high, low = split(x)
-    return jnp.dot(jnp.concatenate([high, low, high], axis=1), table, preferred_element_type=f32)
-
-
-def rows_forward(re, im, left, cols):
-    def halves(x):
-        return x[:HALF], x[HALF:]
-
-    tr, br = halves(re)
-    ti, bi = halves(im)
-    e = left_mul(left[0], jnp.concatenate([tr + br, ti + bi], axis=0))
-    o = left_mul(left[1], jnp.concatenate([tr - br, ti - bi], axis=0))
+    t_high, t_low = forms[which, 0], forms[which, 1]
+    tall = jnp.concatenate([t_high, t_high, t_low], axis=0)
+    return jnp.dot(jnp.concatenate([high, low, high], axis=1), tall, preferred_element_type=f32)
+
+
+def rows_forward(re, im, forms):
+    tr, br, ti, bi = re[:HALF], re[HALF:], im[:HALF], im[HALF:]
+    e = left_mul(forms, EVEN, jnp.concatenate([tr + br, ti + bi], axis=0))
+    o = left_mul(forms, ODD, jnp.concatenate([tr - br, ti - bi], axis=0))
     return e, o
 
 
-def rows_inverse(xr, xi, left):
-    u = left_mul(left[2], jnp.concatenate([xr[:HALF], xi[:HALF]], axis=0))
-    v = left_mul(left[3], jnp.concatenate([xr[HALF:], xi[HALF:]], axis=0))
+def rows_inverse(re, im, forms):
+    u = left_mul(forms, EVEN_T, jnp.concatenate([re[:HALF], im[:HALF]], axis=0))
+    v = left_mul(forms, ODD_T, jnp.concatenate([re[HALF:], im[HALF:]], axis=0))
     return u, v
 
 
-def lanes_forward(re, im, right):
-    lr, rr = re[:, :HALF], re[:, HALF:]
-    li, ri = im[:, :HALF], im[:, HALF:]
-    e = right_mul(jnp.concatenate([lr + rr, li + ri], axis=1), right[0])
-    o = right_mul(jnp.concatenate([lr - rr, li - ri], axis=1), right[1])
+def lanes_forward(re, im, forms):
+    lr, rr, li, ri = re[:, :HALF], re[:, HALF:], im[:, :HALF], im[:, HALF:]
+    e = right_mul(jnp.concatenate([lr + rr, li + ri], axis=1), forms, EVEN_T)
+    o = right_mul(jnp.concatenate([lr - rr, li - ri], axis=1), forms, ODD_T)
     return (
         jnp.concatenate([e[:, :HALF], o[:, :HALF]], axis=1),
         jnp.concatenate([e[:, HALF:], o[:, HALF:]], axis=1),
     )
 
 
-def lanes_inverse(re, im, right):
-    u = right_mul(jnp.concatenate([re[:, :HALF], im[:, :HALF]], axis=1), right[2])
-    v = right_mul(jnp.concatenate([re[:, HALF:], im[:, HALF:]], axis=1), right[3])
+def lanes_inverse(re, im, forms):
+    u = right_mul(jnp.concatenate([re[:, :HALF], im[:, :HALF]], axis=1), forms, EVEN)
+    v = right_mul(jnp.concatenate([re[:, HALF:], im[:, HALF:]], axis=1), forms, ODD)
     return (
         jnp.concatenate([u[:, :HALF] + v[:, :HALF], u[:, :HALF] - v[:, :HALF]], axis=1),
         jnp.concatenate([u[:, HALF:] + v[:, HALF:], u[:, HALF:] - v[:, HALF:]], axis=1),
@@ -123,9 +114,12 @@
     return ar * br + ai * bi, ar * bi - ai * br
 
 
-def decide_kernel(offsets, live, table):
-    count = live[0]
-    rows = [jnp.bitwise_and(offsets[j, 0], WIN - 1) for j in range(CAP)]
+INFO = 16
+
+
+def decide(info, table):
+    count = info[2 * CAP]
+    rows = [jnp.bitwise_and(info[2 * j], WIN - 1) for j in range(CAP)]
     used = [(j < count).astype(jnp.int32) for j in range(CAP)]
     on_a = [used[j] * ((rows[j] + SUB - 1) // SUB) for j in range(CAP)]
     on_b = [used[j] * (GROUPS - rows[j] // SUB + INT_GROUPS) for j in range(CAP)]
@@ -151,15 +145,12 @@
         to_a = used[j] - to_b
         table[FIELDS * j] = to_a * AT_A + to_b * AT_B
         table[FIELDS * j + 1] = rows[j]
-        table[FIELDS * j + 2] = offsets[j, 1]
+        table[FIELDS * j + 2] = info[2 * j + 1]
         table[FIELDS * j + 3] = jnp.where(to_b == 1, at_b, at_a)
         table[FIELDS * j + 4] = jnp.where(to_b == 1, back, at_a)
         at_a = at_a + to_a * on_a[j]
         at_b = at_b + to_b * on_b[j]
         back = back + to_b * (on_b[j] - INT_GROUPS)
-        table[FIELDS * j + 5] = 0
-        table[FIELDS * j + 6] = 0
-        table[FIELDS * j + 7] = 0
 
 
 def slot_of(table, j):
@@ -193,7 +184,7 @@
     total[plane, rows, pl.ds(starts[2], LANES)] += jnp.where(inside, 0.0, left)
 
 
-def pack_to_b_kernel(table, field, intensity, out):
+def pack_to_b(table, field, intensity, out):
     for j in range(CAP):
         state, row, col, start, _ = slot_of(table, j)
 
@@ -222,7 +213,7 @@
             lax.fori_loop(0, INT_GROUPS, body_int, 0)
 
 
-def pack_to_a_kernel(table, field, out):
+def pack_to_a(table, field, out):
     for j in range(CAP):
         state, row, col, start, _ = slot_of(table, j)
 
@@ -238,6 +229,44 @@
                 return carry
 
             lax.fori_loop(0, (row + SUB - 1) // SUB, body, 0)
+
+
+def pack_early_kernel(odd, own, field, intensity, out, table):
+    @pl.when(odd[0] == 1)
+    def _():
+        decide(own, table)
+        pack_to_b(table, field, intensity, out)
+
+
+def pack_late_kernel(odd, own, before, field, intensity, out, inner, table_in, table_out):
+    @pl.when(odd[0] == 0)
+    def _():
+        decide(own, table_in)
+        decide(before, table_out)
+        pack_to_a(table_out, field, out)
+        pack_to_b(table_in, field, intensity, inner)
+
+    @pl.when(odd[0] == 1)
+    def _():
+        decide(before, table_in)
+        decide(own, table_out)
+        pack_to_a(table_in, field, inner)
+
+
+def prepare_kernel(phases, shuffle, out, halves):
+    for plane in range(2):
+        halves[0] = phases[plane, :, :LANES]
+        halves[1] = phases[plane, :, LANES:]
+        for part in range(2):
+            every = pl.ds(part, HALF, stride=2)
+            x = jnp.concatenate([halves[0, every, :], halves[1, every, :]], axis=1)
+            high = x.astype(bf16)
+            rest = x - high.astype(f32)
+            middle, low = split(rest)
+            total = jnp.dot(high, shuffle[...], preferred_element_type=f32)
+            total += jnp.dot(middle, shuffle[...], preferred_element_type=f32)
+            total += jnp.dot(low, shuffle[...], preferred_element_type=f32)
+            out[plane, part * HALF : (part + 1) * HALF, :] = total
 
 
 def slots_kernel(
@@ -248,8 +277,7 @@
     intensity,
     probe,
     kernel,
-    left,
-    right,
+    forms,
     shuffle,
     from_b,
     from_a,
@@ -349,9 +377,9 @@
             def middle(pointwise):
                 for half in range(2):
                     rows = pl.ds(half * HALF, HALF)
-                    re, im = lanes_forward(work[0, rows, :], work[1, rows, :], right)
+                    re, im = lanes_forward(work[0, rows, :], work[1, rows, :], forms)
                     re, im = pointwise(half, rows, re, im)
-                    re, im = lanes_inverse(re, im, right)
+                    re, im = lanes_inverse(re, im, forms)
                     work[0, rows, :], work[1, rows, :] = re, im
 
             def unstack(u, v):
@@ -370,26 +398,25 @@
                 every = pl.ds(half, HALF, stride=2)
                 rows_of = jnp.concatenate([measured[0, every, :], measured[1, every, :]], axis=1)
                 high, low_part = split(rows_of)
-                wanted = jnp.dot(
-                    jnp.concatenate([high, low_part], axis=1), shuffle[...], preferred_element_type=f32
-                )
+                wanted = jnp.dot(high, shuffle[...], preferred_element_type=f32)
+                wanted += jnp.dot(low_part, shuffle[...], preferred_element_type=f32)
                 scale = re * re + im * im - wanted
                 return scale * re, scale * im
 
             re, im = cmul(beam[0], beam[1], tile[0], tile[1])
-            store_rows(*rows_forward(re, im, left, None))
+            store_rows(*rows_forward(re, im, forms))
             middle(propagate)
-            re, im = unstack(*rows_inverse(work[0], work[1], left))
+            re, im = unstack(*rows_inverse(work[0], work[1], forms))
             entered[0], entered[1] = re, im
             re, im = cmul(re, im, tile[2], tile[3])
-            store_rows(*rows_forward(re, im, left, None))
+            store_rows(*rows_forward(re, im, forms))
             middle(residual)
-            br, bi = unstack(*rows_inverse(work[0], work[1], left))
+            br, bi = unstack(*rows_inverse(work[0], work[1], forms))
             re, im = cmul_conj(tile[2], tile[3], br, bi)
             tile[2], tile[3] = cmul_conj(entered[0], entered[1], br, bi)
-            store_rows(*rows_forward(re, im, left, None))
+            store_rows(*rows_forward(re, im, forms))
             middle(propagate_back)
-            br, bi = unstack(*rows_inverse(work[0], work[1], left))
+            br, bi = unstack(*rows_inverse(work[0], work[1], forms))
             tile[0], tile[1] = cmul_conj(beam[0], beam[1], br, bi)
 
             def scatter(group, carry):
@@ -481,8 +508,7 @@
 
 
 def run_slots(first_kind, role, table, field, intensity, probe, kernel, tables, from_b, from_a, total):
-    left, right, shuffle = tables
-    specs = [spec(SM)] * 2 + [spec(VM)] * 7 + [spec(pl.ANY)] * 3
+    specs = [spec(SM)] * 2 + [spec(VM)] * 6 + [spec(pl.ANY)] * 3
     return pl.pallas_call(
         functools.partial(slots_kernel, first_kind),
         out_shape=(
@@ -503,7 +529,7 @@
             pltpu.SemaphoreType.DMA,
         ],
         compiler_params=PARAMS,
-    )(role, table, field, intensity, probe, kernel, left, right, shuffle, from_b, from_a, total)
+    )(role, table, field, intensity, probe, kernel, *tables, from_b, from_a, total)
 
 
 def shards(obj_field, probe_wave, prop_phase, win_offsets, live_counts, intensity):
@@ -517,40 +543,41 @@
     role_in = odd.reshape(1)
     role_out = (1 - odd).reshape(1)
 
-    own = pl.pallas_call(
-        decide_kernel,
-        out_shape=jax.ShapeDtypeStruct((CAP * FIELDS,), jnp.int32),
-        in_specs=[spec(SM)] * 2,
-        out_specs=spec(SM),
-    )(win_offsets, live_counts)
+    flag = odd.reshape(1)
+    own = jnp.concatenate([win_offsets.reshape(-1), live_counts, jnp.zeros((INFO - 2 * CAP - 1,), jnp.int32)])
     before = move(own, within + across)
     to_b = pl.pallas_call(
-        pack_to_b_kernel,
+        pack_early_kernel,
         out_shape=packed(CAP_FWD),
-        in_specs=[spec(SM), spec(VM), spec(VM)],
+        in_specs=[spec(SM)] * 2 + [spec(VM)] * 2,
         out_specs=spec(VM),
+        scratch_shapes=[pltpu.SMEM((CAP * FIELDS,), jnp.int32)],
         compiler_params=PARAMS,
-    )(own, field, intensity)
-    in_from_a = move(to_b, within)
+    )(flag, own, field, intensity)
     out_from_a = move(to_b, across)
-    to_a = pl.pallas_call(
-        pack_to_a_kernel,
-        out_shape=packed(CAP_FWD),
-        in_specs=[spec(SM), spec(VM)],
+    table = jax.ShapeDtypeStruct((CAP * FIELDS,), jnp.int32)
+    to_a, inner, table_in, table_out = pl.pallas_call(
+        pack_late_kernel,
+        out_shape=(packed(CAP_FWD), packed(CAP_FWD), table, table),
+        in_specs=[spec(SM)] * 3 + [spec(VM)] * 2,
+        out_specs=(spec(VM), spec(VM), spec(SM), spec(SM)),
+        compiler_params=PARAMS,
+    )(flag, own, before, field, intensity)
+    out_from_b = move(to_a, back(across))
+    in_from = move(inner, within + back(within))
+
+    forms, shuffle = (jnp.asarray(t) for t in make_tables())
+    kernel = pl.pallas_call(
+        prepare_kernel,
+        out_shape=jax.ShapeDtypeStruct((2, WIN, WIN), f32),
+        in_specs=[spec(VM)] * 2,
         out_specs=spec(VM),
+        scratch_shapes=[pltpu.VMEM((2, WIN, LANES), f32)],
         compiler_params=PARAMS,
-    )(before, field)
-    in_from_b = move(to_a, back(within))
-    out_from_b = move(to_a, back(across))
-    table_in = jnp.where(odd == 0, own, before)
-    table_out = jnp.where(odd == 0, before, own)
-
-    phase = prop_phase.reshape(HALF, 2, HALF, 2).transpose(1, 0, 3, 2).reshape(WIN, WIN)
-    kernel = jnp.stack([jnp.cos(phase), jnp.sin(phase)])
-    tables = tuple(jnp.asarray(t) for t in make_tables())
-
-    args = (field, intensity, probe_wave, kernel, tables)
-    total, in_back_a, in_back_b = run_slots(True, role_in, table_in, *args, in_from_b, in_from_a, field)
+    )(jnp.stack([jnp.cos(prop_phase), jnp.sin(prop_phase)]), shuffle)
+
+    args = (field, intensity, probe_wave, kernel, (forms, shuffle))
+    total, in_back_a, in_back_b = run_slots(True, role_in, table_in, *args, in_from, in_from, field)
     in_a = move(in_back_a, within)
     in_b = move(in_back_b, back(within))
     total, out_back_a, out_back_b = run_slots(False, role_out, table_out, *args, out_from_b, out_from_a, total)

time: 166 us -> 114 us (0.69)
  the two profiles are of different devices: /device:TPU:20 before, /device:TPU:14 now
where the time goes in v2:
time: 114 us; the launch traced here: 112 us
  Pallas kernels  47 us (41%)
  waiting for transfers between devices  42.7 us (37%)
  starting transfers between devices  18.4 us (16%)
  local copies, waits for them, and re-layouts  3.04 us (3%)
    ppermute x8, waiting for transfers between devices, shards(): move = lambda x, pairs: lax.ppermute(x, 'row', pairs)  42.7 us
    pallas_call x2, Pallas kernels, run_slots(): pl.pallas_call(functools.partial(slots_kernel, first_kind), out_shape=(ja...  32.5 us
    ppermute x8, starting transfers between devices, shards(): move = lambda x, pairs: lax.ppermute(x, 'row', pairs)  18.4 us
    pallas_call x1, Pallas kernels, shards(): pl.pallas_call(finish_kernel, out_shape=jax.ShapeDtypeStruct(field.shape,...  5.97 us
    pallas_call x1, Pallas kernels, shards(): pl.pallas_call(pack_late_kernel, out_shape=(packed(CAP_FWD), packed(CAP_F...  4.7 us
    pallas_call x1, Pallas kernels, shards(): pl.pallas_call(pack_early_kernel, out_shape=packed(CAP_FWD), in_specs=[sp...  3.39 us
  transfers between devices with their start and end apart: 8, of which 4 were waited for; matrix products, arithmetic and copies ran while one was open for 1% of the time, Pallas kernels for 14%

profile of v2, /device:TPU:14, one launch (start us, length us, event | category | flops | bytes accessed | tf_op | source)
XLA Modules:
  0.0 112.1 jit_solution(3445706136349650051)
XLA Ops:
  0.7 0.8 copy.11
  1.4 0.1 reshape.17
  1.5 0.1 pad_add_fusion.own
  1.6 1.9 %collective-permute-start = (s32[16]{0:T(128)S(1)}, s32[16]{0:T(128)S(1)}, u32[]{:S(2)}, u32[]{:S(2)}) collective-permute-start(s32[16]{0:T(128)S(1)} %pad_add_fusion.own), channel_id=1, source_target_pairs={{0,1},{2,3},{4,5},{6,7},{8,9},{10,11},{12,13},{14,15},{1,2},{3,4},... | collective-permute-start | bytes 200 | tf_op jit(solution)/shard_map/ppermute | solution.py:541
  3.5 2.9 %collective-permute-done.before = s32[16]{0:T(128)S(1)} collective-permute-done((s32[16]{0:T(128)S(1)}, s32[16]{0:T(128)S(1)}, u32[]{:S(2)}, u32[]{:S(2)}) %collective-permute-start) | collective-permute-done | bytes 96 | tf_op jit(solution)/shard_map/ppermute | solution.py:541
  6.4 1.2 %copy-done = f32[4,256,256]{2,1,0:T(8,128)S(1)} copy-done((f32[4,256,256]{2,1,0:T(8,128)S(1)}, f32[4,256,256]{2,1,0:T(8,128)}, u32[]{:S(2)}) %copy-start) | copy-done | bytes 1048600
  7.7 4.7 %shard_map.82 = (f32[48,4,8,256]{3,2,1,0:T(8,128)}, f32[48,4,8,256]{3,2,1,0:T(8,128)}, s32[32]{0:T(128)S(1)}, s32[32]{0:T(128)S(1)}) custom-call(s32[1]{0:T(128)} %bitcast.odd.role.role_in, s32[16]{0:T(128)S(1)} %pad_add_fusion.own, s32[16]{0:T(128)S(1)} %collective-permute-done.before, f32[4,256,1024]{2,1,0:T(8,128)} %bitcast.8, f32[4,256,256]{2,1,0:T(8,128)S(1)} %copy-done), custom_call_target="tpu_custom_call" | custom-call | tf_op jit(solution)/shard_map/pallas_call | solution.py:559
  12.4 0.0 copy-start.5
  12.4 0.1 collective-permute-start.3
  12.5 3.4 %shard_map.84 = f32[48,4,8,256]{3,2,1,0:T(8,128)} custom-call(s32[1]{0:T(128)} %bitcast.odd.role.role_in, s32[16]{0:T(128)S(1)} %pad_add_fusion.own, f32[4,256,1024]{2,1,0:T(8,128)} %bitcast.9, f32[4,256,256]{2,1,0:T(8,128)S(1)} %copy-done.1), custom_call_target="tpu_custom_call" | custom-call | tf_op jit(solution)/shard_map/pallas_call | solution.py:549
  15.9 1.4 %collective-permute-start.2 = (f32[48,4,8,256]{3,2,1,0:T(8,128)}, f32[48,4,8,256]{3,2,1,0:T(8,128)}, u32[]{:S(2)}, u32[]{:S(2)}) collective-permute-start(f32[48,4,8,256]{3,2,1,0:T(8,128)} %shard_map.84), channel_id=1, source_target_pairs={{1,2},{3,4},{5,6},{7,8},{9,10},{11,12},{13,14},{17,18},{19,20},{21... | collective-permute-start | bytes 4718600 | tf_op jit(solution)/shard_map/ppermute | solution.py:541
  17.3 6.7 %collective-permute-start.1 = (f32[48,4,8,256]{3,2,1,0:T(8,128)}, f32[48,4,8,256]{3,2,1,0:T(8,128)}, u32[]{:S(2)}, u32[]{:S(2)}) collective-permute-start(f32[48,4,8,256]{3,2,1,0:T(8,128)} %get-tuple-element.17), channel_id=1, source_target_pairs={{2,1},{4,3},{6,5},{8,7},{10,9},{12,11},{14,13},{18,17},{20,19},{22... | collective-permute-start | bytes 4718600 | tf_op jit(solution)/shard_map/ppermute | solution.py:541
  24.0 0.9 cosine_bitcast_fusion
  25.0 0.4 shard_map.83.kernel
  25.4 12.1 %shard_map.85 = (f32[4,256,1024]{2,1,0:T(8,128)}, f32[48,4,8,256]{3,2,1,0:T(8,128)S(1)}, f32[32,4,8,256]{3,2,1,0:T(8,128)S(1)}) custom-call(s32[1]{0:T(128)} %bitcast.odd.role.role_in, s32[32]{0:T(128)S(1)} %get-tuple-element.15.table.table_in, f32[4,256,1024]{2,1,0:T(8,128)} %bitcast.10, f32[4,256,256]{2,1,0:T(8,128)S(1)} %copy-done.1, ...), custom_call_target="tpu_custom_call" | custom-call | tf_op jit(solution)/shard_map/pallas_call | solution.py:512
  37.5 17.4 %collective-permute-done.2.from_a = f32[48,4,8,256]{3,2,1,0:T(8,128)} collective-permute-done((f32[48,4,8,256]{3,2,1,0:T(8,128)}, f32[48,4,8,256]{3,2,1,0:T(8,128)}, u32[]{:S(2)}, u32[]{:S(2)}) %collective-permute-start.2) | collective-permute-done | bytes 1572896 | tf_op jit(solution)/shard_map/ppermute | solution.py:541
  54.9 20.4 %shard_map.86 = (f32[4,256,1024]{2,1,0:T(8,128)}, f32[48,4,8,256]{3,2,1,0:T(8,128)S(1)}, f32[32,4,8,256]{3,2,1,0:T(8,128)S(1)}) custom-call(s32[1]{0:T(128)} %bitcast.2.role.role_out, s32[32]{0:T(128)S(1)} %get-tuple-element.16.table.table_out, f32[4,256,1024]{2,1,0:T(8,128)} %bitcast.12, f32[4,256,256]{2,1,0:T(8,128)S(1)} %copy-done.1, ...), custom_call_target="tpu_custom_call" | custom-call | tf_op jit(solution)/shard_map/pallas_call | solution.py:512
  75.3 1.3 %collective-permute-start.6 = (f32[48,4,8,256]{3,2,1,0:T(8,128)S(1)}, f32[48,4,8,256]{3,2,1,0:T(8,128)S(1)}, u32[]{:S(2)}, u32[]{:S(2)}) collective-permute-start(f32[48,4,8,256]{3,2,1,0:T(8,128)S(1)} %get-tuple-element.23), channel_id=1, source_target_pairs={{1,2},{3,4},{5,6},{7,8},{9,10},{11,12},{13,14},{17,18},{19,20},{21... | collective-permute-start | bytes 4718600 | tf_op jit(solution)/shard_map/ppermute | solution.py:541
  76.6 1.4 %collective-permute-start.4 = (f32[48,4,8,256]{3,2,1,0:T(8,128)S(1)}, f32[48,4,8,256]{3,2,1,0:T(8,128)S(1)}, u32[]{:S(2)}, u32[]{:S(2)}) collective-permute-start(f32[48,4,8,256]{3,2,1,0:T(8,128)S(1)} %get-tuple-element.21), channel_id=1, source_target_pairs={{0,1},{2,3},{4,5},{6,7},{8,9},{10,11},{12,13},{14,15},{16,17},{18,... | collective-permute-start | bytes 4718600 | tf_op jit(solution)/shard_map/ppermute | solution.py:541
  78.0 4.3 %collective-permute-start.7 = (f32[32,4,8,256]{3,2,1,0:T(8,128)S(1)}, f32[32,4,8,256]{3,2,1,0:T(8,128)S(1)}, u32[]{:S(2)}, u32[]{:S(2)}) collective-permute-start(f32[32,4,8,256]{3,2,1,0:T(8,128)S(1)} %get-tuple-element.24), channel_id=1, source_target_pairs={{2,1},{4,3},{6,5},{8,7},{10,9},{12,11},{14,13},{18,17},{20,19},{22... | collective-permute-start | bytes 3145736 | tf_op jit(solution)/shard_map/ppermute | solution.py:541
  82.4 1.3 %collective-permute-start.5 = (f32[32,4,8,256]{3,2,1,0:T(8,128)S(1)}, f32[32,4,8,256]{3,2,1,0:T(8,128)S(1)}, u32[]{:S(2)}, u32[]{:S(2)}) collective-permute-start(f32[32,4,8,256]{3,2,1,0:T(8,128)S(1)} %get-tuple-element.22), channel_id=1, source_target_pairs={{1,0},{3,2},{5,4},{7,6},{9,8},{11,10},{13,12},{15,14},{17,16},{19,... | collective-permute-start | bytes 3145736 | tf_op jit(solution)/shard_map/ppermute | solution.py:541
  83.7 10.9 %collective-permute-done.7.out_b = f32[32,4,8,256]{3,2,1,0:T(8,128)S(1)} collective-permute-done((f32[32,4,8,256]{3,2,1,0:T(8,128)S(1)}, f32[32,4,8,256]{3,2,1,0:T(8,128)S(1)}, u32[]{:S(2)}, u32[]{:S(2)}) %collective-permute-start.7) | collective-permute-done | bytes 1048608 | tf_op jit(solution)/shard_map/ppermute | solution.py:541
  94.6 11.5 %collective-permute-done.6.out_a = f32[48,4,8,256]{3,2,1,0:T(8,128)S(1)} collective-permute-done((f32[48,4,8,256]{3,2,1,0:T(8,128)S(1)}, f32[48,4,8,256]{3,2,1,0:T(8,128)S(1)}, u32[]{:S(2)}, u32[]{:S(2)}) %collective-permute-start.6) | collective-permute-done | bytes 1572896 | tf_op jit(solution)/shard_map/ppermute | solution.py:541
  106.1 6.0 %shard_map.87 = f32[4,256,1024]{2,1,0:T(8,128)} custom-call(s32[1]{0:T(128)} %bitcast.odd.role.role_in, s32[32]{0:T(128)S(1)} %get-tuple-element.15.table.table_in, s32[1]{0:T(128)} %bitcast.2.role.role_out, s32[32]{0:T(128)S(1)} %get-tuple-element.16.table.table_out, f32[4,256,1024]{2,1,0:T(8,128)} %get-tuple-element.20.total_in, ...), custom_call_target="tpu_custom_call", output_to_operand_aliasing={{}: (4, {})} | custom-call | tf_op jit(solution)/shard_map/pallas_call | solution.py:586
  (16 shorter events, 0.1 us)
Async XLA Ops:
  1.6 4.9 %collective-permute-start = (s32[16]{0:T(128)S(1)}, s32[16]{0:T(128)S(1)}, u32[]{:S(2)}, u32[]{:S(2)}) collective-permute-start(s32[16]{0:T(128)S(1)} %pad_add_fusion.own), channel_id=1, source_target_pairs={{0,1},{2,3},{4,5},{6,7},{8,9},{10,11},{12,13},{14,15},{1,2},{3,4},... | collective-permute-start | bytes 200 | tf_op jit(solution)/shard_map/ppermute | solution.py:541
  6.4 1.2 %copy-start = (f32[4,256,256]{2,1,0:T(8,128)S(1)}, f32[4,256,256]{2,1,0:T(8,128)}, u32[]{:S(2)}) copy-start(f32[4,256,256]{2,1,0:T(8,128)} %intensity.7) | copy-start | bytes 3145732
  7.7 4.8 %copy-start.1 = (f32[4,256,256]{2,1,0:T(8,128)S(1)}, f32[4,256,256]{2,1,0:T(8,128)}, u32[]{:S(2)}) copy-start(f32[4,256,256]{2,1,0:T(8,128)} %intensity.7) | copy-start | bytes 3145732
  12.4 11.6 %copy-start.5 = (f32[256,256]{1,0:T(8,128)S(1)}, f32[256,256]{1,0:T(8,128)}, u32[]{:S(2)}) copy-start(f32[256,256]{1,0:T(8,128)} %param.10) | copy-start | bytes 786436
  12.4 13.0 %collective-permute-start.3 = (f32[48,4,8,256]{3,2,1,0:T(8,128)}, f32[48,4,8,256]{3,2,1,0:T(8,128)}, u32[]{:S(2)}, u32[]{:S(2)}) collective-permute-start(f32[48,4,8,256]{3,2,1,0:T(8,128)} %get-tuple-element.18), channel_id=1, source_target_pairs={{0,1},{2,3},{4,5},{6,7},{8,9},{10,11},{12,13},{14,15},{1,0},{3,2},... | collective-permute-start | bytes 4718600 | tf_op jit(solution)/shard_map/ppermute | solution.py:541
  15.9 9.1 %copy-start.4 = (bf16[256,256]{1,0:T(8,128)(2,1)S(1)}, bf16[256,256]{1,0:T(8,128)(2,1)}, u32[]{:S(2)}) copy-start(bf16[256,256]{1,0:T(8,128)(2,1)} %constant.13.clone.shuffle) | copy-start | bytes 393220
  15.9 9.6 %copy-start.2 = (bf16[4,2,256,256]{3,2,1,0:T(8,128)(2,1)S(1)}, bf16[4,2,256,256]{3,2,1,0:T(8,128)(2,1)}, u32[]{:S(2)}) copy-start(bf16[4,2,256,256]{3,2,1,0:T(8,128)(2,1)} %constant.12.clone.forms) | copy-start | bytes 3145732
  15.9 9.6 %copy-start.3 = (f32[2,256,256]{2,1,0:T(8,128)S(1)}, f32[2,256,256]{2,1,0:T(8,128)}, u32[]{:S(2)}) copy-start(f32[2,256,256]{2,1,0:T(8,128)} %probe.3) | copy-start | bytes 1572868
  15.9 39.0 %collective-permute-start.2 = (f32[48,4,8,256]{3,2,1,0:T(8,128)}, f32[48,4,8,256]{3,2,1,0:T(8,128)}, u32[]{:S(2)}, u32[]{:S(2)}) collective-permute-start(f32[48,4,8,256]{3,2,1,0:T(8,128)} %shard_map.84), channel_id=1, source_target_pairs={{1,2},{3,4},{5,6},{7,8},{9,10},{11,12},{13,14},{17,18},{19,20},{21... | collective-permute-start | bytes 4718600 | tf_op jit(solution)/shard_map/ppermute | solution.py:541
  17.3 37.6 %collective-permute-start.1 = (f32[48,4,8,256]{3,2,1,0:T(8,128)}, f32[48,4,8,256]{3,2,1,0:T(8,128)}, u32[]{:S(2)}, u32[]{:S(2)}) collective-permute-start(f32[48,4,8,256]{3,2,1,0:T(8,128)} %get-tuple-element.17), channel_id=1, source_target_pairs={{2,1},{4,3},{6,5},{8,7},{10,9},{12,11},{14,13},{18,17},{20,19},{22... | collective-permute-start | bytes 4718600 | tf_op jit(solution)/shard_map/ppermute | solution.py:541
  75.3 30.8 %collective-permute-start.6 = (f32[48,4,8,256]{3,2,1,0:T(8,128)S(1)}, f32[48,4,8,256]{3,2,1,0:T(8,128)S(1)}, u32[]{:S(2)}, u32[]{:S(2)}) collective-permute-start(f32[48,4,8,256]{3,2,1,0:T(8,128)S(1)} %get-tuple-element.23), channel_id=1, source_target_pairs={{1,2},{3,4},{5,6},{7,8},{9,10},{11,12},{13,14},{17,18},{19,20},{21... | collective-permute-start | bytes 4718600 | tf_op jit(solution)/shard_map/ppermute | solution.py:541
  76.6 29.5 %collective-permute-start.4 = (f32[48,4,8,256]{3,2,1,0:T(8,128)S(1)}, f32[48,4,8,256]{3,2,1,0:T(8,128)S(1)}, u32[]{:S(2)}, u32[]{:S(2)}) collective-permute-start(f32[48,4,8,256]{3,2,1,0:T(8,128)S(1)} %get-tuple-element.21), channel_id=1, source_target_pairs={{0,1},{2,3},{4,5},{6,7},{8,9},{10,11},{12,13},{14,15},{16,17},{18,... | collective-permute-start | bytes 4718600 | tf_op jit(solution)/shard_map/ppermute | solution.py:541
  78.0 16.6 %collective-permute-start.7 = (f32[32,4,8,256]{3,2,1,0:T(8,128)S(1)}, f32[32,4,8,256]{3,2,1,0:T(8,128)S(1)}, u32[]{:S(2)}, u32[]{:S(2)}) collective-permute-start(f32[32,4,8,256]{3,2,1,0:T(8,128)S(1)} %get-tuple-element.24), channel_id=1, source_target_pairs={{2,1},{4,3},{6,5},{8,7},{10,9},{12,11},{14,13},{18,17},{20,19},{22... | collective-permute-start | bytes 3145736 | tf_op jit(solution)/shard_map/ppermute | solution.py:541
  82.4 12.2 %collective-permute-start.5 = (f32[32,4,8,256]{3,2,1,0:T(8,128)S(1)}, f32[32,4,8,256]{3,2,1,0:T(8,128)S(1)}, u32[]{:S(2)}, u32[]{:S(2)}) collective-permute-start(f32[32,4,8,256]{3,2,1,0:T(8,128)S(1)} %get-tuple-element.22), channel_id=1, source_target_pairs={{1,0},{3,2},{5,4},{7,6},{9,8},{11,10},{13,12},{15,14},{17,16},{19,... | collective-permute-start | bytes 3145736 | tf_op jit(solution)/shard_map/ppermute | solution.py:541

commit v3 on v2

--- a/solution.py
+++ b/solution.py
@@ -18,6 +18,7 @@
 CAP_FWD = 48
 CAP_BACK_A = 48
 CAP_BACK_B = 32
+UNEVEN = 24
 DEAD, AT_A, AT_B = 0, 1, 2
 FIELDS = 8
 f32 = jnp.float32
@@ -127,12 +128,18 @@
     for mask in range(1 << CAP):
         total_a = jnp.int32(0)
         total_b = jnp.int32(0)
+        slots_a = jnp.int32(0)
+        slots_b = jnp.int32(0)
         for j in range(CAP):
             if mask >> j & 1:
                 total_b = total_b + on_b[j]
+                slots_b = slots_b + used[j]
             else:
                 total_a = total_a + on_a[j]
+                slots_a = slots_a + used[j]
         cost = jnp.maximum(total_a, total_b)
+        cost = cost + jnp.where(cost > CAP_FWD, 1000, 0)
+        cost = cost + jnp.where(jnp.maximum(slots_a, slots_b) > 2, UNEVEN, 0)
         better = cost < best
         best = jnp.where(better, cost, best)
         chosen = jnp.where(better, mask, chosen)
@@ -269,225 +276,238 @@
             out[plane, part * HALF : (part + 1) * HALF, :] = total
 
 
-def slots_kernel(
-    first_kind,
-    role,
-    table,
-    field,
-    intensity,
-    probe,
-    kernel,
-    forms,
-    shuffle,
-    from_b,
-    from_a,
-    total_in,
-    total,
-    back_a,
-    back_b,
-    got,
-    tile,
-    measured,
-    twice,
-    beam,
-    work,
-    entered,
-    sem,
-):
+def slots_kernel(joint, role, table, field, intensity, probe, kernel, forms, shuffle, from_b, from_a, *rest):
+    back_a, back_b = rest[0], rest[0 if joint else 1]
+    tiles, got, tile, measured, twice, beam, work, entered, chosen, got_sem, tile_sem = rest[1 if joint else 2 :]
     is_a = role[0] == 0
     mine = jnp.where(is_a, AT_A, AT_B)
 
-    def fetch(source):
-        copy = pltpu.make_async_copy(source, got, sem)
-        copy.start()
-        copy.wait()
-
     @pl.when(is_a)
     def _():
-        fetch(from_b)
+        pltpu.make_async_copy(from_b, got, got_sem).start()
 
     @pl.when(jnp.logical_not(is_a))
     def _():
-        fetch(from_a)
-
-    if first_kind:
-        total[...] = jnp.zeros_like(total)
-    else:
-        copy = pltpu.make_async_copy(total_in, total, sem)
-        copy.start()
-        copy.wait()
+        pltpu.make_async_copy(from_a, got, got_sem).start()
+
     for plane in range(2):
         for part in range(2):
             cut = probe[plane, :, part * LANES : (part + 1) * LANES]
             twice[2 * plane + part, :WIN] = cut
             twice[2 * plane + part, WIN:] = cut
-
-    def slot_body(j, carry):
-        state, row, col, start, back = slot_of(table, j)
+    found = jnp.int32(0)
+    for j in range(CAP):
+        chosen[j] = 0
+    for j in range(CAP):
+        state = table[FIELDS * j]
 
         @pl.when(state == mine)
+        def _():
+            chosen[found] = j
+
+        found = found + (state == mine).astype(jnp.int32)
+    pltpu.make_async_copy(from_b, got, got_sem).wait()
+    sublane = lax.broadcasted_iota(jnp.int32, (SUB, LANES), 0)
+
+    def load(m, j):
+        _, row, col, start, _ = slot_of(table, j)
+        starts, shift = lane_blocks(col)
+        low = row // SUB
+        base = jnp.where(is_a, start, start - low)
+
+        def gather(group, carry):
+            below = (group * SUB + sublane < row).astype(jnp.int32)
+            own = below == jnp.where(is_a, 0, 1)
+            at = jnp.clip(base + group, 0, CAP_FWD - 1)
+            rows = pl.ds(pl.multiple_of(group * SUB, SUB), SUB)
+            for plane in range(4):
+                lf, rt = load_group(field, plane, group, starts, shift)
+                tile[m, plane, rows, :LANES] = jnp.where(own, lf, got[at, plane, :, :LANES])
+                tile[m, plane, rows, LANES:] = jnp.where(own, rt, got[at, plane, :, LANES:])
+            return carry
+
+        lax.fori_loop(0, GROUPS, gather, 0)
+
+        @pl.when(is_a)
+        def _():
+            measured[m, 0] = intensity[j, :, :LANES]
+            measured[m, 1] = intensity[j, :, LANES:]
+
+        @pl.when(jnp.logical_not(is_a))
+        def _():
+            after = start + GROUPS - low
+
+            def unpack(group, carry):
+                for plane in range(4):
+                    rows = pl.ds(pl.multiple_of((group * 4 + plane) * SUB, SUB), SUB)
+                    measured[m, 0, rows, :] = got[after + group, plane, :, :LANES]
+                    measured[m, 1, rows, :] = got[after + group, plane, :, LANES:]
+                return carry
+
+            lax.fori_loop(0, INT_GROUPS, unpack, 0)
+
+        for plane in range(2):
+            parts = [twice[2 * plane + part, pl.ds(WIN - row, WIN), :] for part in range(2)]
+            beam[m, plane] = pltpu.roll(jnp.concatenate(parts, axis=1), shift, 1)
+
+    def store_rows(m, e, o):
+        work[m, 0, :HALF], work[m, 1, :HALF] = e[:HALF], e[HALF:]
+        work[m, 0, HALF:], work[m, 1, HALF:] = o[:HALF], o[HALF:]
+
+    def middle(pointwise):
+        for half in range(2):
+            rows = pl.ds(half * HALF, HALF)
+            for m in range(2):
+                re, im = lanes_forward(work[m, 0, rows, :], work[m, 1, rows, :], forms)
+                re, im = pointwise(m, half, rows, re, im)
+                re, im = lanes_inverse(re, im, forms)
+                work[m, 0, rows, :], work[m, 1, rows, :] = re, im
+
+    def rows_back(m):
+        u, v = rows_inverse(work[m, 0], work[m, 1], forms)
+        return (
+            jnp.concatenate([u[:HALF] + v[:HALF], u[:HALF] - v[:HALF]], axis=0),
+            jnp.concatenate([u[HALF:] + v[HALF:], u[HALF:] - v[HALF:]], axis=0),
+        )
+
+    def propagate(m, half, rows, re, im):
+        return cmul(kernel[0, rows, :], kernel[1, rows, :], re, im)
+
+    def propagate_back(m, half, rows, re, im):
+        return cmul_conj(kernel[0, rows, :], kernel[1, rows, :], re, im)
+
+    def residual(m, half, rows, re, im):
+        every = pl.ds(half, HALF, stride=2)
+        rows_of = jnp.concatenate([measured[m, 0, every, :], measured[m, 1, every, :]], axis=1)
+        high, low = split(rows_of)
+        wanted = jnp.dot(high, shuffle[...], preferred_element_type=f32)
+        wanted += jnp.dot(low, shuffle[...], preferred_element_type=f32)
+        scale = re * re + im * im - wanted
+        return scale * re, scale * im
+
+    def write(m, j):
+        _, row, _, _, back = slot_of(table, j)
+        low = row // SUB
+
+        def send(out, offset):
+            def body(group, carry):
+                rows = pl.ds(pl.multiple_of(group * SUB, SUB), SUB)
+                for plane in range(4):
+                    out[offset + group, plane] = tile[m, plane, rows, :]
+                return carry
+
+            return body
+
+        pltpu.make_async_copy(tile.at[m], tiles.at[j], tile_sem.at[m]).start()
+
+        @pl.when(is_a)
+        def _():
+            lax.fori_loop(0, (row + SUB - 1) // SUB, send(back_a, back), 0)
+
+        @pl.when(jnp.logical_not(is_a))
+        def _():
+            lax.fori_loop(low, GROUPS, send(back_b, back - low), 0)
+
+        pltpu.make_async_copy(tile.at[m], tiles.at[j], tile_sem.at[m]).wait()
+
+    def pair(p, carry):
+        two = 2 * p + 1 < found
+        first = chosen[2 * p]
+        second = jnp.where(two, chosen[jnp.minimum(2 * p + 1, CAP - 1)], first)
+        load(0, first)
+        load(1, second)
+        for m in range(2):
+            re, im = cmul(beam[m, 0], beam[m, 1], tile[m, 0], tile[m, 1])
+            store_rows(m, *rows_forward(re, im, forms))
+        middle(propagate)
+        for m in range(2):
+            re, im = rows_back(m)
+            entered[m, 0], entered[m, 1] = re, im
+            re, im = cmul(re, im, tile[m, 2], tile[m, 3])
+            store_rows(m, *rows_forward(re, im, forms))
+        middle(residual)
+        for m in range(2):
+            br, bi = rows_back(m)
+            re, im = cmul_conj(tile[m, 2], tile[m, 3], br, bi)
+            tile[m, 2], tile[m, 3] = cmul_conj(entered[m, 0], entered[m, 1], br, bi)
+            store_rows(m, *rows_forward(re, im, forms))
+        middle(propagate_back)
+        for m in range(2):
+            br, bi = rows_back(m)
+            tile[m, 0], tile[m, 1] = cmul_conj(beam[m, 0], beam[m, 1], br, bi)
+        write(0, first)
+
+        @pl.when(two)
+        def _():
+            write(1, second)
+
+        return carry
+
+    lax.fori_loop(0, (found + 1) // 2, pair, 0)
+
+
+def add_back(role, table, got, total, planes):
+    is_a = role[0] == 0
+    theirs = jnp.where(is_a, AT_B, AT_A)
+    for j in range(CAP):
+        state, row, col, _, back = slot_of(table, j)
+
+        @pl.when(state == theirs)
         def _():
             starts, shift = lane_blocks(col)
             low = row // SUB
-            base = jnp.where(is_a, start, start - low)
+            base = jnp.where(is_a, back - low, back)
             sublane = lax.broadcasted_iota(jnp.int32, (SUB, LANES), 0)
 
-            def own_rows(group):
+            def body(group, carry):
                 below = (group * SUB + sublane < row).astype(jnp.int32)
-                return below == jnp.where(is_a, 0, 1)
-
-            def gather(group, carry):
-                own = own_rows(group)
-                at = jnp.clip(base + group, 0, CAP_FWD - 1)
-                rows = pl.ds(pl.multiple_of(group * SUB, SUB), SUB)
-                for plane in range(4):
-                    lf, rt = load_group(field, plane, group, starts, shift)
-                    tile[plane, rows, :LANES] = jnp.where(own, lf, got[at, plane, :, :LANES])
-                    tile[plane, rows, LANES:] = jnp.where(own, rt, got[at, plane, :, LANES:])
-                return carry
-
-            lax.fori_loop(0, GROUPS, gather, 0)
-
-            @pl.when(is_a)
-            def _():
-                measured[0] = intensity[j, :, :LANES]
-                measured[1] = intensity[j, :, LANES:]
-
-            @pl.when(jnp.logical_not(is_a))
-            def _():
-                after = start + GROUPS - low
-
-                def unpack(group, carry):
-                    for plane in range(4):
-                        rows = pl.ds(pl.multiple_of((group * 4 + plane) * SUB, SUB), SUB)
-                        measured[0, rows, :] = got[after + group, plane, :, :LANES]
-                        measured[1, rows, :] = got[after + group, plane, :, LANES:]
-                    return carry
-
-                lax.fori_loop(0, INT_GROUPS, unpack, 0)
-
-            for plane in range(2):
-                parts = [twice[2 * plane + part, pl.ds(WIN - row, WIN), :] for part in range(2)]
-                beam[plane] = pltpu.roll(jnp.concatenate(parts, axis=1), shift, 1)
-
-            def store_rows(e, o):
-                work[0, :HALF], work[1, :HALF] = e[:HALF], e[HALF:]
-                work[0, HALF:], work[1, HALF:] = o[:HALF], o[HALF:]
-
-            def middle(pointwise):
-                for half in range(2):
-                    rows = pl.ds(half * HALF, HALF)
-                    re, im = lanes_forward(work[0, rows, :], work[1, rows, :], forms)
-                    re, im = pointwise(half, rows, re, im)
-                    re, im = lanes_inverse(re, im, forms)
-                    work[0, rows, :], work[1, rows, :] = re, im
-
-            def unstack(u, v):
-                return (
-                    jnp.concatenate([u[:HALF] + v[:HALF], u[:HALF] - v[:HALF]], axis=0),
-                    jnp.concatenate([u[HALF:] + v[HALF:], u[HALF:] - v[HALF:]], axis=0),
-                )
-
-            def propagate(half, rows, re, im):
-                return cmul(kernel[0, rows, :], kernel[1, rows, :], re, im)
-
-            def propagate_back(half, rows, re, im):
-                return cmul_conj(kernel[0, rows, :], kernel[1, rows, :], re, im)
-
-            def residual(half, rows, re, im):
-                every = pl.ds(half, HALF, stride=2)
-                rows_of = jnp.concatenate([measured[0, every, :], measured[1, every, :]], axis=1)
-                high, low_part = split(rows_of)
-                wanted = jnp.dot(high, shuffle[...], preferred_element_type=f32)
-                wanted += jnp.dot(low_part, shuffle[...], preferred_element_type=f32)
-                scale = re * re + im * im - wanted
-                return scale * re, scale * im
-
-            re, im = cmul(beam[0], beam[1], tile[0], tile[1])
-            store_rows(*rows_forward(re, im, forms))
-            middle(propagate)
-            re, im = unstack(*rows_inverse(work[0], work[1], forms))
-            entered[0], entered[1] = re, im
-            re, im = cmul(re, im, tile[2], tile[3])
-            store_rows(*rows_forward(re, im, forms))
-            middle(residual)
-            br, bi = unstack(*rows_inverse(work[0], work[1], forms))
-            re, im = cmul_conj(tile[2], tile[3], br, bi)
-            tile[2], tile[3] = cmul_conj(entered[0], entered[1], br, bi)
-            store_rows(*rows_forward(re, im, forms))
-            middle(propagate_back)
-            br, bi = unstack(*rows_inverse(work[0], work[1], forms))
-            tile[0], tile[1] = cmul_conj(beam[0], beam[1], br, bi)
-
-            def scatter(group, carry):
-                own = own_rows(group)
-                rows = pl.ds(pl.multiple_of(group * SUB, SUB), SUB)
-                for plane in range(4):
-                    lf = jnp.where(own, tile[plane, rows, :LANES], 0.0)
-                    rt = jnp.where(own, tile[plane, rows, LANES:], 0.0)
+                own = below == jnp.where(is_a, 0, 1)
+                for plane in planes:
+                    lf = jnp.where(own, got[base + group, plane, :, :LANES], 0.0)
+                    rt = jnp.where(own, got[base + group, plane, :, LANES:], 0.0)
                     add_group(total, plane, group, starts, shift, lf, rt)
                 return carry
 
-            lax.fori_loop(jnp.where(is_a, low, 0), jnp.where(is_a, GROUPS, (row + SUB - 1) // SUB), scatter, 0)
-
-            def send(out, offset):
-                def body(group, carry):
-                    rows = pl.ds(pl.multiple_of(group * SUB, SUB), SUB)
-                    for plane in range(4):
-                        out[offset + group, plane] = tile[plane, rows, :]
-                    return carry
-
-                return body
-
-            @pl.when(is_a)
+            lax.fori_loop(jnp.where(is_a, low, 0), jnp.where(is_a, GROUPS, (row + SUB - 1) // SUB), body, 0)
+
+
+def sum_kernel(
+    role_in, table_in, role_out, table_out, in_back, tiles_in, tiles_out, total, got, tile, got_sem, tile_sem
+):
+    pltpu.make_async_copy(in_back, got, got_sem).start()
+    sublane = lax.broadcasted_iota(jnp.int32, (SUB, LANES), 0)
+    kinds = ((role_in, table_in, tiles_in), (role_out, table_out, tiles_out))
+    for k, (role, table, tiles) in enumerate(kinds):
+        mine = jnp.where(role[0] == 0, AT_A, AT_B)
+        for j in range(CAP):
+
+            @pl.when(table[FIELDS * j] == mine)
             def _():
-                lax.fori_loop(0, (row + SUB - 1) // SUB, send(back_a, back), 0)
-
-            @pl.when(jnp.logical_not(is_a))
+                pltpu.make_async_copy(tiles.at[j], tile.at[k * CAP + j], tile_sem.at[k * CAP + j]).start()
+
+    total[...] = jnp.zeros_like(total)
+    pltpu.make_async_copy(in_back, got, got_sem).wait()
+    add_back(role_in, table_in, got, total, range(4))
+    for k, (role, table, tiles) in enumerate(kinds):
+        is_a = role[0] == 0
+        mine = jnp.where(is_a, AT_A, AT_B)
+        for j in range(CAP):
+            state, row, col, _, _ = slot_of(table, j)
+
+            @pl.when(state == mine)
             def _():
-                lax.fori_loop(low, GROUPS, send(back_b, back - low), 0)
-
-        return carry
-
-    lax.fori_loop(0, CAP, slot_body, 0)
-
-
-def finish_kernel(
-    role_in, table_in, role_out, table_out, total_in, in_a, in_b, out_a, out_b, total, got_in, got_out, sem
-):
-    def start_copies(role, from_a, from_b, got, at):
-        @pl.when(role[0] == 0)
-        def _():
-            pltpu.make_async_copy(from_b, got.at[pl.ds(0, CAP_BACK_B)], sem.at[at]).start()
-            pltpu.make_async_copy(from_b, got.at[pl.ds(0, CAP_BACK_B)], sem.at[at]).wait()
-
-        @pl.when(role[0] == 1)
-        def _():
-            pltpu.make_async_copy(from_a, got, sem.at[at]).start()
-            pltpu.make_async_copy(from_a, got, sem.at[at]).wait()
-
-    start_copies(role_in, in_a, in_b, got_in, 0)
-    start_copies(role_out, out_a, out_b, got_out, 1)
-    total[...] = total_in[...]
-    for role, table, got in ((role_in, table_in, got_in), (role_out, table_out, got_out)):
-        is_a = role[0] == 0
-        theirs = jnp.where(is_a, AT_B, AT_A)
-        for j in range(CAP):
-            state, row, col, _, back = slot_of(table, j)
-
-            @pl.when(state == theirs)
-            def _():
+                at = k * CAP + j
+                pltpu.make_async_copy(tiles.at[j], tile.at[at], tile_sem.at[at]).wait()
                 starts, shift = lane_blocks(col)
                 low = row // SUB
-                base = jnp.where(is_a, back - low, back)
-                sublane = lax.broadcasted_iota(jnp.int32, (SUB, LANES), 0)
 
                 def body(group, carry):
                     below = (group * SUB + sublane < row).astype(jnp.int32)
                     own = below == jnp.where(is_a, 0, 1)
+                    rows = pl.ds(pl.multiple_of(group * SUB, SUB), SUB)
                     for plane in range(4):
-                        lf = jnp.where(own, got[base + group, plane, :, :LANES], 0.0)
-                        rt = jnp.where(own, got[base + group, plane, :, LANES:], 0.0)
+                        lf = jnp.where(own, tile[at, plane, rows, :LANES], 0.0)
+                        rt = jnp.where(own, tile[at, plane, rows, LANES:], 0.0)
                         add_group(total, plane, group, starts, shift, lf, rt)
                     return carry
 
@@ -496,6 +516,29 @@
                 )
 
 
+def finish_kernel(role, table, total_in, out_a, out_b, grad, total, got, got_sem, out_sem):
+    is_a = role[0] == 0
+
+    @pl.when(is_a)
+    def _():
+        copy = pltpu.make_async_copy(out_b, got.at[pl.ds(0, CAP_BACK_B)], got_sem)
+        copy.start()
+        copy.wait()
+
+    @pl.when(jnp.logical_not(is_a))
+    def _():
+        copy = pltpu.make_async_copy(out_a, got, got_sem)
+        copy.start()
+        copy.wait()
+
+    for plane in range(4):
+        total[plane] = total_in[plane]
+        add_back(role, table, got, total, (plane,))
+        pltpu.make_async_copy(total.at[plane], grad.at[plane], out_sem.at[plane]).start()
+    for plane in range(4):
+        pltpu.make_async_copy(total.at[plane], grad.at[plane], out_sem.at[plane]).wait()
+
+
 def spec(space):
     return pl.BlockSpec(memory_space=space)
 
@@ -507,29 +550,27 @@
     return jax.ShapeDtypeStruct((groups, 4, SUB, WIN), f32)
 
 
-def run_slots(first_kind, role, table, field, intensity, probe, kernel, tables, from_b, from_a, total):
-    specs = [spec(SM)] * 2 + [spec(VM)] * 6 + [spec(pl.ANY)] * 3
+def run_slots(joint, role, table, field, intensity, probe, kernel, tables, from_b, from_a):
+    backs = (CAP_BACK_A,) if joint else (CAP_BACK_A, CAP_BACK_B)
     return pl.pallas_call(
-        functools.partial(slots_kernel, first_kind),
-        out_shape=(
-            jax.ShapeDtypeStruct(field.shape, f32),
-            packed(CAP_BACK_A),
-            packed(CAP_BACK_B),
-        ),
-        in_specs=specs,
-        out_specs=(spec(VM),) * 3,
+        functools.partial(slots_kernel, joint),
+        out_shape=tuple(packed(n) for n in backs) + (jax.ShapeDtypeStruct((CAP, 4, WIN, WIN), f32),),
+        in_specs=[spec(SM)] * 2 + [spec(VM)] * 6 + [spec(pl.ANY)] * 2,
+        out_specs=(spec(VM),) * len(backs) + (spec(pl.ANY),),
         scratch_shapes=[
             pltpu.VMEM((CAP_FWD, 4, SUB, WIN), f32),
-            pltpu.VMEM((4, WIN, WIN), f32),
-            pltpu.VMEM((2, WIN, LANES), f32),
+            pltpu.VMEM((2, 4, WIN, WIN), f32),
+            pltpu.VMEM((2, 2, WIN, LANES), f32),
             pltpu.VMEM((4, 2 * WIN, LANES), f32),
-            pltpu.VMEM((2, WIN, WIN), f32),
-            pltpu.VMEM((2, WIN, WIN), f32),
-            pltpu.VMEM((2, WIN, WIN), f32),
+            pltpu.VMEM((2, 2, WIN, WIN), f32),
+            pltpu.VMEM((2, 2, WIN, WIN), f32),
+            pltpu.VMEM((2, 2, WIN, WIN), f32),
+            pltpu.SMEM((CAP,), jnp.int32),
             pltpu.SemaphoreType.DMA,
+            pltpu.SemaphoreType.DMA((2,)),
         ],
         compiler_params=PARAMS,
-    )(role, table, field, intensity, probe, kernel, *tables, from_b, from_a, total)
+    )(role, table, field, intensity, probe, kernel, *tables, from_b, from_a)
 
 
 def shards(obj_field, probe_wave, prop_phase, win_offsets, live_counts, intensity):
@@ -577,25 +618,37 @@
     )(jnp.stack([jnp.cos(prop_phase), jnp.sin(prop_phase)]), shuffle)
 
     args = (field, intensity, probe_wave, kernel, (forms, shuffle))
-    total, in_back_a, in_back_b = run_slots(True, role_in, table_in, *args, in_from, in_from, field)
-    in_a = move(in_back_a, within)
-    in_b = move(in_back_b, back(within))
-    total, out_back_a, out_back_b = run_slots(False, role_out, table_out, *args, out_from_b, out_from_a, total)
+    in_back, tiles_in = run_slots(True, role_in, table_in, *args, in_from, in_from)
+    in_back = move(in_back, within + back(within))
+    out_back_a, out_back_b, tiles_out = run_slots(False, role_out, table_out, *args, out_from_b, out_from_a)
     out_a = move(out_back_a, across)
     out_b = move(out_back_b, back(across))
+    total = pl.pallas_call(
+        sum_kernel,
+        out_shape=jax.ShapeDtypeStruct(field.shape, f32),
+        in_specs=[spec(SM)] * 4 + [spec(pl.ANY)] * 3,
+        out_specs=spec(VM),
+        scratch_shapes=[
+            pltpu.VMEM((CAP_BACK_A, 4, SUB, WIN), f32),
+            pltpu.VMEM((2 * CAP, 4, WIN, WIN), f32),
+            pltpu.SemaphoreType.DMA,
+            pltpu.SemaphoreType.DMA((2 * CAP,)),
+        ],
+        compiler_params=PARAMS,
+    )(role_in, table_in, role_out, table_out, in_back, tiles_in, tiles_out)
     grad = pl.pallas_call(
         finish_kernel,
         out_shape=jax.ShapeDtypeStruct(field.shape, f32),
-        in_specs=[spec(SM)] * 4 + [spec(VM)] + [spec(pl.ANY)] * 4,
-        out_specs=spec(VM),
+        in_specs=[spec(SM)] * 2 + [spec(VM)] + [spec(pl.ANY)] * 2,
+        out_specs=spec(pl.ANY),
         scratch_shapes=[
+            pltpu.VMEM(field.shape, f32),
             pltpu.VMEM((CAP_BACK_A, 4, SUB, WIN), f32),
-            pltpu.VMEM((CAP_BACK_A, 4, SUB, WIN), f32),
-            pltpu.SemaphoreType.DMA((2,)),
+            pltpu.SemaphoreType.DMA,
+            pltpu.SemaphoreType.DMA((4,)),
         ],
-        input_output_aliases={4: 0},
         compiler_params=PARAMS,
-    )(role_in, table_in, role_out, table_out, total, in_a, in_b, out_a, out_b)
+    )(role_out, table_out, total, out_a, out_b)
     return grad.reshape(obj_field.shape)
 
 

time: 114 us -> 113 us (level)
  the two profiles are of different devices: /device:TPU:14 before, /device:TPU:20 now
where the time goes in v3:
time: 113 us; the launch traced here: 112 us
  waiting for transfers between devices  45.9 us (41%)
  Pallas kernels  44.4 us (39%)
  starting transfers between devices  15.8 us (14%)
  local copies, waits for them, and re-layouts  5 us (4%)
    ppermute x7, waiting for transfers between devices, shards(): move = lambda x, pairs: lax.ppermute(x, 'row', pairs)  45.9 us
    pallas_call x2, Pallas kernels, run_slots(): pl.pallas_call(functools.partial(slots_kernel, joint), out_shape=tuple((p...  27.9 us
    ppermute x7, starting transfers between devices, shards(): move = lambda x, pairs: lax.ppermute(x, 'row', pairs)  15.8 us
    pallas_call x1, Pallas kernels, shards(): pl.pallas_call(finish_kernel, out_shape=jax.ShapeDtypeStruct(field.shape,...  4.73 us
    pallas_call x1, Pallas kernels, shards(): pl.pallas_call(pack_late_kernel, out_shape=(packed(CAP_FWD), packed(CAP_F...  4.47 us
    unnamed x15, local copies, waits for them, and re-layouts  3.97 us
    pallas_call x1, Pallas kernels, shards(): pl.pallas_call(pack_early_kernel, out_shape=packed(CAP_FWD), in_specs=[sp...  3.45 us
    pallas_call x1, Pallas kernels, shards(): pl.pallas_call(sum_kernel, out_shape=jax.ShapeDtypeStruct(field.shape, f3...  3.38 us
  transfers between devices with their start and end apart: 7, of which 5 were waited for; matrix products, arithmetic and copies ran while one was open for 1% of the time, Pallas kernels for 31%

profile of v3, /device:TPU:20, one launch (start us, length us, event | category | flops | bytes accessed | tf_op | source)
XLA Modules:
  0.0 112.2 jit_solution(6835940865029713761)
XLA Ops:
  0.7 0.8 copy.10
  1.4 0.1 reshape.18
  1.5 0.1 pad_add_fusion.own
  1.6 1.9 %collective-permute-start = (s32[16]{0:T(128)S(1)}, s32[16]{0:T(128)S(1)}, u32[]{:S(2)}, u32[]{:S(2)}) collective-permute-start(s32[16]{0:T(128)S(1)} %pad_add_fusion.own), channel_id=1, source_target_pairs={{0,1},{2,3},{4,5},{6,7},{8,9},{10,11},{12,13},{14,15},{1,2},{3,4},... | collective-permute-start | bytes 200 | tf_op jit(solution)/shard_map/ppermute | solution.py:582
  3.5 2.9 %collective-permute-done.before = s32[16]{0:T(128)S(1)} collective-permute-done((s32[16]{0:T(128)S(1)}, s32[16]{0:T(128)S(1)}, u32[]{:S(2)}, u32[]{:S(2)}) %collective-permute-start) | collective-permute-done | bytes 96 | tf_op jit(solution)/shard_map/ppermute | solution.py:582
  6.4 1.2 %copy-done.1 = f32[4,256,256]{2,1,0:T(8,128)S(1)} copy-done((f32[4,256,256]{2,1,0:T(8,128)S(1)}, f32[4,256,256]{2,1,0:T(8,128)}, u32[]{:S(2)}) %copy-start.1) | copy-done | bytes 1048600
  7.7 4.5 %shard_map.82 = (f32[48,4,8,256]{3,2,1,0:T(8,128)}, f32[48,4,8,256]{3,2,1,0:T(8,128)}, s32[32]{0:T(128)S(1)}, s32[32]{0:T(128)S(1)}) custom-call(s32[1]{0:T(128)} %bitcast.1.odd.role.role_in, s32[16]{0:T(128)S(1)} %pad_add_fusion.own, s32[16]{0:T(128)S(1)} %collective-permute-done.before, f32[4,256,1024]{2,1,0:T(8,128)} %bitcast.8, f32[4,256,256]{2,1,0:T(8,128)S(1)} %copy-done.1), custom_call_target="tpu_custom_call" | custom-call | tf_op jit(solution)/shard_map/pallas_call | solution.py:600
  12.1 0.1 collective-permute-start.1
  12.2 3.4 %shard_map.85 = f32[48,4,8,256]{3,2,1,0:T(8,128)} custom-call(s32[1]{0:T(128)} %bitcast.1.odd.role.role_in, s32[16]{0:T(128)S(1)} %pad_add_fusion.own, f32[4,256,1024]{2,1,0:T(8,128)} %bitcast.9, f32[4,256,256]{2,1,0:T(8,128)S(1)} %copy-done.2), custom_call_target="tpu_custom_call" | custom-call | tf_op jit(solution)/shard_map/pallas_call | solution.py:590
  15.7 1.4 %collective-permute-start.4 = (f32[48,4,8,256]{3,2,1,0:T(8,128)}, f32[48,4,8,256]{3,2,1,0:T(8,128)}, u32[]{:S(2)}, u32[]{:S(2)}) collective-permute-start(f32[48,4,8,256]{3,2,1,0:T(8,128)} %shard_map.85), channel_id=1, source_target_pairs={{1,2},{3,4},{5,6},{7,8},{9,10},{11,12},{13,14},{17,18},{19,20},{21... | collective-permute-start | bytes 4718600 | tf_op jit(solution)/shard_map/ppermute | solution.py:582
  17.1 6.6 %collective-permute-start.3 = (f32[48,4,8,256]{3,2,1,0:T(8,128)}, f32[48,4,8,256]{3,2,1,0:T(8,128)}, u32[]{:S(2)}, u32[]{:S(2)}) collective-permute-start(f32[48,4,8,256]{3,2,1,0:T(8,128)} %get-tuple-element.19), channel_id=1, source_target_pairs={{2,1},{4,3},{6,5},{8,7},{10,9},{12,11},{14,13},{18,17},{20,19},{22... | collective-permute-start | bytes 4718600 | tf_op jit(solution)/shard_map/ppermute | solution.py:582
  23.7 0.9 cosine_bitcast_fusion
  24.8 0.4 shard_map.83.kernel
  25.2 13.9 %shard_map.84 = (f32[48,4,8,256]{3,2,1,0:T(8,128)S(1)}, f32[4,4,256,256]{3,2,1,0:T(8,128)}) custom-call(s32[1]{0:T(128)} %bitcast.1.odd.role.role_in, s32[32]{0:T(128)S(1)} %get-tuple-element.15.table.table_in, f32[4,256,1024]{2,1,0:T(8,128)} %bitcast.10, f32[4,256,256]{2,1,0:T(8,128)S(1)} %copy-done.2, f32[2,256,256]{2,1,0:T(8,128)S(1)} %copy-done.4, ...), custom_call_target="tpu_custom_call" | custom-call | tf_op jit(solution)/shard_map/pallas_call | solution.py:555
  39.2 15.5 %collective-permute-done.4.from_a = f32[48,4,8,256]{3,2,1,0:T(8,128)} collective-permute-done((f32[48,4,8,256]{3,2,1,0:T(8,128)}, f32[48,4,8,256]{3,2,1,0:T(8,128)}, u32[]{:S(2)}, u32[]{:S(2)}) %collective-permute-start.4) | collective-permute-done | bytes 1572896 | tf_op jit(solution)/shard_map/ppermute | solution.py:582
  54.7 16.9 %collective-permute-done.3.from_b = f32[48,4,8,256]{3,2,1,0:T(8,128)} collective-permute-done((f32[48,4,8,256]{3,2,1,0:T(8,128)}, f32[48,4,8,256]{3,2,1,0:T(8,128)}, u32[]{:S(2)}, u32[]{:S(2)}) %collective-permute-start.3) | collective-permute-done | bytes 1572896 | tf_op jit(solution)/shard_map/ppermute | solution.py:582
  71.6 14.0 %shard_map.86 = (f32[48,4,8,256]{3,2,1,0:T(8,128)S(1)}, f32[32,4,8,256]{3,2,1,0:T(8,128)S(1)}, f32[4,4,256,256]{3,2,1,0:T(8,128)}) custom-call(s32[1]{0:T(128)} %bitcast.role.role_out, s32[32]{0:T(128)S(1)} %get-tuple-element.14.table.table_out, f32[4,256,1024]{2,1,0:T(8,128)} %bitcast.11, f32[4,256,256]{2,1,0:T(8,128)S(1)} %copy-done.2, ...), custom_call_target="tpu_custom_call" | custom-call | tf_op jit(solution)/shard_map/pallas_call | solution.py:555
  85.6 1.3 %collective-permute-start.5 = (f32[48,4,8,256]{3,2,1,0:T(8,128)S(1)}, f32[48,4,8,256]{3,2,1,0:T(8,128)S(1)}, u32[]{:S(2)}, u32[]{:S(2)}) collective-permute-start(f32[48,4,8,256]{3,2,1,0:T(8,128)S(1)} %get-tuple-element.21), channel_id=1, source_target_pairs={{1,2},{3,4},{5,6},{7,8},{9,10},{11,12},{13,14},{17,18},{19,20},{21... | collective-permute-start | bytes 4718600 | tf_op jit(solution)/shard_map/ppermute | solution.py:582
  86.9 4.4 %collective-permute-start.6 = (f32[32,4,8,256]{3,2,1,0:T(8,128)S(1)}, f32[32,4,8,256]{3,2,1,0:T(8,128)S(1)}, u32[]{:S(2)}, u32[]{:S(2)}) collective-permute-start(f32[32,4,8,256]{3,2,1,0:T(8,128)S(1)} %get-tuple-element.22), channel_id=1, source_target_pairs={{2,1},{4,3},{6,5},{8,7},{10,9},{12,11},{14,13},{18,17},{20,19},{22... | collective-permute-start | bytes 3145736 | tf_op jit(solution)/shard_map/ppermute | solution.py:582
  91.3 3.4 %shard_map.87.total_in = f32[4,256,1024]{2,1,0:T(8,128)S(1)} custom-call(s32[1]{0:T(128)} %bitcast.1.odd.role.role_in, s32[32]{0:T(128)S(1)} %get-tuple-element.15.table.table_in, s32[1]{0:T(128)} %bitcast.role.role_out, s32[32]{0:T(128)S(1)} %get-tuple-element.14.table.table_out, f32[48,4,8,256]{3,2,1,0:T(8,128)S(1)} %collective-permute-done.2.in_back, ...), custom_call_target="tpu_custom_call" | custom-call | tf_op jit(solution)/shard_map/pallas_call | solution.py:626
  94.7 2.0 %copy-done = f32[4,256,1024]{2,1,0:T(8,128)} copy-done((f32[4,256,1024]{2,1,0:T(8,128)}, f32[4,256,1024]{2,1,0:T(8,128)S(1)}, u32[]{:S(2)}) %copy-start) | copy-done | bytes 4194328
  96.7 6.9 %collective-permute-done.6.out_b = f32[32,4,8,256]{3,2,1,0:T(8,128)S(1)} collective-permute-done((f32[32,4,8,256]{3,2,1,0:T(8,128)S(1)}, f32[32,4,8,256]{3,2,1,0:T(8,128)S(1)}, u32[]{:S(2)}, u32[]{:S(2)}) %collective-permute-start.6) | collective-permute-done | bytes 1048608 | tf_op jit(solution)/shard_map/ppermute | solution.py:582
  103.5 3.8 %collective-permute-done.5.out_a = f32[48,4,8,256]{3,2,1,0:T(8,128)S(1)} collective-permute-done((f32[48,4,8,256]{3,2,1,0:T(8,128)S(1)}, f32[48,4,8,256]{3,2,1,0:T(8,128)S(1)}, u32[]{:S(2)}, u32[]{:S(2)}) %collective-permute-start.5) | collective-permute-done | bytes 1572896 | tf_op jit(solution)/shard_map/ppermute | solution.py:582
  107.3 4.7 %shard_map.88 = f32[4,256,1024]{2,1,0:T(8,128)} custom-call(s32[1]{0:T(128)} %bitcast.role.role_out, s32[32]{0:T(128)S(1)} %get-tuple-element.14.table.table_out, f32[4,256,1024]{2,1,0:T(8,128)} %copy-done, f32[48,4,8,256]{3,2,1,0:T(8,128)S(1)} %collective-permute-done.5.out_a, f32[32,4,8,256]{3,2,1,0:T(8,128)S(1)} %collective-permute-done.6.out_b), custom_call_target="tpu_custom_call" | custom-call | tf_op jit(solution)/shard_map/pallas_call | solution.py:639
  (17 shorter events, 0.1 us)
Async XLA Ops:
  1.6 4.9 %collective-permute-start = (s32[16]{0:T(128)S(1)}, s32[16]{0:T(128)S(1)}, u32[]{:S(2)}, u32[]{:S(2)}) collective-permute-start(s32[16]{0:T(128)S(1)} %pad_add_fusion.own), channel_id=1, source_target_pairs={{0,1},{2,3},{4,5},{6,7},{8,9},{10,11},{12,13},{14,15},{1,2},{3,4},... | collective-permute-start | bytes 200 | tf_op jit(solution)/shard_map/ppermute | solution.py:582
  6.4 1.2 %copy-start.1 = (f32[4,256,256]{2,1,0:T(8,128)S(1)}, f32[4,256,256]{2,1,0:T(8,128)}, u32[]{:S(2)}) copy-start(f32[4,256,256]{2,1,0:T(8,128)} %intensity.7) | copy-start | bytes 3145732
  7.7 4.6 %copy-start.2 = (f32[4,256,256]{2,1,0:T(8,128)S(1)}, f32[4,256,256]{2,1,0:T(8,128)}, u32[]{:S(2)}) copy-start(f32[4,256,256]{2,1,0:T(8,128)} %intensity.7) | copy-start | bytes 3145732
  12.1 11.6 %copy-start.6 = (f32[256,256]{1,0:T(8,128)S(1)}, f32[256,256]{1,0:T(8,128)}, u32[]{:S(2)}) copy-start(f32[256,256]{1,0:T(8,128)} %param.10) | copy-start | bytes 786436
  12.1 13.0 %collective-permute-start.1 = (f32[48,4,8,256]{3,2,1,0:T(8,128)}, f32[48,4,8,256]{3,2,1,0:T(8,128)}, u32[]{:S(2)}, u32[]{:S(2)}) collective-permute-start(f32[48,4,8,256]{3,2,1,0:T(8,128)} %get-tuple-element.16), channel_id=1, source_target_pairs={{0,1},{2,3},{4,5},{6,7},{8,9},{10,11},{12,13},{14,15},{1,0},{3,2},... | collective-permute-start | bytes 4718600 | tf_op jit(solution)/shard_map/ppermute | solution.py:582
  15.7 9.1 %copy-start.5 = (bf16[256,256]{1,0:T(8,128)(2,1)S(1)}, bf16[256,256]{1,0:T(8,128)(2,1)}, u32[]{:S(2)}) copy-start(bf16[256,256]{1,0:T(8,128)(2,1)} %constant.13.clone.shuffle) | copy-start | bytes 393220
  15.7 9.5 %copy-start.3 = (bf16[4,2,256,256]{3,2,1,0:T(8,128)(2,1)S(1)}, bf16[4,2,256,256]{3,2,1,0:T(8,128)(2,1)}, u32[]{:S(2)}) copy-start(bf16[4,2,256,256]{3,2,1,0:T(8,128)(2,1)} %constant.12.clone.forms) | copy-start | bytes 3145732
  15.7 9.5 %copy-start.4 = (f32[2,256,256]{2,1,0:T(8,128)S(1)}, f32[2,256,256]{2,1,0:T(8,128)}, u32[]{:S(2)}) copy-start(f32[2,256,256]{2,1,0:T(8,128)} %probe.3) | copy-start | bytes 1572868
  15.7 39.0 %collective-permute-start.4 = (f32[48,4,8,256]{3,2,1,0:T(8,128)}, f32[48,4,8,256]{3,2,1,0:T(8,128)}, u32[]{:S(2)}, u32[]{:S(2)}) collective-permute-start(f32[48,4,8,256]{3,2,1,0:T(8,128)} %shard_map.85), channel_id=1, source_target_pairs={{1,2},{3,4},{5,6},{7,8},{9,10},{11,12},{13,14},{17,18},{19,20},{21... | collective-permute-start | bytes 4718600 | tf_op jit(solution)/shard_map/ppermute | solution.py:582
  17.1 54.5 %collective-permute-start.3 = (f32[48,4,8,256]{3,2,1,0:T(8,128)}, f32[48,4,8,256]{3,2,1,0:T(8,128)}, u32[]{:S(2)}, u32[]{:S(2)}) collective-permute-start(f32[48,4,8,256]{3,2,1,0:T(8,128)} %get-tuple-element.19), channel_id=1, source_target_pairs={{2,1},{4,3},{6,5},{8,7},{10,9},{12,11},{14,13},{18,17},{20,19},{22... | collective-permute-start | bytes 4718600 | tf_op jit(solution)/shard_map/ppermute | solution.py:582
  39.1 52.2 %collective-permute-start.2 = (f32[48,4,8,256]{3,2,1,0:T(8,128)S(1)}, f32[48,4,8,256]{3,2,1,0:T(8,128)S(1)}, u32[]{:S(2)}, u32[]{:S(2)}) collective-permute-start(f32[48,4,8,256]{3,2,1,0:T(8,128)S(1)} %get-tuple-element.17), channel_id=1, source_target_pairs={{0,1},{2,3},{4,5},{6,7},{8,9},{10,11},{12,13},{14,15},{1,0},{3,2},... | collective-permute-start | bytes 4718600 | tf_op jit(solution)/shard_map/ppermute | solution.py:582
  85.6 21.7 %collective-permute-start.5 = (f32[48,4,8,256]{3,2,1,0:T(8,128)S(1)}, f32[48,4,8,256]{3,2,1,0:T(8,128)S(1)}, u32[]{:S(2)}, u32[]{:S(2)}) collective-permute-start(f32[48,4,8,256]{3,2,1,0:T(8,128)S(1)} %get-tuple-element.21), channel_id=1, source_target_pairs={{1,2},{3,4},{5,6},{7,8},{9,10},{11,12},{13,14},{17,18},{19,20},{21... | collective-permute-start | bytes 4718600 | tf_op jit(solution)/shard_map/ppermute | solution.py:582
  86.9 16.7 %collective-permute-start.6 = (f32[32,4,8,256]{3,2,1,0:T(8,128)S(1)}, f32[32,4,8,256]{3,2,1,0:T(8,128)S(1)}, u32[]{:S(2)}, u32[]{:S(2)}) collective-permute-start(f32[32,4,8,256]{3,2,1,0:T(8,128)S(1)} %get-tuple-element.22), channel_id=1, source_target_pairs={{2,1},{4,3},{6,5},{8,7},{10,9},{12,11},{14,13},{18,17},{20,19},{22... | collective-permute-start | bytes 3145736 | tf_op jit(solution)/shard_map/ppermute | solution.py:582
  94.7 2.0 %copy-start = (f32[4,256,1024]{2,1,0:T(8,128)}, f32[4,256,1024]{2,1,0:T(8,128)S(1)}, u32[]{:S(2)}) copy-start(f32[4,256,1024]{2,1,0:T(8,128)S(1)} %shard_map.87.total_in) | copy-start | bytes 12582916

commit v4 on v3

--- a/solution.py
+++ b/solution.py
@@ -171,6 +171,16 @@
     return [pl.multiple_of(start, LANES) for start in starts], jnp.bitwise_and(col, LANES - 1)
 
 
+WIDE = 3 * LANES
+
+
+def near_columns(col):
+    first = jnp.minimum(col // LANES, 5)
+    skip = col // LANES - first
+    starts = [pl.multiple_of(jnp.minimum(skip + k, 2) * LANES, LANES) for k in range(3)]
+    return pl.ds(pl.multiple_of(first * LANES, LANES), WIDE), starts, jnp.bitwise_and(col, LANES - 1)
+
+
 def lane_iota():
     return lax.broadcasted_iota(jnp.int32, (SUB, LANES), 1)
 
@@ -191,73 +201,89 @@
     total[plane, rows, pl.ds(starts[2], LANES)] += jnp.where(inside, 0.0, left)
 
 
-def pack_to_b(table, field, intensity, out):
+def fetch_columns(table, wanted, field, held, sem, base):
+    for j in range(CAP):
+
+        @pl.when(table[FIELDS * j] == wanted)
+        def _():
+            columns, _, _ = near_columns(table[FIELDS * j + 2])
+            pltpu.make_async_copy(field.at[:, :, columns], held.at[base + j], sem.at[base + j]).start()
+
+
+def copy_groups(held, out, at, offset, low, high, starts, shift):
+    def body(group, carry):
+        for plane in range(4):
+            left, right = load_group(held.at[at], plane, group, starts, shift)
+            out[offset + group, plane, :, :LANES] = left
+            out[offset + group, plane, :, LANES:] = right
+        return carry
+
+    lax.fori_loop(low, high, body, 0)
+
+
+def pack_to_b(table, field, intensity, out, held, sem, int_sem, base):
+    def intensity_copy(j):
+        _, row, _, start, _ = slot_of(table, j)
+        after = start + GROUPS - row // SUB
+        return pltpu.make_async_copy(intensity.at[j], out.at[pl.ds(after, INT_GROUPS)], int_sem.at[j])
+
+    for j in range(CAP):
+
+        @pl.when(table[FIELDS * j] == AT_B)
+        def _():
+            intensity_copy(j).start()
+
     for j in range(CAP):
         state, row, col, start, _ = slot_of(table, j)
 
         @pl.when(state == AT_B)
         def _():
-            starts, shift = lane_blocks(col)
-            first = row // SUB
-
-            def body(group, carry):
-                at = start + group - first
-                for plane in range(4):
-                    left, right = load_group(field, plane, group, starts, shift)
-                    out[at, plane, :, :LANES] = left
-                    out[at, plane, :, LANES:] = right
-                return carry
-
-            lax.fori_loop(first, GROUPS, body, 0)
-            after = start + GROUPS - first
-
-            def body_int(group, carry):
-                for plane in range(4):
-                    rows = pl.ds(pl.multiple_of((group * 4 + plane) * SUB, SUB), SUB)
-                    out[after + group, plane] = intensity[j, rows, :]
-                return carry
-
-            lax.fori_loop(0, INT_GROUPS, body_int, 0)
-
-
-def pack_to_a(table, field, out):
+            columns, starts, shift = near_columns(col)
+            at = base + j
+            pltpu.make_async_copy(field.at[:, :, columns], held.at[at], sem.at[at]).wait()
+            copy_groups(held, out, at, start - row // SUB, row // SUB, GROUPS, starts, shift)
+            intensity_copy(j).wait()
+
+
+def pack_to_a(table, field, out, held, sem, base):
     for j in range(CAP):
         state, row, col, start, _ = slot_of(table, j)
 
         @pl.when(state == AT_A)
         def _():
-            starts, shift = lane_blocks(col)
-
-            def body(group, carry):
-                for plane in range(4):
-                    left, right = load_group(field, plane, group, starts, shift)
-                    out[start + group, plane, :, :LANES] = left
-                    out[start + group, plane, :, LANES:] = right
-                return carry
-
-            lax.fori_loop(0, (row + SUB - 1) // SUB, body, 0)
-
-
-def pack_early_kernel(odd, own, field, intensity, out, table):
+            columns, starts, shift = near_columns(col)
+            at = base + j
+            pltpu.make_async_copy(field.at[:, :, columns], held.at[at], sem.at[at]).wait()
+            copy_groups(held, out, at, start, 0, (row + SUB - 1) // SUB, starts, shift)
+
+
+def pack_early_kernel(odd, own, field, intensity, out, info, table, held, sem, int_sem):
+    for j in range(INFO):
+        info[j] = own[j]
+
     @pl.when(odd[0] == 1)
     def _():
         decide(own, table)
-        pack_to_b(table, field, intensity, out)
-
-
-def pack_late_kernel(odd, own, before, field, intensity, out, inner, table_in, table_out):
+        fetch_columns(table, AT_B, field, held, sem, 0)
+        pack_to_b(table, field, intensity, out, held, sem, int_sem, 0)
+
+
+def pack_late_kernel(odd, own, before, field, intensity, out, inner, table_in, table_out, held, sem, int_sem):
     @pl.when(odd[0] == 0)
     def _():
+        decide(before, table_out)
+        fetch_columns(table_out, AT_A, field, held, sem, 0)
         decide(own, table_in)
-        decide(before, table_out)
-        pack_to_a(table_out, field, out)
-        pack_to_b(table_in, field, intensity, inner)
+        fetch_columns(table_in, AT_B, field, held, sem, CAP)
+        pack_to_a(table_out, field, out, held, sem, 0)
+        pack_to_b(table_in, field, intensity, inner, held, sem, int_sem, CAP)
 
     @pl.when(odd[0] == 1)
     def _():
         decide(before, table_in)
+        fetch_columns(table_in, AT_A, field, held, sem, 0)
         decide(own, table_out)
-        pack_to_a(table_in, field, inner)
+        pack_to_a(table_in, field, inner, held, sem, 0)
 
 
 def prepare_kernel(phases, shuffle, out, halves):
@@ -278,7 +304,8 @@
 
 def slots_kernel(joint, role, table, field, intensity, probe, kernel, forms, shuffle, from_b, from_a, *rest):
     back_a, back_b = rest[0], rest[0 if joint else 1]
-    tiles, got, tile, measured, twice, beam, work, entered, chosen, got_sem, tile_sem = rest[1 if joint else 2 :]
+    tiles, held, got, tile, measured, twice, beam, work, entered, chosen = rest[1 if joint else 2 : -4]
+    held_sem, int_sem, got_sem, tile_sem = rest[-4:]
     is_a = role[0] == 0
     mine = jnp.where(is_a, AT_A, AT_B)
 
@@ -289,6 +316,23 @@
     @pl.when(jnp.logical_not(is_a))
     def _():
         pltpu.make_async_copy(from_a, got, got_sem).start()
+
+    fetch_columns(table, mine, field, held, held_sem, 0)
+
+    def intensity_copies(j):
+        return [
+            pltpu.make_async_copy(
+                intensity.at[j, :, pl.ds(part * LANES, LANES)], measured.at[j, part], int_sem.at[j, part]
+            )
+            for part in range(2)
+        ]
+
+    for j in range(CAP):
+
+        @pl.when(jnp.logical_and(is_a, table[FIELDS * j] == AT_A))
+        def _():
+            for copy in intensity_copies(j):
+                copy.start()
 
     for plane in range(2):
         for part in range(2):
@@ -311,27 +355,36 @@
 
     def load(m, j):
         _, row, col, start, _ = slot_of(table, j)
-        starts, shift = lane_blocks(col)
+        columns, starts, shift = near_columns(col)
         low = row // SUB
+        high = (row + SUB - 1) // SUB
         base = jnp.where(is_a, start, start - low)
 
-        def gather(group, carry):
-            below = (group * SUB + sublane < row).astype(jnp.int32)
-            own = below == jnp.where(is_a, 0, 1)
-            at = jnp.clip(base + group, 0, CAP_FWD - 1)
+        def own_groups(group, carry):
             rows = pl.ds(pl.multiple_of(group * SUB, SUB), SUB)
             for plane in range(4):
-                lf, rt = load_group(field, plane, group, starts, shift)
-                tile[m, plane, rows, :LANES] = jnp.where(own, lf, got[at, plane, :, :LANES])
-                tile[m, plane, rows, LANES:] = jnp.where(own, rt, got[at, plane, :, LANES:])
+                lf, rt = load_group(held.at[j], plane, group, starts, shift)
+                tile[m, plane, rows, :LANES] = lf
+                tile[m, plane, rows, LANES:] = rt
             return carry
 
-        lax.fori_loop(0, GROUPS, gather, 0)
-
-        @pl.when(is_a)
-        def _():
-            measured[m, 0] = intensity[j, :, :LANES]
-            measured[m, 1] = intensity[j, :, LANES:]
+        def their_groups(group, carry):
+            rows = pl.ds(pl.multiple_of(group * SUB, SUB), SUB)
+            for plane in range(4):
+                tile[m, plane, rows, :] = got[base + group, plane]
+            return carry
+
+        lax.fori_loop(jnp.where(is_a, 0, low), jnp.where(is_a, high, GROUPS), their_groups, 0)
+        lax.fori_loop(jnp.where(is_a, high, 0), jnp.where(is_a, GROUPS, low), own_groups, 0)
+
+        @pl.when(low < high)
+        def _():
+            own = (low * SUB + sublane < row).astype(jnp.int32) == jnp.where(is_a, 0, 1)
+            rows = pl.ds(pl.multiple_of(low * SUB, SUB), SUB)
+            for plane in range(4):
+                lf, rt = load_group(held.at[j], plane, low, starts, shift)
+                tile[m, plane, rows, :LANES] = jnp.where(own, lf, tile[m, plane, rows, :LANES])
+                tile[m, plane, rows, LANES:] = jnp.where(own, rt, tile[m, plane, rows, LANES:])
 
         @pl.when(jnp.logical_not(is_a))
         def _():
@@ -340,8 +393,8 @@
             def unpack(group, carry):
                 for plane in range(4):
                     rows = pl.ds(pl.multiple_of((group * 4 + plane) * SUB, SUB), SUB)
-                    measured[m, 0, rows, :] = got[after + group, plane, :, :LANES]
-                    measured[m, 1, rows, :] = got[after + group, plane, :, LANES:]
+                    measured[j, 0, rows, :] = got[after + group, plane, :, :LANES]
+                    measured[j, 1, rows, :] = got[after + group, plane, :, LANES:]
                 return carry
 
             lax.fori_loop(0, INT_GROUPS, unpack, 0)
@@ -350,16 +403,25 @@
             parts = [twice[2 * plane + part, pl.ds(WIN - row, WIN), :] for part in range(2)]
             beam[m, plane] = pltpu.roll(jnp.concatenate(parts, axis=1), shift, 1)
 
+    def arrive(j):
+        columns, _, _ = near_columns(table[FIELDS * j + 2])
+        pltpu.make_async_copy(field.at[:, :, columns], held.at[j], held_sem.at[j]).wait()
+
+        @pl.when(is_a)
+        def _():
+            for copy in intensity_copies(j):
+                copy.wait()
+
     def store_rows(m, e, o):
         work[m, 0, :HALF], work[m, 1, :HALF] = e[:HALF], e[HALF:]
         work[m, 0, HALF:], work[m, 1, HALF:] = o[:HALF], o[HALF:]
 
-    def middle(pointwise):
+    def middle(pointwise, slots=None):
         for half in range(2):
             rows = pl.ds(half * HALF, HALF)
             for m in range(2):
                 re, im = lanes_forward(work[m, 0, rows, :], work[m, 1, rows, :], forms)
-                re, im = pointwise(m, half, rows, re, im)
+                re, im = pointwise(m, half, rows, re, im, slots)
                 re, im = lanes_inverse(re, im, forms)
                 work[m, 0, rows, :], work[m, 1, rows, :] = re, im
 
@@ -370,20 +432,24 @@
             jnp.concatenate([u[HALF:] + v[HALF:], u[HALF:] - v[HALF:]], axis=0),
         )
 
-    def propagate(m, half, rows, re, im):
+    def propagate(m, half, rows, re, im, slots):
         return cmul(kernel[0, rows, :], kernel[1, rows, :], re, im)
 
-    def propagate_back(m, half, rows, re, im):
+    def propagate_back(m, half, rows, re, im, slots):
         return cmul_conj(kernel[0, rows, :], kernel[1, rows, :], re, im)
 
-    def residual(m, half, rows, re, im):
+    def residual(m, half, rows, re, im, slots):
         every = pl.ds(half, HALF, stride=2)
-        rows_of = jnp.concatenate([measured[m, 0, every, :], measured[m, 1, every, :]], axis=1)
+        at = slots[m]
+        rows_of = jnp.concatenate([measured[at, 0, every, :], measured[at, 1, every, :]], axis=1)
         high, low = split(rows_of)
         wanted = jnp.dot(high, shuffle[...], preferred_element_type=f32)
         wanted += jnp.dot(low, shuffle[...], preferred_element_type=f32)
         scale = re * re + im * im - wanted
         return scale * re, scale * im
+
+    def tile_copy(m, j):
+        return pltpu.make_async_copy(tile.at[m], tiles.at[j], tile_sem.at[m])
 
     def write(m, j):
         _, row, _, _, back = slot_of(table, j)
@@ -398,7 +464,7 @@
 
             return body
 
-        pltpu.make_async_copy(tile.at[m], tiles.at[j], tile_sem.at[m]).start()
+        tile_copy(m, j).start()
 
         @pl.when(is_a)
         def _():
@@ -407,13 +473,23 @@
         @pl.when(jnp.logical_not(is_a))
         def _():
             lax.fori_loop(low, GROUPS, send(back_b, back - low), 0)
-
-        pltpu.make_async_copy(tile.at[m], tiles.at[j], tile_sem.at[m]).wait()
 
     def pair(p, carry):
         two = 2 * p + 1 < found
         first = chosen[2 * p]
         second = jnp.where(two, chosen[jnp.minimum(2 * p + 1, CAP - 1)], first)
+
+        @pl.when(p > 0)
+        def _():
+            tile_copy(0, chosen[2 * p - 2]).wait()
+            tile_copy(1, chosen[2 * p - 1]).wait()
+
+        arrive(first)
+
+        @pl.when(two)
+        def _():
+            arrive(second)
+
         load(0, first)
         load(1, second)
         for m in range(2):
@@ -425,7 +501,7 @@
             entered[m, 0], entered[m, 1] = re, im
             re, im = cmul(re, im, tile[m, 2], tile[m, 3])
             store_rows(m, *rows_forward(re, im, forms))
-        middle(residual)
+        middle(residual, (first, second))
         for m in range(2):
             br, bi = rows_back(m)
             re, im = cmul_conj(tile[m, 2], tile[m, 3], br, bi)
@@ -445,6 +521,14 @@
 
     lax.fori_loop(0, (found + 1) // 2, pair, 0)
 
+    @pl.when(found > 0)
+    def _():
+        tile_copy(0, 0).wait()
+
+    @pl.when(jnp.logical_and(found > 0, jnp.bitwise_and(found, 1) == 0))
+    def _():
+        tile_copy(1, 0).wait()
+
 
 def add_back(role, table, got, total, planes):
     is_a = role[0] == 0
@@ -543,7 +627,8 @@
     return pl.BlockSpec(memory_space=space)
 
 
-PARAMS = pltpu.CompilerParams(vmem_limit_bytes=48 << 20)
+def vmem(mib):
+    return pltpu.CompilerParams(vmem_limit_bytes=mib << 20)
 
 
 def packed(groups):
@@ -555,21 +640,24 @@
     return pl.pallas_call(
         functools.partial(slots_kernel, joint),
         out_shape=tuple(packed(n) for n in backs) + (jax.ShapeDtypeStruct((CAP, 4, WIN, WIN), f32),),
-        in_specs=[spec(SM)] * 2 + [spec(VM)] * 6 + [spec(pl.ANY)] * 2,
+        in_specs=[spec(SM)] * 2 + [spec(pl.ANY)] * 2 + [spec(VM)] * 4 + [spec(pl.ANY)] * 2,
         out_specs=(spec(VM),) * len(backs) + (spec(pl.ANY),),
         scratch_shapes=[
+            pltpu.VMEM((CAP, 4, WIN, WIDE), f32),
             pltpu.VMEM((CAP_FWD, 4, SUB, WIN), f32),
             pltpu.VMEM((2, 4, WIN, WIN), f32),
-            pltpu.VMEM((2, 2, WIN, LANES), f32),
+            pltpu.VMEM((CAP, 2, WIN, LANES), f32),
             pltpu.VMEM((4, 2 * WIN, LANES), f32),
             pltpu.VMEM((2, 2, WIN, WIN), f32),
             pltpu.VMEM((2, 2, WIN, WIN), f32),
             pltpu.VMEM((2, 2, WIN, WIN), f32),
             pltpu.SMEM((CAP,), jnp.int32),
+            pltpu.SemaphoreType.DMA((CAP,)),
+            pltpu.SemaphoreType.DMA((CAP, 2)),
             pltpu.SemaphoreType.DMA,
             pltpu.SemaphoreType.DMA((2,)),
         ],
-        compiler_params=PARAMS,
+        compiler_params=vmem(32),
     )(role, table, field, intensity, probe, kernel, *tables, from_b, from_a)
 
 
@@ -586,24 +674,35 @@
 
     flag = odd.reshape(1)
     own = jnp.concatenate([win_offsets.reshape(-1), live_counts, jnp.zeros((INFO - 2 * CAP - 1,), jnp.int32)])
-    before = move(own, within + across)
-    to_b = pl.pallas_call(
+    maps = intensity.reshape(CAP, INT_GROUPS, 4, SUB, WIN)
+    to_b, info = pl.pallas_call(
         pack_early_kernel,
-        out_shape=packed(CAP_FWD),
-        in_specs=[spec(SM)] * 2 + [spec(VM)] * 2,
-        out_specs=spec(VM),
-        scratch_shapes=[pltpu.SMEM((CAP * FIELDS,), jnp.int32)],
-        compiler_params=PARAMS,
-    )(flag, own, field, intensity)
+        out_shape=(packed(CAP_FWD), jax.ShapeDtypeStruct((INFO,), jnp.int32)),
+        in_specs=[spec(SM)] * 2 + [spec(pl.ANY)] * 2,
+        out_specs=(spec(VM), spec(SM)),
+        scratch_shapes=[
+            pltpu.SMEM((CAP * FIELDS,), jnp.int32),
+            pltpu.VMEM((CAP, 4, WIN, WIDE), f32),
+            pltpu.SemaphoreType.DMA((CAP,)),
+            pltpu.SemaphoreType.DMA((CAP,)),
+        ],
+        compiler_params=vmem(16),
+    )(flag, own, field, maps)
     out_from_a = move(to_b, across)
+    before = move(info, within + across)
     table = jax.ShapeDtypeStruct((CAP * FIELDS,), jnp.int32)
     to_a, inner, table_in, table_out = pl.pallas_call(
         pack_late_kernel,
         out_shape=(packed(CAP_FWD), packed(CAP_FWD), table, table),
-        in_specs=[spec(SM)] * 3 + [spec(VM)] * 2,
+        in_specs=[spec(SM)] * 3 + [spec(pl.ANY)] * 2,
         out_specs=(spec(VM), spec(VM), spec(SM), spec(SM)),
-        compiler_params=PARAMS,
-    )(flag, own, before, field, intensity)
+        scratch_shapes=[
+            pltpu.VMEM((2 * CAP, 4, WIN, WIDE), f32),
+            pltpu.SemaphoreType.DMA((2 * CAP,)),
+            pltpu.SemaphoreType.DMA((CAP,)),
+        ],
+        compiler_params=vmem(24),
+    )(flag, own, before, field, maps)
     out_from_b = move(to_a, back(across))
     in_from = move(inner, within + back(within))
 
@@ -614,7 +713,7 @@
         in_specs=[spec(VM)] * 2,
         out_specs=spec(VM),
         scratch_shapes=[pltpu.VMEM((2, WIN, LANES), f32)],
-        compiler_params=PARAMS,
+        compiler_params=vmem(8),
     )(jnp.stack([jnp.cos(prop_phase), jnp.sin(prop_phase)]), shuffle)
 
     args = (field, intensity, probe_wave, kernel, (forms, shuffle))
@@ -634,7 +733,7 @@
             pltpu.SemaphoreType.DMA,
             pltpu.SemaphoreType.DMA((2 * CAP,)),
         ],
-        compiler_params=PARAMS,
+        compiler_params=vmem(20),
     )(role_in, table_in, role_out, table_out, in_back, tiles_in, tiles_out)
     grad = pl.pallas_call(
         finish_kernel,
@@ -647,7 +746,7 @@
             pltpu.SemaphoreType.DMA,
             pltpu.SemaphoreType.DMA((4,)),
         ],
-        compiler_params=PARAMS,
+        compiler_params=vmem(16),
     )(role_out, table_out, total, out_a, out_b)
     return grad.reshape(obj_field.shape)
 

time: 113 us -> 109 us (0.965)
  Pallas kernels: 44.4 us -> 36.5 us
  local copies, waits for them, and re-layouts: 5 us -> 7.43 us
  waiting for transfers between devices: 45.9 us -> 47.2 us
    pallas_call x2, Pallas kernels: 27.9 us -> 22.5 us  [run_slots(): pl.pallas_call(functools.partial(slots_kernel, joint), out_shape=tuple((p...]
    unnamed x15 -> x21, local copies, waits for them, and re-layouts: 3.97 us -> 6.4 us
    pallas_call x1, Pallas kernels: 3.45 us -> 1.78 us  [shards(): pl.pallas_call(pack_early_kernel, out_shape=(packed(CAP_FWD), jax.ShapeDt...]
    ppermute x7, waiting for transfers between devices: 45.9 us -> 47.2 us  [shards(): move = lambda x, pairs: lax.ppermute(x, 'row', pairs)]
  transfers between devices with their start and end apart: 7 -> 7, of which waited for: 5 -> 5; matrix products, arithmetic and copies ran while one was open for 1% -> 1% of each run, Pallas kernels for 31% -> 25%
where the time goes in v4:
time: 109 us; the launch traced here: 108 us
  waiting for transfers between devices  47.2 us (43%)
  Pallas kernels  36.5 us (33%)
  starting transfers between devices  16 us (15%)
  local copies, waits for them, and re-layouts  7.43 us (7%)
    ppermute x7, waiting for transfers between devices, shards(): move = lambda x, pairs: lax.ppermute(x, 'row', pairs)  47.2 us
    pallas_call x2, Pallas kernels, run_slots(): pl.pallas_call(functools.partial(slots_kernel, joint), out_shape=tuple((p...  22.5 us
    ppermute x7, starting transfers between devices, shards(): move = lambda x, pairs: lax.ppermute(x, 'row', pairs)  16 us
    unnamed x21, local copies, waits for them, and re-layouts  6.4 us
    pallas_call x1, Pallas kernels, shards(): pl.pallas_call(finish_kernel, out_shape=jax.ShapeDtypeStruct(field.shape,...  4.16 us
    pallas_call x1, Pallas kernels, shards(): pl.pallas_call(sum_kernel, out_shape=jax.ShapeDtypeStruct(field.shape, f3...  3.97 us
    pallas_call x1, Pallas kernels, shards(): pl.pallas_call(pack_late_kernel, out_shape=(packed(CAP_FWD), packed(CAP_F...  3.67 us
  transfers between devices with their start and end apart: 7, of which 5 were waited for; matrix products, arithmetic and copies ran while one was open for 1% of the time, Pallas kernels for 25%

profile of v4, /device:TPU:20, one launch (start us, length us, event | category | flops | bytes accessed | tf_op | source)
XLA Modules:
  0.0 108.2 jit_solution(16783822150664465475)
XLA Ops:
  0.7 0.8 copy.10
  1.4 0.1 reshape.21
  1.5 0.1 pad_add_fusion.own
  1.6 2.2 %copy-done = f32[2,2,256,1024]{3,2,1,0:T(8,128)S(1)} copy-done((f32[2,2,256,1024]{3,2,1,0:T(8,128)S(1)}, f32[2,2,256,1024]{3,2,1,0:T(8,128)}, u32[]{:S(2)}) %copy-start) | copy-done | bytes 4194328
  3.8 1.2 %copy-done.4 = f32[4,256,256]{2,1,0:T(8,128)S(1)} copy-done((f32[4,256,256]{2,1,0:T(8,128)S(1)}, f32[4,256,256]{2,1,0:T(8,128)}, u32[]{:S(2)}) %copy-start.4) | copy-done | bytes 1048600
  5.0 1.8 %shard_map.82 = (f32[48,4,8,256]{3,2,1,0:T(8,128)}, s32[16]{0:T(128)S(1)}) custom-call(s32[1]{0:T(128)} %bitcast.1.odd.role.role_in, s32[16]{0:T(128)S(1)} %pad_add_fusion.own, f32[4,256,1024]{2,1,0:T(8,128)S(1)} %bitcast.9, f32[4,8,4,8,256]{4,3,2,1,0:T(8,128)S(1)} %bitcast.13), custom_call_target="tpu_custom_call" | custom-call | tf_op jit(solution)/shard_map/pallas_call | solution.py:678
  6.8 2.1 %collective-permute-start = (s32[16]{0:T(128)S(1)}, s32[16]{0:T(128)S(1)}, u32[]{:S(2)}, u32[]{:S(2)}) collective-permute-start(s32[16]{0:T(128)S(1)} %get-tuple-element.16), channel_id=1, source_target_pairs={{0,1},{2,3},{4,5},{6,7},{8,9},{10,11},{12,13},{14,15},{1,2},{3,4},... | collective-permute-start | bytes 200 | tf_op jit(solution)/shard_map/ppermute | solution.py:670
  8.9 2.9 %collective-permute-done.before = s32[16]{0:T(128)S(1)} collective-permute-done((s32[16]{0:T(128)S(1)}, s32[16]{0:T(128)S(1)}, u32[]{:S(2)}, u32[]{:S(2)}) %collective-permute-start) | collective-permute-done | bytes 96 | tf_op jit(solution)/shard_map/ppermute | solution.py:670
  11.8 3.7 %shard_map.83 = (f32[48,4,8,256]{3,2,1,0:T(8,128)}, f32[48,4,8,256]{3,2,1,0:T(8,128)}, s32[32]{0:T(128)S(1)}, s32[32]{0:T(128)S(1)}) custom-call(s32[1]{0:T(128)} %bitcast.1.odd.role.role_in, s32[16]{0:T(128)S(1)} %pad_add_fusion.own, s32[16]{0:T(128)S(1)} %collective-permute-done.before, f32[4,256,1024]{2,1,0:T(8,128)S(1)} %bitcast.10, ...), custom_call_target="tpu_custom_call" | custom-call | tf_op jit(solution)/shard_map/pallas_call | solution.py:694
  15.6 1.4 %collective-permute-start.4 = (f32[48,4,8,256]{3,2,1,0:T(8,128)}, f32[48,4,8,256]{3,2,1,0:T(8,128)}, u32[]{:S(2)}, u32[]{:S(2)}) collective-permute-start(f32[48,4,8,256]{3,2,1,0:T(8,128)} %get-tuple-element.23), channel_id=1, source_target_pairs={{1,2},{3,4},{5,6},{7,8},{9,10},{11,12},{13,14},{17,18},{19,20},{21... | collective-permute-start | bytes 4718600 | tf_op jit(solution)/shard_map/ppermute | solution.py:670
  17.0 6.6 %collective-permute-start.3 = (f32[48,4,8,256]{3,2,1,0:T(8,128)}, f32[48,4,8,256]{3,2,1,0:T(8,128)}, u32[]{:S(2)}, u32[]{:S(2)}) collective-permute-start(f32[48,4,8,256]{3,2,1,0:T(8,128)} %get-tuple-element.22), channel_id=1, source_target_pairs={{2,1},{4,3},{6,5},{8,7},{10,9},{12,11},{14,13},{18,17},{20,19},{22... | collective-permute-start | bytes 4718600 | tf_op jit(solution)/shard_map/ppermute | solution.py:670
  23.6 0.9 cosine_bitcast_fusion
  24.6 0.4 shard_map.84.kernel
  25.1 2.2 %copy-done.2 = f32[2,2,256,1024]{3,2,1,0:T(8,128)S(1)} copy-done((f32[2,2,256,1024]{3,2,1,0:T(8,128)S(1)}, f32[2,2,256,1024]{3,2,1,0:T(8,128)}, u32[]{:S(2)}) %copy-start.2) | copy-done | bytes 4194328
  27.3 10.7 %shard_map.85 = (f32[48,4,8,256]{3,2,1,0:T(8,128)S(1)}, f32[4,4,256,256]{3,2,1,0:T(8,128)S(1)}) custom-call(s32[1]{0:T(128)} %bitcast.1.odd.role.role_in, s32[32]{0:T(128)S(1)} %get-tuple-element.18.table.table_in, f32[4,256,1024]{2,1,0:T(8,128)S(1)} %bitcast.11, f32[4,256,256]{2,1,0:T(8,128)S(1)} %copy-done.5, f32[2,256,256]{2,1,0:T(8,128)S(1)} %copy-done.7, ...), custom_call_target="tpu_custom_call" | custom-call | tf_op jit(solution)/shard_map/pallas_call | solution.py:640
  38.1 16.5 %collective-permute-done.4.from_a = f32[48,4,8,256]{3,2,1,0:T(8,128)} collective-permute-done((f32[48,4,8,256]{3,2,1,0:T(8,128)}, f32[48,4,8,256]{3,2,1,0:T(8,128)}, u32[]{:S(2)}, u32[]{:S(2)}) %collective-permute-start.4) | collective-permute-done | bytes 1572896 | tf_op jit(solution)/shard_map/ppermute | solution.py:670
  54.6 15.7 %collective-permute-done.3.from_b = f32[48,4,8,256]{3,2,1,0:T(8,128)} collective-permute-done((f32[48,4,8,256]{3,2,1,0:T(8,128)}, f32[48,4,8,256]{3,2,1,0:T(8,128)}, u32[]{:S(2)}, u32[]{:S(2)}) %collective-permute-start.3) | collective-permute-done | bytes 1572896 | tf_op jit(solution)/shard_map/ppermute | solution.py:670
  70.3 11.8 %shard_map.86 = (f32[48,4,8,256]{3,2,1,0:T(8,128)S(1)}, f32[32,4,8,256]{3,2,1,0:T(8,128)S(1)}, f32[4,4,256,256]{3,2,1,0:T(8,128)S(1)}) custom-call(s32[1]{0:T(128)} %bitcast.role.role_out, s32[32]{0:T(128)S(1)} %get-tuple-element.17.table.table_out, f32[4,256,1024]{2,1,0:T(8,128)S(1)} %bitcast.12, f32[4,256,256]{2,1,0:T(8,128)S(1)} %copy-done.5, ...), custom_call_target="tpu_custom_call" | custom-call | tf_op jit(solution)/shard_map/pallas_call | solution.py:640
  82.1 1.3 %collective-permute-start.5 = (f32[48,4,8,256]{3,2,1,0:T(8,128)S(1)}, f32[48,4,8,256]{3,2,1,0:T(8,128)S(1)}, u32[]{:S(2)}, u32[]{:S(2)}) collective-permute-start(f32[48,4,8,256]{3,2,1,0:T(8,128)S(1)} %get-tuple-element.25), channel_id=1, source_target_pairs={{1,2},{3,4},{5,6},{7,8},{9,10},{11,12},{13,14},{17,18},{19,20},{21... | collective-permute-start | bytes 4718600 | tf_op jit(solution)/shard_map/ppermute | solution.py:670
  83.4 4.4 %collective-permute-start.6 = (f32[32,4,8,256]{3,2,1,0:T(8,128)S(1)}, f32[32,4,8,256]{3,2,1,0:T(8,128)S(1)}, u32[]{:S(2)}, u32[]{:S(2)}) collective-permute-start(f32[32,4,8,256]{3,2,1,0:T(8,128)S(1)} %get-tuple-element.26), channel_id=1, source_target_pairs={{2,1},{4,3},{6,5},{8,7},{10,9},{12,11},{14,13},{18,17},{20,19},{22... | collective-permute-start | bytes 3145736 | tf_op jit(solution)/shard_map/ppermute | solution.py:670
  87.9 4.0 %shard_map.87.total_in = f32[4,256,1024]{2,1,0:T(8,128)S(1)} custom-call(s32[1]{0:T(128)} %bitcast.1.odd.role.role_in, s32[32]{0:T(128)S(1)} %get-tuple-element.18.table.table_in, s32[1]{0:T(128)} %bitcast.role.role_out, s32[32]{0:T(128)S(1)} %get-tuple-element.17.table.table_out, f32[48,4,8,256]{3,2,1,0:T(8,128)S(1)} %collective-permute-done.2.in_back, ...), custom_call_target="tpu_custom_call" | custom-call | tf_op jit(solution)/shard_map/pallas_call | solution.py:725
  91.8 8.2 %collective-permute-done.6.out_b = f32[32,4,8,256]{3,2,1,0:T(8,128)S(1)} collective-permute-done((f32[32,4,8,256]{3,2,1,0:T(8,128)S(1)}, f32[32,4,8,256]{3,2,1,0:T(8,128)S(1)}, u32[]{:S(2)}, u32[]{:S(2)}) %collective-permute-start.6) | collective-permute-done | bytes 1048608 | tf_op jit(solution)/shard_map/ppermute | solution.py:670
  100.1 3.8 %collective-permute-done.5.out_a = f32[48,4,8,256]{3,2,1,0:T(8,128)S(1)} collective-permute-done((f32[48,4,8,256]{3,2,1,0:T(8,128)S(1)}, f32[48,4,8,256]{3,2,1,0:T(8,128)S(1)}, u32[]{:S(2)}, u32[]{:S(2)}) %collective-permute-start.5) | collective-permute-done | bytes 1572896 | tf_op jit(solution)/shard_map/ppermute | solution.py:670
  103.8 4.2 %shard_map.88 = f32[4,256,1024]{2,1,0:T(8,128)} custom-call(s32[1]{0:T(128)} %bitcast.role.role_out, s32[32]{0:T(128)S(1)} %get-tuple-element.17.table.table_out, f32[4,256,1024]{2,1,0:T(8,128)S(1)} %shard_map.87.total_in, f32[48,4,8,256]{3,2,1,0:T(8,128)S(1)} %collective-permute-done.5.out_a, f32[32,4,8,256]{3,2,1,0:T(8,128)S(1)} %collective-permute-done.6.out_b), custom_call_target="tpu_custom_call" | custom-call | tf_op jit(solution)/shard_map/pallas_call | solution.py:738
  (23 shorter events, 0.2 us)
Async XLA Ops:
  1.6 2.2 %copy-start = (f32[2,2,256,1024]{3,2,1,0:T(8,128)S(1)}, f32[2,2,256,1024]{3,2,1,0:T(8,128)}, u32[]{:S(2)}) copy-start(f32[2,2,256,1024]{3,2,1,0:T(8,128)} %param.8) | copy-start | bytes 12582916
  3.8 1.2 %copy-start.4 = (f32[4,256,256]{2,1,0:T(8,128)S(1)}, f32[4,256,256]{2,1,0:T(8,128)}, u32[]{:S(2)}) copy-start(f32[4,256,256]{2,1,0:T(8,128)} %intensity.3) | copy-start | bytes 3145732
  5.0 6.8 %copy-start.1 = (f32[2,2,256,1024]{3,2,1,0:T(8,128)S(1)}, f32[2,2,256,1024]{3,2,1,0:T(8,128)}, u32[]{:S(2)}) copy-start(f32[2,2,256,1024]{3,2,1,0:T(8,128)} %param.8) | copy-start | bytes 12582916
  5.0 6.8 %copy-start.5 = (f32[4,256,256]{2,1,0:T(8,128)S(1)}, f32[4,256,256]{2,1,0:T(8,128)}, u32[]{:S(2)}) copy-start(f32[4,256,256]{2,1,0:T(8,128)} %intensity.3) | copy-start | bytes 3145732
  6.8 16.8 %copy-start.9 = (f32[256,256]{1,0:T(8,128)S(1)}, f32[256,256]{1,0:T(8,128)}, u32[]{:S(2)}) copy-start(f32[256,256]{1,0:T(8,128)} %param.10) | copy-start | bytes 786436
  6.8 5.0 %collective-permute-start = (s32[16]{0:T(128)S(1)}, s32[16]{0:T(128)S(1)}, u32[]{:S(2)}, u32[]{:S(2)}) collective-permute-start(s32[16]{0:T(128)S(1)} %get-tuple-element.16), channel_id=1, source_target_pairs={{0,1},{2,3},{4,5},{6,7},{8,9},{10,11},{12,13},{14,15},{1,2},{3,4},... | collective-permute-start | bytes 200 | tf_op jit(solution)/shard_map/ppermute | solution.py:670
  15.5 9.2 %copy-start.8 = (bf16[256,256]{1,0:T(8,128)(2,1)S(1)}, bf16[256,256]{1,0:T(8,128)(2,1)}, u32[]{:S(2)}) copy-start(bf16[256,256]{1,0:T(8,128)(2,1)} %constant.13.clone.shuffle) | copy-start | bytes 393220
  15.5 9.6 %copy-start.7 = (f32[2,256,256]{2,1,0:T(8,128)S(1)}, f32[2,256,256]{2,1,0:T(8,128)}, u32[]{:S(2)}) copy-start(f32[2,256,256]{2,1,0:T(8,128)} %probe.3) | copy-start | bytes 1572868
  15.5 9.6 %collective-permute-start.1 = (f32[48,4,8,256]{3,2,1,0:T(8,128)}, f32[48,4,8,256]{3,2,1,0:T(8,128)S(1)}, u32[]{:S(2)}, u32[]{:S(2)}) collective-permute-start(f32[48,4,8,256]{3,2,1,0:T(8,128)} %get-tuple-element.19), channel_id=1, source_target_pairs={{0,1},{2,3},{4,5},{6,7},{8,9},{10,11},{12,13},{14,15},{1,0},{3,2},... | collective-permute-start | bytes 4718600 | tf_op jit(solution)/shard_map/ppermute | solution.py:670
  15.6 39.0 %collective-permute-start.4 = (f32[48,4,8,256]{3,2,1,0:T(8,128)}, f32[48,4,8,256]{3,2,1,0:T(8,128)}, u32[]{:S(2)}, u32[]{:S(2)}) collective-permute-start(f32[48,4,8,256]{3,2,1,0:T(8,128)} %get-tuple-element.23), channel_id=1, source_target_pairs={{1,2},{3,4},{5,6},{7,8},{9,10},{11,12},{13,14},{17,18},{19,20},{21... | collective-permute-start | bytes 4718600 | tf_op jit(solution)/shard_map/ppermute | solution.py:670
  17.0 53.3 %collective-permute-start.3 = (f32[48,4,8,256]{3,2,1,0:T(8,128)}, f32[48,4,8,256]{3,2,1,0:T(8,128)}, u32[]{:S(2)}, u32[]{:S(2)}) collective-permute-start(f32[48,4,8,256]{3,2,1,0:T(8,128)} %get-tuple-element.22), channel_id=1, source_target_pairs={{2,1},{4,3},{6,5},{8,7},{10,9},{12,11},{14,13},{18,17},{20,19},{22... | collective-permute-start | bytes 4718600 | tf_op jit(solution)/shard_map/ppermute | solution.py:670
  23.6 1.5 %copy-start.6 = (bf16[4,2,256,256]{3,2,1,0:T(8,128)(2,1)S(1)}, bf16[4,2,256,256]{3,2,1,0:T(8,128)(2,1)}, u32[]{:S(2)}) copy-start(bf16[4,2,256,256]{3,2,1,0:T(8,128)(2,1)} %constant.12.clone.forms) | copy-start | bytes 3145732
  25.1 2.2 %copy-start.2 = (f32[2,2,256,1024]{3,2,1,0:T(8,128)S(1)}, f32[2,2,256,1024]{3,2,1,0:T(8,128)}, u32[]{:S(2)}) copy-start(f32[2,2,256,1024]{3,2,1,0:T(8,128)} %param.8) | copy-start | bytes 12582916
  27.3 43.0 %copy-start.3 = (f32[2,2,256,1024]{3,2,1,0:T(8,128)S(1)}, f32[2,2,256,1024]{3,2,1,0:T(8,128)}, u32[]{:S(2)}) copy-start(f32[2,2,256,1024]{3,2,1,0:T(8,128)} %param.8) | copy-start | bytes 12582916
  38.0 49.8 %collective-permute-start.2 = (f32[48,4,8,256]{3,2,1,0:T(8,128)S(1)}, f32[48,4,8,256]{3,2,1,0:T(8,128)S(1)}, u32[]{:S(2)}, u32[]{:S(2)}) collective-permute-start(f32[48,4,8,256]{3,2,1,0:T(8,128)S(1)} %get-tuple-element.20), channel_id=1, source_target_pairs={{0,1},{2,3},{4,5},{6,7},{8,9},{10,11},{12,13},{14,15},{1,0},{3,2},... | collective-permute-start | bytes 4718600 | tf_op jit(solution)/shard_map/ppermute | solution.py:670
  82.1 21.7 %collective-permute-start.5 = (f32[48,4,8,256]{3,2,1,0:T(8,128)S(1)}, f32[48,4,8,256]{3,2,1,0:T(8,128)S(1)}, u32[]{:S(2)}, u32[]{:S(2)}) collective-permute-start(f32[48,4,8,256]{3,2,1,0:T(8,128)S(1)} %get-tuple-element.25), channel_id=1, source_target_pairs={{1,2},{3,4},{5,6},{7,8},{9,10},{11,12},{13,14},{17,18},{19,20},{21... | collective-permute-start | bytes 4718600 | tf_op jit(solution)/shard_map/ppermute | solution.py:670
  83.4 16.7 %collective-permute-start.6 = (f32[32,4,8,256]{3,2,1,0:T(8,128)S(1)}, f32[32,4,8,256]{3,2,1,0:T(8,128)S(1)}, u32[]{:S(2)}, u32[]{:S(2)}) collective-permute-start(f32[32,4,8,256]{3,2,1,0:T(8,128)S(1)} %get-tuple-element.26), channel_id=1, source_target_pairs={{2,1},{4,3},{6,5},{8,7},{10,9},{12,11},{14,13},{18,17},{20,19},{22... | collective-permute-start | bytes 3145736 | tf_op jit(solution)/shard_map/ppermute | solution.py:670

commit v5 on v4

--- a/solution.py
+++ b/solution.py
@@ -25,6 +25,8 @@
 bf16 = jnp.bfloat16
 VM = pltpu.MemorySpace.VMEM
 SM = pltpu.MemorySpace.SMEM
+HB = pltpu.MemorySpace.HBM
+CHEAP = pl.CostEstimate(flops=1, transcendentals=0, bytes_accessed=1)
 
 
 def real_tables():
@@ -302,7 +304,8 @@
             out[plane, part * HALF : (part + 1) * HALF, :] = total
 
 
-def slots_kernel(joint, role, table, field, intensity, probe, kernel, forms, shuffle, from_b, from_a, *rest):
+def slots_kernel(joint, role, table, field, intensity, probe, kernel, forms, shuffle, from_b, from_a, after, *rest):
+    del after
     back_a, back_b = rest[0], rest[0 if joint else 1]
     tiles, held, got, tile, measured, twice, beam, work, entered, chosen = rest[1 if joint else 2 : -4]
     held_sem, int_sem, got_sem, tile_sem = rest[-4:]
@@ -635,13 +638,13 @@
     return jax.ShapeDtypeStruct((groups, 4, SUB, WIN), f32)
 
 
-def run_slots(joint, role, table, field, intensity, probe, kernel, tables, from_b, from_a):
+def run_slots(joint, role, table, field, intensity, probe, kernel, tables, from_b, from_a, after):
     backs = (CAP_BACK_A,) if joint else (CAP_BACK_A, CAP_BACK_B)
     return pl.pallas_call(
         functools.partial(slots_kernel, joint),
         out_shape=tuple(packed(n) for n in backs) + (jax.ShapeDtypeStruct((CAP, 4, WIN, WIN), f32),),
-        in_specs=[spec(SM)] * 2 + [spec(pl.ANY)] * 2 + [spec(VM)] * 4 + [spec(pl.ANY)] * 2,
-        out_specs=(spec(VM),) * len(backs) + (spec(pl.ANY),),
+        in_specs=[spec(SM)] * 2 + [spec(HB)] * 2 + [spec(VM)] * 4 + [spec(pl.ANY)] * 3,
+        out_specs=(spec(VM),) * len(backs) + (spec(HB),),
         scratch_shapes=[
             pltpu.VMEM((CAP, 4, WIN, WIDE), f32),
             pltpu.VMEM((CAP_FWD, 4, SUB, WIN), f32),
@@ -657,8 +660,9 @@
             pltpu.SemaphoreType.DMA,
             pltpu.SemaphoreType.DMA((2,)),
         ],
-        compiler_params=vmem(32),
-    )(role, table, field, intensity, probe, kernel, *tables, from_b, from_a)
+        cost_estimate=CHEAP,
+        compiler_params=vmem(56),
+    )(role, table, field, intensity, probe, kernel, *tables, from_b, from_a, after)
 
 
 def shards(obj_field, probe_wave, prop_phase, win_offsets, live_counts, intensity):
@@ -678,7 +682,7 @@
     to_b, info = pl.pallas_call(
         pack_early_kernel,
         out_shape=(packed(CAP_FWD), jax.ShapeDtypeStruct((INFO,), jnp.int32)),
-        in_specs=[spec(SM)] * 2 + [spec(pl.ANY)] * 2,
+        in_specs=[spec(SM)] * 2 + [spec(HB)] * 2,
         out_specs=(spec(VM), spec(SM)),
         scratch_shapes=[
             pltpu.SMEM((CAP * FIELDS,), jnp.int32),
@@ -686,7 +690,8 @@
             pltpu.SemaphoreType.DMA((CAP,)),
             pltpu.SemaphoreType.DMA((CAP,)),
         ],
-        compiler_params=vmem(16),
+        cost_estimate=CHEAP,
+        compiler_params=vmem(58),
     )(flag, own, field, maps)
     out_from_a = move(to_b, across)
     before = move(info, within + across)
@@ -694,14 +699,15 @@
     to_a, inner, table_in, table_out = pl.pallas_call(
         pack_late_kernel,
         out_shape=(packed(CAP_FWD), packed(CAP_FWD), table, table),
-        in_specs=[spec(SM)] * 3 + [spec(pl.ANY)] * 2,
+        in_specs=[spec(SM)] * 3 + [spec(HB)] * 2,
         out_specs=(spec(VM), spec(VM), spec(SM), spec(SM)),
         scratch_shapes=[
             pltpu.VMEM((2 * CAP, 4, WIN, WIDE), f32),
             pltpu.SemaphoreType.DMA((2 * CAP,)),
             pltpu.SemaphoreType.DMA((CAP,)),
         ],
-        compiler_params=vmem(24),
+        cost_estimate=CHEAP,
+        compiler_params=vmem(58),
     )(flag, own, before, field, maps)
     out_from_b = move(to_a, back(across))
     in_from = move(inner, within + back(within))
@@ -713,13 +719,14 @@
         in_specs=[spec(VM)] * 2,
         out_specs=spec(VM),
         scratch_shapes=[pltpu.VMEM((2, WIN, LANES), f32)],
+        cost_estimate=CHEAP,
         compiler_params=vmem(8),
     )(jnp.stack([jnp.cos(prop_phase), jnp.sin(prop_phase)]), shuffle)
 
     args = (field, intensity, probe_wave, kernel, (forms, shuffle))
-    in_back, tiles_in = run_slots(True, role_in, table_in, *args, in_from, in_from)
+    in_back, tiles_in = run_slots(True, role_in, table_in, *args, in_from, in_from, out_from_a)
     in_back = move(in_back, within + back(within))
-    out_back_a, out_back_b, tiles_out = run_slots(False, role_out, table_out, *args, out_from_b, out_from_a)
+    out_back_a, out_back_b, tiles_out = run_slots(False, role_out, table_out, *args, out_from_b, out_from_a, out_from_a)
     out_a = move(out_back_a, across)
     out_b = move(out_back_b, back(across))
     total = pl.pallas_call(
@@ -733,19 +740,21 @@
             pltpu.SemaphoreType.DMA,
             pltpu.SemaphoreType.DMA((2 * CAP,)),
         ],
+        cost_estimate=CHEAP,
         compiler_params=vmem(20),
     )(role_in, table_in, role_out, table_out, in_back, tiles_in, tiles_out)
     grad = pl.pallas_call(
         finish_kernel,
         out_shape=jax.ShapeDtypeStruct(field.shape, f32),
         in_specs=[spec(SM)] * 2 + [spec(VM)] + [spec(pl.ANY)] * 2,
-        out_specs=spec(pl.ANY),
+        out_specs=spec(HB),
         scratch_shapes=[
             pltpu.VMEM(field.shape, f32),
             pltpu.VMEM((CAP_BACK_A, 4, SUB, WIN), f32),
             pltpu.SemaphoreType.DMA,
             pltpu.SemaphoreType.DMA((4,)),
         ],
+        cost_estimate=CHEAP,
         compiler_params=vmem(16),
     )(role_out, table_out, total, out_a, out_b)
     return grad.reshape(obj_field.shape)

time: 109 us -> 114 us (1.046)
  Pallas kernels: 36.5 us -> 44.7 us
  starting transfers between devices: 16 us -> 13.9 us
    pallas_call x2, Pallas kernels: 22.5 us -> 31.2 us  [run_slots(): pl.pallas_call(functools.partial(slots_kernel, joint), out_shape=tuple((p...]
    ppermute x7, starting transfers between devices: 16 us -> 13.9 us  [shards(): move = lambda x, pairs: lax.ppermute(x, 'row', pairs)]
    pallas_call x1, Pallas kernels: 4.16 us -> 2.8 us  [shards(): pl.pallas_call(finish_kernel, out_shape=jax.ShapeDtypeStruct(field.shape,...]
    unnamed x21 -> x19, local copies, waits for them, and re-layouts: 6.4 us -> 5.52 us
  transfers between devices with their start and end apart: 7 -> 7, of which waited for: 5 -> 4; matrix products, arithmetic and copies ran while one was open for 1% -> 1% of each run, Pallas kernels for 25% -> 35%
where the time goes in v5:
time: 114 us
  waiting for transfers between devices  46.7 us (41%)
  Pallas kernels  44.7 us (39%)
  starting transfers between devices  13.9 us (12%)
  local copies, waits for them, and re-layouts  6.55 us (6%)
    ppermute x7, waiting for transfers between devices, shards(): move = lambda x, pairs: lax.ppermute(x, 'row', pairs)  46.7 us
    pallas_call x2, Pallas kernels, run_slots(): pl.pallas_call(functools.partial(slots_kernel, joint), out_shape=tuple((p...  31.2 us
    ppermute x7, starting transfers between devices, shards(): move = lambda x, pairs: lax.ppermute(x, 'row', pairs)  13.9 us
    unnamed x19, local copies, waits for them, and re-layouts  5.52 us
    pallas_call x1, Pallas kernels, shards(): pl.pallas_call(pack_late_kernel, out_shape=(packed(CAP_FWD), packed(CAP_F...  4.68 us
    pallas_call x1, Pallas kernels, shards(): pl.pallas_call(sum_kernel, out_shape=jax.ShapeDtypeStruct(field.shape, f3...  3.74 us
    pallas_call x1, Pallas kernels, shards(): pl.pallas_call(finish_kernel, out_shape=jax.ShapeDtypeStruct(field.shape,...  2.8 us
  transfers between devices with their start and end apart: 7, of which 4 were waited for; matrix products, arithmetic and copies ran while one was open for 1% of the time, Pallas kernels for 35%

profile of v5, /device:TPU:20, one launch (start us, length us, event | category | flops | bytes accessed | tf_op | source)
XLA Modules:
  0.0 113.6 jit_solution(11384997308217264306)
XLA Ops:
  0.7 0.8 copy.10
  1.5 0.7 pad_add_fusion.own
  2.2 1.9 %shard_map.82 = (f32[48,4,8,256]{3,2,1,0:T(8,128)}, s32[16]{0:T(128)}) custom-call(s32[1]{0:T(128)} %bitcast.1.odd.role.role_in, s32[16]{0:T(128)} %pad_add_fusion.own, f32[4,256,1024]{2,1,0:T(8,128)} %bitcast.9, f32[4,8,4,8,256]{4,3,2,1,0:T(8,128)} %bitcast.13), custom_call_target="tpu_custom_call" | custom-call | flops 1 | bytes 1 | tf_op jit(solution)/shard_map/pallas_call | solution.py:682
  4.1 1.9 %collective-permute-start = (s32[16]{0:T(128)}, s32[16]{0:T(128)S(1)}, u32[]{:S(2)}, u32[]{:S(2)}) collective-permute-start(s32[16]{0:T(128)} %get-tuple-element.16), channel_id=1, source_target_pairs={{0,1},{2,3},{4,5},{6,7},{8,9},{10,11},{12,13},{14,15},{1,2},{3,4},... | collective-permute-start | bytes 200 | tf_op jit(solution)/shard_map/ppermute | solution.py:674
  6.0 1.4 %collective-permute-start.2 = (f32[48,4,8,256]{3,2,1,0:T(8,128)}, f32[48,4,8,256]{3,2,1,0:T(8,128)S(1)}, u32[]{:S(2)}, u32[]{:S(2)}) collective-permute-start(f32[48,4,8,256]{3,2,1,0:T(8,128)} %get-tuple-element.20), channel_id=1, source_target_pairs={{1,2},{3,4},{5,6},{7,8},{9,10},{11,12},{13,14},{17,18},{19,20},{21... | collective-permute-start | bytes 4718600 | tf_op jit(solution)/shard_map/ppermute | solution.py:674
  7.5 1.5 %collective-permute-done.before = s32[16]{0:T(128)S(1)} collective-permute-done((s32[16]{0:T(128)}, s32[16]{0:T(128)S(1)}, u32[]{:S(2)}, u32[]{:S(2)}) %collective-permute-start) | collective-permute-done | bytes 96 | tf_op jit(solution)/shard_map/ppermute | solution.py:674
  9.0 0.6 copy-done.8
  9.6 4.7 %shard_map.83 = (f32[48,4,8,256]{3,2,1,0:T(8,128)}, f32[48,4,8,256]{3,2,1,0:T(8,128)}, s32[32]{0:T(128)}, s32[32]{0:T(128)}) custom-call(s32[1]{0:T(128)} %bitcast.1.odd.role.role_in, s32[16]{0:T(128)} %pad_add_fusion.own, s32[16]{0:T(128)} %copy-done.8, f32[4,256,1024]{2,1,0:T(8,128)} %bitcast.10, f32[4,8,4,8,256]{4,3,2,1,0:T(8,128)} %bitcast.14), custom_call_target="tpu_custom_call" | custom-call | flops 1 | bytes 1 | tf_op jit(solution)/shard_map/pallas_call | solution.py:699
  14.3 2.3 %collective-permute-start.1 = (f32[48,4,8,256]{3,2,1,0:T(8,128)}, f32[48,4,8,256]{3,2,1,0:T(8,128)}, u32[]{:S(2)}, u32[]{:S(2)}) collective-permute-start(f32[48,4,8,256]{3,2,1,0:T(8,128)} %get-tuple-element.19), channel_id=1, source_target_pairs={{0,1},{2,3},{4,5},{6,7},{8,9},{10,11},{12,13},{14,15},{1,0},{3,2},... | collective-permute-start | bytes 4718600 | tf_op jit(solution)/shard_map/ppermute | solution.py:674
  16.6 2.5 %collective-permute-start.4 = (f32[48,4,8,256]{3,2,1,0:T(8,128)}, f32[48,4,8,256]{3,2,1,0:T(8,128)}, u32[]{:S(2)}, u32[]{:S(2)}) collective-permute-start(f32[48,4,8,256]{3,2,1,0:T(8,128)} %get-tuple-element.23), channel_id=1, source_target_pairs={{2,1},{4,3},{6,5},{8,7},{10,9},{12,11},{14,13},{18,17},{20,19},{22... | collective-permute-start | bytes 4718600 | tf_op jit(solution)/shard_map/ppermute | solution.py:674
  19.1 0.9 cosine_bitcast_fusion
  20.1 0.4 shard_map.84.kernel
  20.5 0.8 copy-done
  21.3 23.7 %collective-permute-done.2.after.from_a = f32[48,4,8,256]{3,2,1,0:T(8,128)S(1)} collective-permute-done((f32[48,4,8,256]{3,2,1,0:T(8,128)}, f32[48,4,8,256]{3,2,1,0:T(8,128)S(1)}, u32[]{:S(2)}, u32[]{:S(2)}) %collective-permute-start.2) | collective-permute-done | bytes 1572896 | tf_op jit(solution)/shard_map/ppermute | solution.py:674
  45.0 1.2 %copy-done.6 = f32[48,4,8,256]{3,2,1,0:T(8,128)} copy-done((f32[48,4,8,256]{3,2,1,0:T(8,128)}, f32[48,4,8,256]{3,2,1,0:T(8,128)S(1)}, u32[]{:S(2)}) %copy-start.6) | copy-done | bytes 1572888
  46.2 15.7 %shard_map.85 = (f32[48,4,8,256]{3,2,1,0:T(8,128)}, f32[4,4,256,256]{3,2,1,0:T(8,128)}) custom-call(s32[1]{0:T(128)} %bitcast.1.odd.role.role_in, s32[32]{0:T(128)} %get-tuple-element.18.table.table_in, f32[4,256,1024]{2,1,0:T(8,128)} %bitcast.11, f32[4,256,256]{2,1,0:T(8,128)} %intensity.3, f32[2,256,256]{2,1,0:T(8,128)} %probe.3, f32[2,256,256]{2,1,0:T(8,128)} %copy-done, ...), custom_call_target="tpu_custom_call" | custom-call | flops 1 | bytes 1 | tf_op jit(solution)/shard_map/pallas_call | solution.py:643
  62.0 15.5 %shard_map.86 = (f32[48,4,8,256]{3,2,1,0:T(8,128)}, f32[32,4,8,256]{3,2,1,0:T(8,128)}, f32[4,4,256,256]{3,2,1,0:T(8,128)}) custom-call(s32[1]{0:T(128)} %bitcast.role.role_out, s32[32]{0:T(128)} %get-tuple-element.17.table.table_out, f32[4,256,1024]{2,1,0:T(8,128)} %bitcast.12, f32[4,256,256]{2,1,0:T(8,128)} %intensity.3, f32[2,256,256]{2,1,0:T(8,128)} %probe.3, ...), custom_call_target="tpu_custom_call" | custom-call | flops 1 | bytes 1 | tf_op jit(solution)/shard_map/pallas_call | solution.py:643
  77.5 1.3 %collective-permute-start.5 = (f32[48,4,8,256]{3,2,1,0:T(8,128)}, f32[48,4,8,256]{3,2,1,0:T(8,128)S(1)}, u32[]{:S(2)}, u32[]{:S(2)}) collective-permute-start(f32[48,4,8,256]{3,2,1,0:T(8,128)} %get-tuple-element.25), channel_id=1, source_target_pairs={{1,2},{3,4},{5,6},{7,8},{9,10},{11,12},{13,14},{17,18},{19,20},{21... | collective-permute-start | bytes 4718600 | tf_op jit(solution)/shard_map/ppermute | solution.py:674
  78.8 4.4 %collective-permute-start.6 = (f32[32,4,8,256]{3,2,1,0:T(8,128)}, f32[32,4,8,256]{3,2,1,0:T(8,128)S(1)}, u32[]{:S(2)}, u32[]{:S(2)}) collective-permute-start(f32[32,4,8,256]{3,2,1,0:T(8,128)} %get-tuple-element.26), channel_id=1, source_target_pairs={{2,1},{4,3},{6,5},{8,7},{10,9},{12,11},{14,13},{18,17},{20,19},{22... | collective-permute-start | bytes 3145736 | tf_op jit(solution)/shard_map/ppermute | solution.py:674
  83.3 2.2 %copy-done.2 = f32[4,4,256,256]{3,2,1,0:T(8,128)S(1)} copy-done((f32[4,4,256,256]{3,2,1,0:T(8,128)S(1)}, f32[4,4,256,256]{3,2,1,0:T(8,128)}, u32[]{:S(2)}) %copy-start.2) | copy-done | bytes 4194328
  85.5 3.7 %shard_map.87.total_in = f32[4,256,1024]{2,1,0:T(8,128)S(1)} custom-call(s32[1]{0:T(128)} %bitcast.1.odd.role.role_in, s32[32]{0:T(128)S(1)} %copy-done.5, s32[1]{0:T(128)} %bitcast.role.role_out, s32[32]{0:T(128)S(1)} %copy-done.4, f32[48,4,8,256]{3,2,1,0:T(8,128)S(1)} %collective-permute-done.3.in_back, f32[4,4,256,256]{3,2,1,0:T(8,128)S(1)} %copy-done.1, ...), custom_call_target="tpu_custom_call" | custom-call | flops 1 | bytes 1 | tf_op jit(solution)/shard_map/pallas_call | solution.py:732
  89.2 8.3 %collective-permute-done.6.out_b = f32[32,4,8,256]{3,2,1,0:T(8,128)S(1)} collective-permute-done((f32[32,4,8,256]{3,2,1,0:T(8,128)}, f32[32,4,8,256]{3,2,1,0:T(8,128)S(1)}, u32[]{:S(2)}, u32[]{:S(2)}) %collective-permute-start.6) | collective-permute-done | bytes 1048608 | tf_op jit(solution)/shard_map/ppermute | solution.py:674
  97.5 13.2 %collective-permute-done.5.out_a = f32[48,4,8,256]{3,2,1,0:T(8,128)S(1)} collective-permute-done((f32[48,4,8,256]{3,2,1,0:T(8,128)}, f32[48,4,8,256]{3,2,1,0:T(8,128)S(1)}, u32[]{:S(2)}, u32[]{:S(2)}) %collective-permute-start.5) | collective-permute-done | bytes 1572896 | tf_op jit(solution)/shard_map/ppermute | solution.py:674
  110.7 2.8 %shard_map.88 = f32[4,256,1024]{2,1,0:T(8,128)} custom-call(s32[1]{0:T(128)} %bitcast.role.role_out, s32[32]{0:T(128)S(1)} %copy-done.4, f32[4,256,1024]{2,1,0:T(8,128)S(1)} %shard_map.87.total_in, f32[48,4,8,256]{3,2,1,0:T(8,128)S(1)} %collective-permute-done.5.out_a, f32[32,4,8,256]{3,2,1,0:T(8,128)S(1)} %collective-permute-done.6.out_b), custom_call_target="tpu_custom_call" | custom-call | flops 1 | bytes 1 | tf_op jit(solution)/shard_map/pallas_call | solution.py:746
  (21 shorter events, 0.2 us)
Async XLA Ops:
  4.1 4.9 %collective-permute-start = (s32[16]{0:T(128)}, s32[16]{0:T(128)S(1)}, u32[]{:S(2)}, u32[]{:S(2)}) collective-permute-start(s32[16]{0:T(128)} %get-tuple-element.16), channel_id=1, source_target_pairs={{0,1},{2,3},{4,5},{6,7},{8,9},{10,11},{12,13},{14,15},{1,2},{3,4},... | collective-permute-start | bytes 200 | tf_op jit(solution)/shard_map/ppermute | solution.py:674
  6.0 13.0 %copy-start.7 = (f32[256,256]{1,0:T(8,128)S(1)}, f32[256,256]{1,0:T(8,128)}, u32[]{:S(2)}) copy-start(f32[256,256]{1,0:T(8,128)} %param.10) | copy-start | bytes 786436
  6.0 38.9 %collective-permute-start.2 = (f32[48,4,8,256]{3,2,1,0:T(8,128)}, f32[48,4,8,256]{3,2,1,0:T(8,128)S(1)}, u32[]{:S(2)}, u32[]{:S(2)}) collective-permute-start(f32[48,4,8,256]{3,2,1,0:T(8,128)} %get-tuple-element.20), channel_id=1, source_target_pairs={{1,2},{3,4},{5,6},{7,8},{9,10},{11,12},{13,14},{17,18},{19,20},{21... | collective-permute-start | bytes 4718600 | tf_op jit(solution)/shard_map/ppermute | solution.py:674
  9.0 0.6 copy-start.8
  14.3 5.8 %copy-start.3 = (bf16[256,256]{1,0:T(8,128)(2,1)S(1)}, bf16[256,256]{1,0:T(8,128)(2,1)}, u32[]{:S(2)}) copy-start(bf16[256,256]{1,0:T(8,128)(2,1)} %constant.13.clone.shuffle) | copy-start | bytes 393220
  14.3 30.7 %collective-permute-start.1 = (f32[48,4,8,256]{3,2,1,0:T(8,128)}, f32[48,4,8,256]{3,2,1,0:T(8,128)}, u32[]{:S(2)}, u32[]{:S(2)}) collective-permute-start(f32[48,4,8,256]{3,2,1,0:T(8,128)} %get-tuple-element.19), channel_id=1, source_target_pairs={{0,1},{2,3},{4,5},{6,7},{8,9},{10,11},{12,13},{14,15},{1,0},{3,2},... | collective-permute-start | bytes 4718600 | tf_op jit(solution)/shard_map/ppermute | solution.py:674
  16.6 45.4 %collective-permute-start.4 = (f32[48,4,8,256]{3,2,1,0:T(8,128)}, f32[48,4,8,256]{3,2,1,0:T(8,128)}, u32[]{:S(2)}, u32[]{:S(2)}) collective-permute-start(f32[48,4,8,256]{3,2,1,0:T(8,128)} %get-tuple-element.23), channel_id=1, source_target_pairs={{2,1},{4,3},{6,5},{8,7},{10,9},{12,11},{14,13},{18,17},{20,19},{22... | collective-permute-start | bytes 4718600 | tf_op jit(solution)/shard_map/ppermute | solution.py:674
  20.5 0.8 copy-start
  45.0 1.2 %copy-start.6 = (f32[48,4,8,256]{3,2,1,0:T(8,128)}, f32[48,4,8,256]{3,2,1,0:T(8,128)S(1)}, u32[]{:S(2)}) copy-start(f32[48,4,8,256]{3,2,1,0:T(8,128)S(1)} %collective-permute-done.2.after.from_a) | copy-start | bytes 4718596
  61.9 21.4 %collective-permute-start.3 = (f32[48,4,8,256]{3,2,1,0:T(8,128)}, f32[48,4,8,256]{3,2,1,0:T(8,128)S(1)}, u32[]{:S(2)}, u32[]{:S(2)}) collective-permute-start(f32[48,4,8,256]{3,2,1,0:T(8,128)} %get-tuple-element.21), channel_id=1, source_target_pairs={{0,1},{2,3},{4,5},{6,7},{8,9},{10,11},{12,13},{14,15},{1,0},{3,2},... | collective-permute-start | bytes 4718600 | tf_op jit(solution)/shard_map/ppermute | solution.py:674
  61.9 21.3 %copy-start.1 = (f32[4,4,256,256]{3,2,1,0:T(8,128)S(1)}, f32[4,4,256,256]{3,2,1,0:T(8,128)}, u32[]{:S(2)}) copy-start(f32[4,4,256,256]{3,2,1,0:T(8,128)} %get-tuple-element.22.tiles_in) | copy-start | bytes 12582916
  62.0 21.3 %copy-start.4 = (s32[32]{0:T(128)S(1)}, s32[32]{0:T(128)}, u32[]{:S(2)}) copy-start(s32[32]{0:T(128)} %get-tuple-element.17.table.table_out) | copy-start | bytes 388
  62.0 21.3 %copy-start.5 = (s32[32]{0:T(128)S(1)}, s32[32]{0:T(128)}, u32[]{:S(2)}) copy-start(s32[32]{0:T(128)} %get-tuple-element.18.table.table_in) | copy-start | bytes 388
  77.5 33.2 %collective-permute-start.5 = (f32[48,4,8,256]{3,2,1,0:T(8,128)}, f32[48,4,8,256]{3,2,1,0:T(8,128)S(1)}, u32[]{:S(2)}, u32[]{:S(2)}) collective-permute-start(f32[48,4,8,256]{3,2,1,0:T(8,128)} %get-tuple-element.25), channel_id=1, source_target_pairs={{1,2},{3,4},{5,6},{7,8},{9,10},{11,12},{13,14},{17,18},{19,20},{21... | collective-permute-start | bytes 4718600 | tf_op jit(solution)/shard_map/ppermute | solution.py:674
  78.8 18.7 %collective-permute-start.6 = (f32[32,4,8,256]{3,2,1,0:T(8,128)}, f32[32,4,8,256]{3,2,1,0:T(8,128)S(1)}, u32[]{:S(2)}, u32[]{:S(2)}) collective-permute-start(f32[32,4,8,256]{3,2,1,0:T(8,128)} %get-tuple-element.26), channel_id=1, source_target_pairs={{2,1},{4,3},{6,5},{8,7},{10,9},{12,11},{14,13},{18,17},{20,19},{22... | collective-permute-start | bytes 3145736 | tf_op jit(solution)/shard_map/ppermute | solution.py:674
  83.3 2.2 %copy-start.2 = (f32[4,4,256,256]{3,2,1,0:T(8,128)S(1)}, f32[4,4,256,256]{3,2,1,0:T(8,128)}, u32[]{:S(2)}) copy-start(f32[4,4,256,256]{3,2,1,0:T(8,128)} %get-tuple-element.24.tiles_out) | copy-start | bytes 12582916

commit v6 on v4

--- a/solution.py
+++ b/solution.py
@@ -25,6 +25,8 @@
 bf16 = jnp.bfloat16
 VM = pltpu.MemorySpace.VMEM
 SM = pltpu.MemorySpace.SMEM
+HB = pltpu.MemorySpace.HBM
+CHEAP = pl.CostEstimate(flops=1, transcendentals=0, bytes_accessed=1)
 
 
 def real_tables():
@@ -257,33 +259,24 @@
             copy_groups(held, out, at, start, 0, (row + SUB - 1) // SUB, starts, shift)
 
 
-def pack_early_kernel(odd, own, field, intensity, out, info, table, held, sem, int_sem):
-    for j in range(INFO):
-        info[j] = own[j]
-
-    @pl.when(odd[0] == 1)
-    def _():
-        decide(own, table)
-        fetch_columns(table, AT_B, field, held, sem, 0)
-        pack_to_b(table, field, intensity, out, held, sem, int_sem, 0)
-
-
-def pack_late_kernel(odd, own, before, field, intensity, out, inner, table_in, table_out, held, sem, int_sem):
+def pack_kernel(odd, own, before, field, intensity, inner, outer, table_in, table_out, held, sem, int_sem):
     @pl.when(odd[0] == 0)
     def _():
         decide(before, table_out)
         fetch_columns(table_out, AT_A, field, held, sem, 0)
         decide(own, table_in)
         fetch_columns(table_in, AT_B, field, held, sem, CAP)
-        pack_to_a(table_out, field, out, held, sem, 0)
+        pack_to_a(table_out, field, outer, held, sem, 0)
         pack_to_b(table_in, field, intensity, inner, held, sem, int_sem, CAP)
 
     @pl.when(odd[0] == 1)
     def _():
+        decide(own, table_out)
+        fetch_columns(table_out, AT_B, field, held, sem, 0)
         decide(before, table_in)
-        fetch_columns(table_in, AT_A, field, held, sem, 0)
-        decide(own, table_out)
-        pack_to_a(table_in, field, inner, held, sem, 0)
+        fetch_columns(table_in, AT_A, field, held, sem, CAP)
+        pack_to_b(table_out, field, intensity, outer, held, sem, int_sem, 0)
+        pack_to_a(table_in, field, inner, held, sem, CAP)
 
 
 def prepare_kernel(phases, shuffle, out, halves):
@@ -640,8 +633,8 @@
     return pl.pallas_call(
         functools.partial(slots_kernel, joint),
         out_shape=tuple(packed(n) for n in backs) + (jax.ShapeDtypeStruct((CAP, 4, WIN, WIN), f32),),
-        in_specs=[spec(SM)] * 2 + [spec(pl.ANY)] * 2 + [spec(VM)] * 4 + [spec(pl.ANY)] * 2,
-        out_specs=(spec(VM),) * len(backs) + (spec(pl.ANY),),
+        in_specs=[spec(SM)] * 2 + [spec(HB)] * 2 + [spec(VM)] * 4 + [spec(pl.ANY)] * 2,
+        out_specs=(spec(VM),) * len(backs) + (spec(HB),),
         scratch_shapes=[
             pltpu.VMEM((CAP, 4, WIN, WIDE), f32),
             pltpu.VMEM((CAP_FWD, 4, SUB, WIN), f32),
@@ -657,12 +650,13 @@
             pltpu.SemaphoreType.DMA,
             pltpu.SemaphoreType.DMA((2,)),
         ],
+        cost_estimate=CHEAP,
         compiler_params=vmem(32),
     )(role, table, field, intensity, probe, kernel, *tables, from_b, from_a)
 
 
 def shards(obj_field, probe_wave, prop_phase, win_offsets, live_counts, intensity):
-    field = obj_field.reshape((4,) + obj_field.shape[2:])
+    field = pltpu.with_memory_space_constraint(obj_field.reshape((4,) + obj_field.shape[2:]), HB)
     count = lax.axis_size("row")
     within = [(i, i + 1) for i in range(0, count - 1, 2)]
     across = [(i, i + 1) for i in range(1, count - 1, 2)]
@@ -674,36 +668,24 @@
 
     flag = odd.reshape(1)
     own = jnp.concatenate([win_offsets.reshape(-1), live_counts, jnp.zeros((INFO - 2 * CAP - 1,), jnp.int32)])
-    maps = intensity.reshape(CAP, INT_GROUPS, 4, SUB, WIN)
-    to_b, info = pl.pallas_call(
-        pack_early_kernel,
-        out_shape=(packed(CAP_FWD), jax.ShapeDtypeStruct((INFO,), jnp.int32)),
-        in_specs=[spec(SM)] * 2 + [spec(pl.ANY)] * 2,
-        out_specs=(spec(VM), spec(SM)),
-        scratch_shapes=[
-            pltpu.SMEM((CAP * FIELDS,), jnp.int32),
-            pltpu.VMEM((CAP, 4, WIN, WIDE), f32),
-            pltpu.SemaphoreType.DMA((CAP,)),
-            pltpu.SemaphoreType.DMA((CAP,)),
-        ],
-        compiler_params=vmem(16),
-    )(flag, own, field, maps)
-    out_from_a = move(to_b, across)
-    before = move(info, within + across)
+    maps = pltpu.with_memory_space_constraint(intensity.reshape(CAP, INT_GROUPS, 4, SUB, WIN), HB)
+    intensity = pltpu.with_memory_space_constraint(intensity, HB)
+    before = move(own, within + across)
     table = jax.ShapeDtypeStruct((CAP * FIELDS,), jnp.int32)
-    to_a, inner, table_in, table_out = pl.pallas_call(
-        pack_late_kernel,
+    inner, outer, table_in, table_out = pl.pallas_call(
+        pack_kernel,
         out_shape=(packed(CAP_FWD), packed(CAP_FWD), table, table),
-        in_specs=[spec(SM)] * 3 + [spec(pl.ANY)] * 2,
+        in_specs=[spec(SM)] * 3 + [spec(HB)] * 2,
         out_specs=(spec(VM), spec(VM), spec(SM), spec(SM)),
         scratch_shapes=[
             pltpu.VMEM((2 * CAP, 4, WIN, WIDE), f32),
             pltpu.SemaphoreType.DMA((2 * CAP,)),
             pltpu.SemaphoreType.DMA((CAP,)),
         ],
+        cost_estimate=CHEAP,
         compiler_params=vmem(24),
     )(flag, own, before, field, maps)
-    out_from_b = move(to_a, back(across))
+    out_from = move(outer, across + back(across))
     in_from = move(inner, within + back(within))
 
     forms, shuffle = (jnp.asarray(t) for t in make_tables())
@@ -713,13 +695,14 @@
         in_specs=[spec(VM)] * 2,
         out_specs=spec(VM),
         scratch_shapes=[pltpu.VMEM((2, WIN, LANES), f32)],
+        cost_estimate=CHEAP,
         compiler_params=vmem(8),
     )(jnp.stack([jnp.cos(prop_phase), jnp.sin(prop_phase)]), shuffle)
 
     args = (field, intensity, probe_wave, kernel, (forms, shuffle))
     in_back, tiles_in = run_slots(True, role_in, table_in, *args, in_from, in_from)
     in_back = move(in_back, within + back(within))
-    out_back_a, out_back_b, tiles_out = run_slots(False, role_out, table_out, *args, out_from_b, out_from_a)
+    out_back_a, out_back_b, tiles_out = run_slots(False, role_out, table_out, *args, out_from, out_from)
     out_a = move(out_back_a, across)
     out_b = move(out_back_b, back(across))
     total = pl.pallas_call(
@@ -733,19 +716,21 @@
             pltpu.SemaphoreType.DMA,
             pltpu.SemaphoreType.DMA((2 * CAP,)),
         ],
+        cost_estimate=CHEAP,
         compiler_params=vmem(20),
     )(role_in, table_in, role_out, table_out, in_back, tiles_in, tiles_out)
     grad = pl.pallas_call(
         finish_kernel,
         out_shape=jax.ShapeDtypeStruct(field.shape, f32),
         in_specs=[spec(SM)] * 2 + [spec(VM)] + [spec(pl.ANY)] * 2,
-        out_specs=spec(pl.ANY),
+        out_specs=spec(HB),
         scratch_shapes=[
             pltpu.VMEM(field.shape, f32),
             pltpu.VMEM((CAP_BACK_A, 4, SUB, WIN), f32),
             pltpu.SemaphoreType.DMA,
             pltpu.SemaphoreType.DMA((4,)),
         ],
+        cost_estimate=CHEAP,
         compiler_params=vmem(16),
     )(role_out, table_out, total, out_a, out_b)
     return grad.reshape(obj_field.shape)

time: 109 us -> 103 us (0.945)
  the two profiles are of different devices: /device:TPU:20 before, /device:TPU:12 now
where the time goes in v6:
time: 103 us
  waiting for transfers between devices  50.5 us (49%)
  Pallas kernels  32.4 us (31%)
  starting transfers between devices  13.5 us (13%)
  local copies, waits for them, and re-layouts  5.96 us (6%)
    ppermute x6, waiting for transfers between devices, shards(): move = lambda x, pairs: lax.ppermute(x, 'row', pairs)  50.5 us
    pallas_call x2, Pallas kernels, run_slots(): pl.pallas_call(functools.partial(slots_kernel, joint), out_shape=tuple((p...  23.6 us
    ppermute x6, starting transfers between devices, shards(): move = lambda x, pairs: lax.ppermute(x, 'row', pairs)  13.5 us
    unnamed x17, local copies, waits for them, and re-layouts  4.91 us
    pallas_call x1, Pallas kernels, shards(): pl.pallas_call(sum_kernel, out_shape=jax.ShapeDtypeStruct(field.shape, f3...  2.85 us
    pallas_call x1, Pallas kernels, shards(): pl.pallas_call(finish_kernel, out_shape=jax.ShapeDtypeStruct(field.shape,...  2.8 us
    pallas_call x1, Pallas kernels, shards(): pl.pallas_call(pack_kernel, out_shape=(packed(CAP_FWD), packed(CAP_FWD),...  2.73 us
  transfers between devices with their start and end apart: 6, of which 4 were waited for; matrix products, arithmetic and copies ran while one was open for 1% of the time, Pallas kernels for 26%

profile of v6, /device:TPU:12, one launch (start us, length us, event | category | flops | bytes accessed | tf_op | source)
XLA Modules:
  0.0 103.4 jit_solution(9184055918439921011)
XLA Ops:
  0.7 0.8 copy.10
  1.4 0.1 reshape.21
  1.5 0.1 pad_add_fusion.own
  1.6 1.9 %collective-permute-start = (s32[16]{0:T(128)S(1)}, s32[16]{0:T(128)S(1)}, u32[]{:S(2)}, u32[]{:S(2)}) collective-permute-start(s32[16]{0:T(128)S(1)} %pad_add_fusion.own), channel_id=1, source_target_pairs={{0,1},{2,3},{4,5},{6,7},{8,9},{10,11},{12,13},{14,15},{1,2},{3,4},... | collective-permute-start | bytes 200 | tf_op jit(solution)/shard_map/ppermute | solution.py:664
  3.5 2.9 %collective-permute-done.before = s32[16]{0:T(128)S(1)} collective-permute-done((s32[16]{0:T(128)S(1)}, s32[16]{0:T(128)S(1)}, u32[]{:S(2)}, u32[]{:S(2)}) %collective-permute-start) | collective-permute-done | bytes 96 | tf_op jit(solution)/shard_map/ppermute | solution.py:664
  6.4 2.7 %shard_map.82 = (f32[48,4,8,256]{3,2,1,0:T(8,128)}, f32[48,4,8,256]{3,2,1,0:T(8,128)}, s32[32]{0:T(128)S(1)}, s32[32]{0:T(128)S(1)}) custom-call(s32[1]{0:T(128)} %bitcast.1.odd.role.role_in, s32[16]{0:T(128)S(1)} %pad_add_fusion.own, s32[16]{0:T(128)S(1)} %collective-permute-done.before, f32[4,256,1024]{2,1,0:T(8,128)} %bitcast.9, f32[4,8,4,8,256]{4,3,2,1,0:T(8,128)} %bitcast.12), custom_call_target="tpu_custom_call" | custom-call | flops 1 | bytes 1 | tf_op jit(solution)/shard_map/pallas_call | solution.py:675
  9.2 1.4 %collective-permute-start.1 = (f32[48,4,8,256]{3,2,1,0:T(8,128)}, f32[48,4,8,256]{3,2,1,0:T(8,128)S(1)}, u32[]{:S(2)}, u32[]{:S(2)}) collective-permute-start(f32[48,4,8,256]{3,2,1,0:T(8,128)} %get-tuple-element.16), channel_id=1, source_target_pairs={{0,1},{2,3},{4,5},{6,7},{8,9},{10,11},{12,13},{14,15},{1,0},{3,2},... | collective-permute-start | bytes 4718600 | tf_op jit(solution)/shard_map/ppermute | solution.py:664
  10.5 4.4 %collective-permute-start.3 = (f32[48,4,8,256]{3,2,1,0:T(8,128)}, f32[48,4,8,256]{3,2,1,0:T(8,128)S(1)}, u32[]{:S(2)}, u32[]{:S(2)}) collective-permute-start(f32[48,4,8,256]{3,2,1,0:T(8,128)} %get-tuple-element.19), channel_id=1, source_target_pairs={{1,2},{3,4},{5,6},{7,8},{9,10},{11,12},{13,14},{2,1},{4,3},{6,5},{... | collective-permute-start | bytes 4718600 | tf_op jit(solution)/shard_map/ppermute | solution.py:664
  15.0 1.0 cosine_bitcast_fusion
  16.0 0.4 shard_map.83.kernel
  16.4 0.8 copy-done
  17.2 1.0 %copy-done.1 = f32[2,256,256]{2,1,0:T(8,128)S(1)} copy-done((f32[2,256,256]{2,1,0:T(8,128)S(1)}, f32[2,256,256]{2,1,0:T(8,128)}, u32[]{:S(2)}) %copy-start.1) | copy-done | bytes 524312
  18.3 1.2 %copy-done.3 = bf16[4,2,256,256]{3,2,1,0:T(8,128)(2,1)S(1)} copy-done((bf16[4,2,256,256]{3,2,1,0:T(8,128)(2,1)S(1)}, bf16[4,2,256,256]{3,2,1,0:T(8,128)(2,1)}, u32[]{:S(2)}) %copy-start.3) | copy-done | bytes 1048600
  19.5 1.0 %copy-done.5 = f32[2,256,256]{2,1,0:T(8,128)S(1)} copy-done((f32[2,256,256]{2,1,0:T(8,128)S(1)}, f32[2,256,256]{2,1,0:T(8,128)}, u32[]{:S(2)}) %copy-start.5) | copy-done | bytes 524312
  20.6 11.8 %shard_map.84 = (f32[48,4,8,256]{3,2,1,0:T(8,128)S(1)}, f32[4,4,256,256]{3,2,1,0:T(8,128)S(1)}) custom-call(s32[1]{0:T(128)} %bitcast.1.odd.role.role_in, s32[32]{0:T(128)S(1)} %get-tuple-element.15.table.table_in, f32[4,256,1024]{2,1,0:T(8,128)} %bitcast.10, f32[4,256,256]{2,1,0:T(8,128)} %intensity.3, f32[2,256,256]{2,1,0:T(8,128)S(1)} %copy-done.5, ...), custom_call_target="tpu_custom_call" | custom-call | flops 1 | bytes 1 | tf_op jit(solution)/shard_map/pallas_call | solution.py:633
  32.4 0.1 collective-permute-start.2
  32.4 34.5 %collective-permute-done.3.from_b.from_a = f32[48,4,8,256]{3,2,1,0:T(8,128)S(1)} collective-permute-done((f32[48,4,8,256]{3,2,1,0:T(8,128)}, f32[48,4,8,256]{3,2,1,0:T(8,128)S(1)}, u32[]{:S(2)}, u32[]{:S(2)}) %collective-permute-start.3) | collective-permute-done | bytes 1572896 | tf_op jit(solution)/shard_map/ppermute | solution.py:664
  66.9 11.8 %shard_map.85 = (f32[48,4,8,256]{3,2,1,0:T(8,128)S(1)}, f32[32,4,8,256]{3,2,1,0:T(8,128)S(1)}, f32[4,4,256,256]{3,2,1,0:T(8,128)S(1)}) custom-call(s32[1]{0:T(128)} %bitcast.role.role_out, s32[32]{0:T(128)S(1)} %get-tuple-element.14.table.table_out, f32[4,256,1024]{2,1,0:T(8,128)} %bitcast.11, f32[4,256,256]{2,1,0:T(8,128)} %intensity.3, ...), custom_call_target="tpu_custom_call" | custom-call | flops 1 | bytes 1 | tf_op jit(solution)/shard_map/pallas_call | solution.py:633
  78.7 1.3 %collective-permute-start.4 = (f32[48,4,8,256]{3,2,1,0:T(8,128)S(1)}, f32[48,4,8,256]{3,2,1,0:T(8,128)S(1)}, u32[]{:S(2)}, u32[]{:S(2)}) collective-permute-start(f32[48,4,8,256]{3,2,1,0:T(8,128)S(1)} %get-tuple-element.21), channel_id=1, source_target_pairs={{1,2},{3,4},{5,6},{7,8},{9,10},{11,12},{13,14},{17,18},{19,20},{21... | collective-permute-start | bytes 4718600 | tf_op jit(solution)/shard_map/ppermute | solution.py:664
  80.0 4.4 %collective-permute-start.5 = (f32[32,4,8,256]{3,2,1,0:T(8,128)S(1)}, f32[32,4,8,256]{3,2,1,0:T(8,128)S(1)}, u32[]{:S(2)}, u32[]{:S(2)}) collective-permute-start(f32[32,4,8,256]{3,2,1,0:T(8,128)S(1)} %get-tuple-element.22), channel_id=1, source_target_pairs={{2,1},{4,3},{6,5},{8,7},{10,9},{12,11},{14,13},{18,17},{20,19},{22... | collective-permute-start | bytes 3145736 | tf_op jit(solution)/shard_map/ppermute | solution.py:664
  84.5 2.8 %shard_map.86.total_in = f32[4,256,1024]{2,1,0:T(8,128)S(1)} custom-call(s32[1]{0:T(128)} %bitcast.1.odd.role.role_in, s32[32]{0:T(128)S(1)} %get-tuple-element.15.table.table_in, s32[1]{0:T(128)} %bitcast.role.role_out, s32[32]{0:T(128)S(1)} %get-tuple-element.14.table.table_out, f32[48,4,8,256]{3,2,1,0:T(8,128)S(1)} %collective-permute-done.2.in_back, ...), custom_call_target="tpu_custom_call" | custom-call | flops 1 | bytes 1 | tf_op jit(solution)/shard_map/pallas_call | solution.py:708
  87.3 9.4 %collective-permute-done.5.out_b = f32[32,4,8,256]{3,2,1,0:T(8,128)S(1)} collective-permute-done((f32[32,4,8,256]{3,2,1,0:T(8,128)S(1)}, f32[32,4,8,256]{3,2,1,0:T(8,128)S(1)}, u32[]{:S(2)}, u32[]{:S(2)}) %collective-permute-start.5) | collective-permute-done | bytes 1048608 | tf_op jit(solution)/shard_map/ppermute | solution.py:664
  96.7 3.8 %collective-permute-done.4.out_a = f32[48,4,8,256]{3,2,1,0:T(8,128)S(1)} collective-permute-done((f32[48,4,8,256]{3,2,1,0:T(8,128)S(1)}, f32[48,4,8,256]{3,2,1,0:T(8,128)S(1)}, u32[]{:S(2)}, u32[]{:S(2)}) %collective-permute-start.4) | collective-permute-done | bytes 1572896 | tf_op jit(solution)/shard_map/ppermute | solution.py:664
  100.4 2.8 %shard_map.87 = f32[4,256,1024]{2,1,0:T(8,128)} custom-call(s32[1]{0:T(128)} %bitcast.role.role_out, s32[32]{0:T(128)S(1)} %get-tuple-element.14.table.table_out, f32[4,256,1024]{2,1,0:T(8,128)S(1)} %shard_map.86.total_in, f32[48,4,8,256]{3,2,1,0:T(8,128)S(1)} %collective-permute-done.4.out_a, f32[32,4,8,256]{3,2,1,0:T(8,128)S(1)} %collective-permute-done.5.out_b), custom_call_target="tpu_custom_call" | custom-call | flops 1 | bytes 1 | tf_op jit(solution)/shard_map/pallas_call | solution.py:722
  (16 shorter events, 0.1 us)
Async XLA Ops:
  1.6 4.9 %collective-permute-start = (s32[16]{0:T(128)S(1)}, s32[16]{0:T(128)S(1)}, u32[]{:S(2)}, u32[]{:S(2)}) collective-permute-start(s32[16]{0:T(128)S(1)} %pad_add_fusion.own), channel_id=1, source_target_pairs={{0,1},{2,3},{4,5},{6,7},{8,9},{10,11},{12,13},{14,15},{1,2},{3,4},... | collective-permute-start | bytes 200 | tf_op jit(solution)/shard_map/ppermute | solution.py:664
  6.4 8.5 %copy-start.7 = (f32[256,256]{1,0:T(8,128)S(1)}, f32[256,256]{1,0:T(8,128)}, u32[]{:S(2)}) copy-start(f32[256,256]{1,0:T(8,128)} %param.10) | copy-start | bytes 786436
  9.2 6.8 %copy-start.6 = (bf16[256,256]{1,0:T(8,128)(2,1)S(1)}, bf16[256,256]{1,0:T(8,128)(2,1)}, u32[]{:S(2)}) copy-start(bf16[256,256]{1,0:T(8,128)(2,1)} %constant.13.clone.shuffle) | copy-start | bytes 393220
  9.2 8.1 %collective-permute-start.1 = (f32[48,4,8,256]{3,2,1,0:T(8,128)}, f32[48,4,8,256]{3,2,1,0:T(8,128)S(1)}, u32[]{:S(2)}, u32[]{:S(2)}) collective-permute-start(f32[48,4,8,256]{3,2,1,0:T(8,128)} %get-tuple-element.16), channel_id=1, source_target_pairs={{0,1},{2,3},{4,5},{6,7},{8,9},{10,11},{12,13},{14,15},{1,0},{3,2},... | collective-permute-start | bytes 4718600 | tf_op jit(solution)/shard_map/ppermute | solution.py:664
  10.5 56.3 %collective-permute-start.3 = (f32[48,4,8,256]{3,2,1,0:T(8,128)}, f32[48,4,8,256]{3,2,1,0:T(8,128)S(1)}, u32[]{:S(2)}, u32[]{:S(2)}) collective-permute-start(f32[48,4,8,256]{3,2,1,0:T(8,128)} %get-tuple-element.19), channel_id=1, source_target_pairs={{1,2},{3,4},{5,6},{7,8},{9,10},{11,12},{13,14},{2,1},{4,3},{6,5},{... | collective-permute-start | bytes 4718600 | tf_op jit(solution)/shard_map/ppermute | solution.py:664
  16.4 0.8 copy-start
  17.2 1.0 %copy-start.1 = (f32[2,256,256]{2,1,0:T(8,128)S(1)}, f32[2,256,256]{2,1,0:T(8,128)}, u32[]{:S(2)}) copy-start(f32[2,256,256]{2,1,0:T(8,128)} %copy-done) | copy-start | bytes 1572868
  18.3 1.2 %copy-start.3 = (bf16[4,2,256,256]{3,2,1,0:T(8,128)(2,1)S(1)}, bf16[4,2,256,256]{3,2,1,0:T(8,128)(2,1)}, u32[]{:S(2)}) copy-start(bf16[4,2,256,256]{3,2,1,0:T(8,128)(2,1)} %constant.12.clone.forms) | copy-start | bytes 3145732
  19.5 1.0 %copy-start.5 = (f32[2,256,256]{2,1,0:T(8,128)S(1)}, f32[2,256,256]{2,1,0:T(8,128)}, u32[]{:S(2)}) copy-start(f32[2,256,256]{2,1,0:T(8,128)} %probe.3) | copy-start | bytes 1572868
  20.5 46.3 %copy-start.2 = (f32[2,256,256]{2,1,0:T(8,128)S(1)}, f32[2,256,256]{2,1,0:T(8,128)}, u32[]{:S(2)}) copy-start(f32[2,256,256]{2,1,0:T(8,128)} %copy-done) | copy-start | bytes 1572868
  20.6 46.3 %copy-start.4 = (bf16[4,2,256,256]{3,2,1,0:T(8,128)(2,1)S(1)}, bf16[4,2,256,256]{3,2,1,0:T(8,128)(2,1)}, u32[]{:S(2)}) copy-start(bf16[4,2,256,256]{3,2,1,0:T(8,128)(2,1)} %constant.12.clone.forms) | copy-start | bytes 3145732
  32.4 52.1 %collective-permute-start.2 = (f32[48,4,8,256]{3,2,1,0:T(8,128)S(1)}, f32[48,4,8,256]{3,2,1,0:T(8,128)S(1)}, u32[]{:S(2)}, u32[]{:S(2)}) collective-permute-start(f32[48,4,8,256]{3,2,1,0:T(8,128)S(1)} %get-tuple-element.17), channel_id=1, source_target_pairs={{0,1},{2,3},{4,5},{6,7},{8,9},{10,11},{12,13},{14,15},{1,0},{3,2},... | collective-permute-start | bytes 4718600 | tf_op jit(solution)/shard_map/ppermute | solution.py:664
  78.7 21.7 %collective-permute-start.4 = (f32[48,4,8,256]{3,2,1,0:T(8,128)S(1)}, f32[48,4,8,256]{3,2,1,0:T(8,128)S(1)}, u32[]{:S(2)}, u32[]{:S(2)}) collective-permute-start(f32[48,4,8,256]{3,2,1,0:T(8,128)S(1)} %get-tuple-element.21), channel_id=1, source_target_pairs={{1,2},{3,4},{5,6},{7,8},{9,10},{11,12},{13,14},{17,18},{19,20},{21... | collective-permute-start | bytes 4718600 | tf_op jit(solution)/shard_map/ppermute | solution.py:664
  80.0 16.7 %collective-permute-start.5 = (f32[32,4,8,256]{3,2,1,0:T(8,128)S(1)}, f32[32,4,8,256]{3,2,1,0:T(8,128)S(1)}, u32[]{:S(2)}, u32[]{:S(2)}) collective-permute-start(f32[32,4,8,256]{3,2,1,0:T(8,128)S(1)} %get-tuple-element.22), channel_id=1, source_target_pairs={{2,1},{4,3},{6,5},{8,7},{10,9},{12,11},{14,13},{18,17},{20,19},{22... | collective-permute-start | bytes 3145736 | tf_op jit(solution)/shard_map/ppermute | solution.py:664

commit v7 on v6

--- a/solution.py
+++ b/solution.py
@@ -15,9 +15,9 @@
 CAP = 4
 GROUPS = WIN // SUB
 INT_GROUPS = GROUPS // 4
-CAP_FWD = 48
-CAP_BACK_A = 48
-CAP_BACK_B = 32
+CAP_WIDE = 48
+CAP_NARROW = 28
+NARROW_SLOTS = 2
 UNEVEN = 24
 DEAD, AT_A, AT_B = 0, 1, 2
 FIELDS = 8
@@ -120,10 +120,11 @@
 INFO = 16
 
 
-def decide(info, table):
+def decide(info, table, first_slot, last_slot, cap):
     count = info[2 * CAP]
     rows = [jnp.bitwise_and(info[2 * j], WIN - 1) for j in range(CAP)]
-    used = [(j < count).astype(jnp.int32) for j in range(CAP)]
+    last_slot = jnp.minimum(last_slot, count)
+    used = [jnp.logical_and(j >= first_slot, j < last_slot).astype(jnp.int32) for j in range(CAP)]
     on_a = [used[j] * ((rows[j] + SUB - 1) // SUB) for j in range(CAP)]
     on_b = [used[j] * (GROUPS - rows[j] // SUB + INT_GROUPS) for j in range(CAP)]
     best, chosen = jnp.int32(10000), jnp.int32(0)
@@ -140,7 +141,7 @@
                 total_a = total_a + on_a[j]
                 slots_a = slots_a + used[j]
         cost = jnp.maximum(total_a, total_b)
-        cost = cost + jnp.where(cost > CAP_FWD, 1000, 0)
+        cost = cost + jnp.where(cost > cap, 1000, 0)
         cost = cost + jnp.where(jnp.maximum(slots_a, slots_b) > 2, UNEVEN, 0)
         better = cost < best
         best = jnp.where(better, cost, best)
@@ -259,23 +260,40 @@
             copy_groups(held, out, at, start, 0, (row + SUB - 1) // SUB, starts, shift)
 
 
-def pack_kernel(odd, own, before, field, intensity, inner, outer, table_in, table_out, held, sem, int_sem):
-    @pl.when(odd[0] == 0)
-    def _():
-        decide(before, table_out)
+def pack_kernel(
+    flags, own, before, field, intensity, inner, wide, narrow, table_in, table_out, held, sem, int_sem
+):
+    turn = flags[2]
+    is_narrow = flags[1] == 1
+    first_slot = jnp.where(is_narrow, NARROW_SLOTS * turn, CAP * turn)
+    last_slot = jnp.where(is_narrow, NARROW_SLOTS * (turn + 1), CAP)
+    cap = jnp.where(is_narrow, CAP_NARROW, CAP_WIDE)
+
+    def outward(pack):
+        @pl.when(is_narrow)
+        def _():
+            pack(narrow)
+
+        @pl.when(jnp.logical_not(is_narrow))
+        def _():
+            pack(wide)
+
+    @pl.when(flags[0] == 0)
+    def _():
+        decide(before, table_out, first_slot, last_slot, cap)
         fetch_columns(table_out, AT_A, field, held, sem, 0)
-        decide(own, table_in)
+        decide(own, table_in, CAP * turn, CAP, CAP_WIDE)
         fetch_columns(table_in, AT_B, field, held, sem, CAP)
-        pack_to_a(table_out, field, outer, held, sem, 0)
+        outward(lambda out: pack_to_a(table_out, field, out, held, sem, 0))
         pack_to_b(table_in, field, intensity, inner, held, sem, int_sem, CAP)
 
-    @pl.when(odd[0] == 1)
-    def _():
-        decide(own, table_out)
+    @pl.when(flags[0] == 1)
+    def _():
+        decide(own, table_out, first_slot, last_slot, cap)
         fetch_columns(table_out, AT_B, field, held, sem, 0)
-        decide(before, table_in)
+        decide(before, table_in, CAP * turn, CAP, CAP_WIDE)
         fetch_columns(table_in, AT_A, field, held, sem, CAP)
-        pack_to_b(table_out, field, intensity, outer, held, sem, int_sem, 0)
+        outward(lambda out: pack_to_b(table_out, field, intensity, out, held, sem, int_sem, 0))
         pack_to_a(table_in, field, inner, held, sem, CAP)
 
 
@@ -295,21 +313,38 @@
             out[plane, part * HALF : (part + 1) * HALF, :] = total
 
 
-def slots_kernel(joint, role, table, field, intensity, probe, kernel, forms, shuffle, from_b, from_a, *rest):
-    back_a, back_b = rest[0], rest[0 if joint else 1]
-    tiles, held, got, tile, measured, twice, beam, work, entered, chosen = rest[1 if joint else 2 : -4]
+def fetch_pieces(is_narrow, wide, narrow, got, sem):
+    @pl.when(is_narrow)
+    def _():
+        pltpu.make_async_copy(narrow, got.at[pl.ds(0, CAP_NARROW)], sem).start()
+
+    @pl.when(jnp.logical_not(is_narrow))
+    def _():
+        pltpu.make_async_copy(wide, got, sem).start()
+
+
+def await_pieces(is_narrow, wide, narrow, got, sem):
+    @pl.when(is_narrow)
+    def _():
+        pltpu.make_async_copy(narrow, got.at[pl.ds(0, CAP_NARROW)], sem).wait()
+
+    @pl.when(jnp.logical_not(is_narrow))
+    def _():
+        pltpu.make_async_copy(wide, got, sem).wait()
+
+
+def slots_kernel(between, flags, table, field, intensity, probe, kernel, forms, shuffle, wide, *rest):
+    narrow = rest[0] if between else wide
+    back_wide, back_narrow = (rest[1], rest[2]) if between else (rest[0], rest[0])
+    tiles, held, got, tile, measured, twice, beam, work, entered, chosen = rest[3 if between else 1 : -4]
     held_sem, int_sem, got_sem, tile_sem = rest[-4:]
-    is_a = role[0] == 0
+    is_a = flags[0] == (1 if between else 0)
+    is_narrow = jnp.logical_and(between, flags[1] == 1)
     mine = jnp.where(is_a, AT_A, AT_B)
-
-    @pl.when(is_a)
-    def _():
-        pltpu.make_async_copy(from_b, got, got_sem).start()
-
-    @pl.when(jnp.logical_not(is_a))
-    def _():
-        pltpu.make_async_copy(from_a, got, got_sem).start()
-
+    if between:
+        fetch_pieces(is_narrow, wide, narrow, got, got_sem)
+    else:
+        pltpu.make_async_copy(wide, got, got_sem).start()
     fetch_columns(table, mine, field, held, held_sem, 0)
 
     def intensity_copies(j):
@@ -343,7 +378,10 @@
             chosen[found] = j
 
         found = found + (state == mine).astype(jnp.int32)
-    pltpu.make_async_copy(from_b, got, got_sem).wait()
+    if between:
+        await_pieces(is_narrow, wide, narrow, got, got_sem)
+    else:
+        pltpu.make_async_copy(wide, got, got_sem).wait()
     sublane = lax.broadcasted_iota(jnp.int32, (SUB, LANES), 0)
 
     def load(m, j):
@@ -459,13 +497,21 @@
 
         tile_copy(m, j).start()
 
-        @pl.when(is_a)
-        def _():
-            lax.fori_loop(0, (row + SUB - 1) // SUB, send(back_a, back), 0)
-
-        @pl.when(jnp.logical_not(is_a))
-        def _():
-            lax.fori_loop(low, GROUPS, send(back_b, back - low), 0)
+        offset = jnp.where(is_a, back, back - low)
+        lower = jnp.where(is_a, 0, low)
+        upper = jnp.where(is_a, (row + SUB - 1) // SUB, GROUPS)
+        if between:
+
+            @pl.when(is_narrow)
+            def _():
+                lax.fori_loop(lower, upper, send(back_narrow, offset), 0)
+
+            @pl.when(jnp.logical_not(is_narrow))
+            def _():
+                lax.fori_loop(lower, upper, send(back_wide, offset), 0)
+
+        else:
+            lax.fori_loop(lower, upper, send(back_wide, offset), 0)
 
     def pair(p, carry):
         two = 2 * p + 1 < found
@@ -523,8 +569,7 @@
         tile_copy(1, 0).wait()
 
 
-def add_back(role, table, got, total, planes):
-    is_a = role[0] == 0
+def add_back(is_a, table, got, total, planes):
     theirs = jnp.where(is_a, AT_B, AT_A)
     for j in range(CAP):
         state, row, col, _, back = slot_of(table, j)
@@ -549,24 +594,32 @@
 
 
 def sum_kernel(
-    role_in, table_in, role_out, table_out, in_back, tiles_in, tiles_out, total, got, tile, got_sem, tile_sem
+    flags, table_in, table_out, in_back, tiles_in, tiles_out, grad, total, got, tile, got_sem, tile_sem, total_sem
 ):
     pltpu.make_async_copy(in_back, got, got_sem).start()
     sublane = lax.broadcasted_iota(jnp.int32, (SUB, LANES), 0)
-    kinds = ((role_in, table_in, tiles_in), (role_out, table_out, tiles_out))
-    for k, (role, table, tiles) in enumerate(kinds):
-        mine = jnp.where(role[0] == 0, AT_A, AT_B)
+    kinds = ((flags[0] == 0, table_in, tiles_in), (flags[0] == 1, table_out, tiles_out))
+    for k, (is_a, table, tiles) in enumerate(kinds):
+        mine = jnp.where(is_a, AT_A, AT_B)
         for j in range(CAP):
 
             @pl.when(table[FIELDS * j] == mine)
             def _():
                 pltpu.make_async_copy(tiles.at[j], tile.at[k * CAP + j], tile_sem.at[k * CAP + j]).start()
 
-    total[...] = jnp.zeros_like(total)
+    @pl.when(flags[2] == 0)
+    def _():
+        total[...] = jnp.zeros_like(total)
+
+    @pl.when(flags[2] > 0)
+    def _():
+        copy = pltpu.make_async_copy(grad, total, total_sem)
+        copy.start()
+        copy.wait()
+
     pltpu.make_async_copy(in_back, got, got_sem).wait()
-    add_back(role_in, table_in, got, total, range(4))
-    for k, (role, table, tiles) in enumerate(kinds):
-        is_a = role[0] == 0
+    add_back(flags[0] == 0, table_in, got, total, range(4))
+    for k, (is_a, table, tiles) in enumerate(kinds):
         mine = jnp.where(is_a, AT_A, AT_B)
         for j in range(CAP):
             state, row, col, _, _ = slot_of(table, j)
@@ -593,24 +646,13 @@
                 )
 
 
-def finish_kernel(role, table, total_in, out_a, out_b, grad, total, got, got_sem, out_sem):
-    is_a = role[0] == 0
-
-    @pl.when(is_a)
-    def _():
-        copy = pltpu.make_async_copy(out_b, got.at[pl.ds(0, CAP_BACK_B)], got_sem)
-        copy.start()
-        copy.wait()
-
-    @pl.when(jnp.logical_not(is_a))
-    def _():
-        copy = pltpu.make_async_copy(out_a, got, got_sem)
-        copy.start()
-        copy.wait()
-
+def finish_kernel(flags, table, total_in, wide, narrow, grad, total, got, got_sem, out_sem):
+    is_narrow = flags[1] == 1
+    fetch_pieces(is_narrow, wide, narrow, got, got_sem)
+    await_pieces(is_narrow, wide, narrow, got, got_sem)
     for plane in range(4):
         total[plane] = total_in[plane]
-        add_back(role, table, got, total, (plane,))
+        add_back(flags[0] == 1, table, got, total, (plane,))
         pltpu.make_async_copy(total.at[plane], grad.at[plane], out_sem.at[plane]).start()
     for plane in range(4):
         pltpu.make_async_copy(total.at[plane], grad.at[plane], out_sem.at[plane]).wait()
@@ -628,16 +670,17 @@
     return jax.ShapeDtypeStruct((groups, 4, SUB, WIN), f32)
 
 
-def run_slots(joint, role, table, field, intensity, probe, kernel, tables, from_b, from_a):
-    backs = (CAP_BACK_A,) if joint else (CAP_BACK_A, CAP_BACK_B)
+def run_slots(flags, table, field, intensity, probe, kernel, tables, *pieces):
+    between = len(pieces) == 2
+    backs = (CAP_WIDE, CAP_NARROW)[: len(pieces)]
     return pl.pallas_call(
-        functools.partial(slots_kernel, joint),
+        functools.partial(slots_kernel, between),
         out_shape=tuple(packed(n) for n in backs) + (jax.ShapeDtypeStruct((CAP, 4, WIN, WIN), f32),),
-        in_specs=[spec(SM)] * 2 + [spec(HB)] * 2 + [spec(VM)] * 4 + [spec(pl.ANY)] * 2,
+        in_specs=[spec(SM)] * 2 + [spec(HB)] * 2 + [spec(VM)] * 4 + [spec(pl.ANY)] * len(pieces),
         out_specs=(spec(VM),) * len(backs) + (spec(HB),),
         scratch_shapes=[
             pltpu.VMEM((CAP, 4, WIN, WIDE), f32),
-            pltpu.VMEM((CAP_FWD, 4, SUB, WIN), f32),
+            pltpu.VMEM((CAP_WIDE, 4, SUB, WIN), f32),
             pltpu.VMEM((2, 4, WIN, WIN), f32),
             pltpu.VMEM((CAP, 2, WIN, LANES), f32),
             pltpu.VMEM((4, 2 * WIN, LANES), f32),
@@ -652,31 +695,30 @@
         ],
         cost_estimate=CHEAP,
         compiler_params=vmem(32),
-    )(role, table, field, intensity, probe, kernel, *tables, from_b, from_a)
-
-
-def shards(obj_field, probe_wave, prop_phase, win_offsets, live_counts, intensity):
-    field = pltpu.with_memory_space_constraint(obj_field.reshape((4,) + obj_field.shape[2:]), HB)
+    )(flags, table, field, intensity, probe, kernel, *tables, *pieces)
+
+
+def both_ways(pairs):
+    return pairs + [(b, a) for a, b in pairs]
+
+
+def one_round(turn, grad, field, maps, intensity, probe_wave, prop_phase, own, before):
     count = lax.axis_size("row")
-    within = [(i, i + 1) for i in range(0, count - 1, 2)]
-    across = [(i, i + 1) for i in range(1, count - 1, 2)]
-    back = lambda pairs: [(b, a) for a, b in pairs]
+    within = both_ways([(i, i + 1) for i in range(0, count - 1, 2)])
+    wide_pairs = both_ways([(i, i + 1) for i in range(1, count - 1, 4)])
+    narrow_pairs = both_ways([(i, i + 1) for i in range(3, count - 1, 4)])
     move = lambda x, pairs: lax.ppermute(x, "row", pairs)
-    odd = jnp.bitwise_and(lax.axis_index("row"), 1)
-    role_in = odd.reshape(1)
-    role_out = (1 - odd).reshape(1)
-
-    flag = odd.reshape(1)
-    own = jnp.concatenate([win_offsets.reshape(-1), live_counts, jnp.zeros((INFO - 2 * CAP - 1,), jnp.int32)])
-    maps = pltpu.with_memory_space_constraint(intensity.reshape(CAP, INT_GROUPS, 4, SUB, WIN), HB)
-    intensity = pltpu.with_memory_space_constraint(intensity, HB)
-    before = move(own, within + across)
+    place = lax.axis_index("row")
+    odd = jnp.bitwise_and(place, 1)
+    is_narrow = (jnp.bitwise_and(place + 1, 2) == 0).astype(jnp.int32)
+    flags = jnp.stack([odd, is_narrow, turn])
+
     table = jax.ShapeDtypeStruct((CAP * FIELDS,), jnp.int32)
-    inner, outer, table_in, table_out = pl.pallas_call(
+    inner, wide, narrow, table_in, table_out = pl.pallas_call(
         pack_kernel,
-        out_shape=(packed(CAP_FWD), packed(CAP_FWD), table, table),
+        out_shape=(packed(CAP_WIDE), packed(CAP_WIDE), packed(CAP_NARROW), table, table),
         in_specs=[spec(SM)] * 3 + [spec(HB)] * 2,
-        out_specs=(spec(VM), spec(VM), spec(SM), spec(SM)),
+        out_specs=(spec(VM),) * 3 + (spec(SM),) * 2,
         scratch_shapes=[
             pltpu.VMEM((2 * CAP, 4, WIN, WIDE), f32),
             pltpu.SemaphoreType.DMA((2 * CAP,)),
@@ -684,9 +726,10 @@
         ],
         cost_estimate=CHEAP,
         compiler_params=vmem(24),
-    )(flag, own, before, field, maps)
-    out_from = move(outer, across + back(across))
-    in_from = move(inner, within + back(within))
+    )(flags, own, before, field, maps)
+    wide = move(wide, wide_pairs)
+    narrow = move(narrow, narrow_pairs)
+    inner = move(inner, within)
 
     forms, shuffle = (jnp.asarray(t) for t in make_tables())
     kernel = pl.pallas_call(
@@ -700,39 +743,64 @@
     )(jnp.stack([jnp.cos(prop_phase), jnp.sin(prop_phase)]), shuffle)
 
     args = (field, intensity, probe_wave, kernel, (forms, shuffle))
-    in_back, tiles_in = run_slots(True, role_in, table_in, *args, in_from, in_from)
-    in_back = move(in_back, within + back(within))
-    out_back_a, out_back_b, tiles_out = run_slots(False, role_out, table_out, *args, out_from, out_from)
-    out_a = move(out_back_a, across)
-    out_b = move(out_back_b, back(across))
+    in_back, tiles_in = run_slots(flags, table_in, *args, inner)
+    in_back = move(in_back, within)
+    back_wide, back_narrow, tiles_out = run_slots(flags, table_out, *args, wide, narrow)
+    back_wide = move(back_wide, wide_pairs)
+    back_narrow = move(back_narrow, narrow_pairs)
     total = pl.pallas_call(
         sum_kernel,
         out_shape=jax.ShapeDtypeStruct(field.shape, f32),
-        in_specs=[spec(SM)] * 4 + [spec(pl.ANY)] * 3,
+        in_specs=[spec(SM)] * 3 + [spec(pl.ANY)] * 3 + [spec(HB)],
         out_specs=spec(VM),
         scratch_shapes=[
-            pltpu.VMEM((CAP_BACK_A, 4, SUB, WIN), f32),
+            pltpu.VMEM((CAP_WIDE, 4, SUB, WIN), f32),
             pltpu.VMEM((2 * CAP, 4, WIN, WIN), f32),
             pltpu.SemaphoreType.DMA,
             pltpu.SemaphoreType.DMA((2 * CAP,)),
+            pltpu.SemaphoreType.DMA,
         ],
         cost_estimate=CHEAP,
         compiler_params=vmem(20),
-    )(role_in, table_in, role_out, table_out, in_back, tiles_in, tiles_out)
-    grad = pl.pallas_call(
+    )(flags, table_in, table_out, in_back, tiles_in, tiles_out, grad)
+    return pl.pallas_call(
         finish_kernel,
         out_shape=jax.ShapeDtypeStruct(field.shape, f32),
         in_specs=[spec(SM)] * 2 + [spec(VM)] + [spec(pl.ANY)] * 2,
         out_specs=spec(HB),
         scratch_shapes=[
             pltpu.VMEM(field.shape, f32),
-            pltpu.VMEM((CAP_BACK_A, 4, SUB, WIN), f32),
+            pltpu.VMEM((CAP_WIDE, 4, SUB, WIN), f32),
             pltpu.SemaphoreType.DMA,
             pltpu.SemaphoreType.DMA((4,)),
         ],
         cost_estimate=CHEAP,
         compiler_params=vmem(16),
-    )(role_out, table_out, total, out_a, out_b)
+    )(flags, table_out, total, back_wide, back_narrow)
+
+
+def shards(obj_field, probe_wave, prop_phase, win_offsets, live_counts, intensity):
+    field = pltpu.with_memory_space_constraint(obj_field.reshape((4,) + obj_field.shape[2:]), HB)
+    maps = pltpu.with_memory_space_constraint(intensity.reshape(CAP, INT_GROUPS, 4, SUB, WIN), HB)
+    intensity = pltpu.with_memory_space_constraint(intensity, HB)
+    count = lax.axis_size("row")
+    own = jnp.concatenate([win_offsets.reshape(-1), live_counts, jnp.zeros((INFO - 2 * CAP - 1,), jnp.int32)])
+    before = lax.ppermute(own, "row", [(i, i + 1) for i in range(count - 1)])
+    narrow_first = jnp.bitwise_and(lax.axis_index("row"), 3) == 3
+    left_over = jnp.logical_and(narrow_first, live_counts[0] > NARROW_SLOTS).astype(jnp.int32)
+
+    def body(state):
+        turn, _, grad = state
+        again = lax.pmax(left_over * (1 - turn), ("groups", "row"))
+        grad = one_round(turn, grad, field, maps, intensity, probe_wave, prop_phase, own, before)
+        return turn + 1, again, grad
+
+    empty = pl.pallas_call(
+        lambda out: None,
+        out_shape=jax.ShapeDtypeStruct(field.shape, f32),
+        out_specs=spec(HB),
+    )()
+    _, _, grad = lax.while_loop(lambda state: state[1] > 0, body, (jnp.int32(0), jnp.int32(1), empty))
     return grad.reshape(obj_field.shape)
 
 

time: 103 us -> 138 us (1.34)
  the two profiles are of different devices: /device:TPU:12 before, /device:TPU:0 now
where the time goes in v7:
time: 138 us; the launch traced here: 136 us
  blocking collectives  97.4 us (71%)
  Pallas kernels  14.4 us (10%)
  starting transfers between devices  11.2 us (8%)
  local copies, waits for them, and re-layouts  10.1 us (7%)
  waiting for transfers between devices  1.57 us (1%)
    pmax x1, blocking collectives, body(): again = lax.pmax(left_over * (1 - turn), ('groups', 'row'))  97.4 us
    ppermute x6, starting transfers between devices, one_round(): move = lambda x, pairs: lax.ppermute(x, 'row', pairs)  8.88 us
    while x8, local copies, waits for them, and re-layouts  8.28 us
    pallas_call x2, Pallas kernels, run_slots(): pl.pallas_call(functools.partial(slots_kernel, between), out_shape=tuple(...  6.51 us
    pallas_call x1, Pallas kernels, one_round(): pl.pallas_call(finish_kernel, out_shape=jax.ShapeDtypeStruct(field.shape,...  3.86 us
  transfers between devices with their start and end apart: 7, of which 1 were waited for; matrix products, arithmetic and copies ran while one was open for 1% of the time, Pallas kernels for 7%

profile of v7, /device:TPU:0, one launch (start us, length us, event | category | flops | bytes accessed | tf_op | source)
XLA Modules:
  0.0 136.3 jit_solution(6166688447213557347)
XLA Ops:
  0.7 0.8 copy.10
  1.5 0.1 reshape.22
  1.6 0.1 pad_add_fusion.1
  1.6 2.3 %collective-permute-start.6 = (s32[16]{0:T(128)S(1)}, s32[16]{0:T(128)S(1)}, u32[]{:S(2)}, u32[]{:S(2)}) collective-permute-start(s32[16]{0:T(128)S(1)} %pad_add_fusion.1), channel_id=1, source_target_pairs={{0,1},{1,2},{2,3},{3,4},{4,5},{5,6},{6,7},{7,8},{8,9},{9,10},{10,1... | collective-permute-start | bytes 200 | tf_op jit(solution)/shard_map/ppermute | solution.py:788
  4.0 1.0 cosine_bitcast_fusion
  5.1 1.2 body.14
  6.3 130.0 %while.15 = (s32[]{:T(128)}, s32[]{:T(128)}, f32[4,256,1024]{2,1,0:T(8,128)}, s32[]{:T(128)}, s32[16]{0:T(128)S(1)}, /*index=5*/s32[16]{0:T(128)S(1)}, f32[4,256...) while((s32[]{:T(128)}, s32[]{:T(128)}, ...), condition=%wide.region_2.0_spmd.clone, body=%wide.region_0.0_spmd.sunk.clone.sunk | while | flops 23 | bytes 99615352 | solution.py:803
  6.3 1.6 %body.15 = (f32[48,4,8,256]{3,2,1,0:T(8,128)S(1)}, f32[48,4,8,256]{3,2,1,0:T(8,128)S(1)}, f32[28,4,8,256]{3,2,1,0:T(8,128)S(1)}, s32[32]{0:T(128)S(1)}, s32[32]{0:T(128)S(1)}) custom-call(s32[3]{0:T(128)S(1)} %pad_add_fusion.3.flags, s32[16]{0:T(128)S(1)} %get-tuple-element.359.own, s32[16]{0:T(128)S(1)} %get-tuple-element.360.before, ...), custom_call_target="tpu_custom_call" | custom-call | flops 1 | bytes 1 | tf_op jit(solution)/shard_map/while/body/pallas_call | solution.py:717
  8.0 4.6 %collective-permute-start = (f32[48,4,8,256]{3,2,1,0:T(8,128)S(1)}, f32[48,4,8,256]{3,2,1,0:T(8,128)S(1)}, u32[]{:S(2)}, u32[]{:S(2)}) collective-permute-start(f32[48,4,8,256]{3,2,1,0:T(8,128)S(1)} %get-tuple-element.313), channel_id=1, source_target_pairs={{0,1},{2,3},{4,5},{6,7},{8,9},{10,11},{12,13},{14,15},{1,0},{3,2},... | collective-permute-start | bytes 4718600 | tf_op jit(solution)/shard_map/while/body/ppermute | solution.py:710
  12.6 0.7 collective-permute-start.2
  13.4 0.7 collective-permute-start.3
  14.1 1.6 %collective-permute-done.wide = f32[48,4,8,256]{3,2,1,0:T(8,128)S(1)} collective-permute-done((f32[48,4,8,256]{3,2,1,0:T(8,128)S(1)}, f32[48,4,8,256]{3,2,1,0:T(8,128)S(1)}, u32[]{:S(2)}, u32[]{:S(2)}) %collective-permute-start) | collective-permute-done | bytes 1572896 | tf_op jit(solution)/shard_map/while/body/ppermute | solution.py:710
  15.7 3.0 %body.16 = (f32[48,4,8,256]{3,2,1,0:T(8,128)}, f32[4,4,256,256]{3,2,1,0:T(8,128)S(1)}) custom-call(s32[3]{0:T(128)S(1)} %pad_add_fusion.3.flags, s32[32]{0:T(128)S(1)} %get-tuple-element.312.table.table_in, f32[4,256,1024]{2,1,0:T(8,128)} %get-tuple-element.361.field, f32[4,256,256]{2,1,0:T(8,128)} %get-tuple-element.363.intensity, ...), custom_call_target="tpu_custom_call" | custom-call | flops 1 | bytes 1 | tf_op jit(solution)/shard_map/while/body/pallas_call | solution.py:676
  18.7 1.9 %copy-done = f32[4,4,256,256]{3,2,1,0:T(8,128)} copy-done((f32[4,4,256,256]{3,2,1,0:T(8,128)}, f32[4,4,256,256]{3,2,1,0:T(8,128)S(1)}, u32[]{:S(2)}) %copy-start) | copy-done | bytes 4194328 | tf_op jit(solution)/shard_map/while
  20.7 0.4 collective-permute-start.1
  21.0 3.5 %body.17 = (f32[48,4,8,256]{3,2,1,0:T(8,128)}, f32[28,4,8,256]{3,2,1,0:T(8,128)}, f32[4,4,256,256]{3,2,1,0:T(8,128)S(1)}) custom-call(s32[3]{0:T(128)S(1)} %pad_add_fusion.3.flags, s32[32]{0:T(128)S(1)} %get-tuple-element.311.table.table_out, f32[4,256,1024]{2,1,0:T(8,128)} %get-tuple-element.361.field, f32[4,256,256]{2,1,0:T(8,128)} %get-tuple-element.363.intensity, ...), custom_call_target="tpu_custom_call" | custom-call | flops 1 | bytes 1 | tf_op jit(solution)/shard_map/while/body/pallas_call | solution.py:676
  24.5 2.0 %copy-done.2 = f32[4,4,256,256]{3,2,1,0:T(8,128)} copy-done((f32[4,4,256,256]{3,2,1,0:T(8,128)}, f32[4,4,256,256]{3,2,1,0:T(8,128)S(1)}, u32[]{:S(2)}) %copy-start.2) | copy-done | bytes 4194328 | tf_op jit(solution)/shard_map/while
  26.5 0.7 collective-permute-start.4
  27.2 1.7 %collective-permute-start.5 = (f32[28,4,8,256]{3,2,1,0:T(8,128)}, f32[28,4,8,256]{3,2,1,0:T(8,128)}, u32[]{:S(2)}, u32[]{:S(2)}) collective-permute-start(f32[28,4,8,256]{3,2,1,0:T(8,128)} %get-tuple-element.320), channel_id=1, source_target_pairs={{3,4},{7,8},{11,12},{4,3},{8,7},{12,11},{19,20},{23,24},{27,28},{2... | collective-permute-start | bytes 2752520 | tf_op jit(solution)/shard_map/while/body/ppermute | solution.py:710
  28.9 97.4 %pmax.12 = s32[]{:T(128)} all-reduce(s32[]{:T(128)S(6)} %mul.8), channel_id=1, replica_groups=mesh['groups'=2,'row'=16] {'groups','row'}, use_global_device_ids=true, to_apply=%region_1.0 | all-reduce | flops 1 | bytes 8 | tf_op jit(solution)/shard_map/while/body/pmax | solution.py:794
  126.3 2.2 %copy-done.1 = f32[4,4,256,256]{3,2,1,0:T(8,128)S(1)} copy-done((f32[4,4,256,256]{3,2,1,0:T(8,128)S(1)}, f32[4,4,256,256]{3,2,1,0:T(8,128)}, u32[]{:S(2)}) %copy-start.1) | copy-done | bytes 4194328 | tf_op jit(solution)/shard_map/while
  128.5 2.2 %copy-done.3 = f32[4,4,256,256]{3,2,1,0:T(8,128)S(1)} copy-done((f32[4,4,256,256]{3,2,1,0:T(8,128)S(1)}, f32[4,4,256,256]{3,2,1,0:T(8,128)}, u32[]{:S(2)}) %copy-start.3) | copy-done | bytes 4194328 | tf_op jit(solution)/shard_map/while
  130.7 1.2 body.18.total_in
  131.9 3.9 %body.19 = f32[4,256,1024]{2,1,0:T(8,128)} custom-call(s32[3]{0:T(128)S(1)} %pad_add_fusion.3.flags, s32[32]{0:T(128)S(1)} %get-tuple-element.311.table.table_out, f32[4,256,1024]{2,1,0:T(8,128)S(1)} %body.18.total_in, f32[48,4,8,256]{3,2,1,0:T(8,128)S(1)} %collective-permute-done.4.wide, f32[28,4,8,256]{3,2,1,0:T(8,128)} %collective-permute-done.5.narrow), custom_call_target="tpu_custom_call" | custom-call | flops 1 | bytes 1 | tf_op jit(solution)/shard_map/while/body/pallas_call | solution.py:766
  (18 shorter events, 0.1 us)
Async XLA Ops:
  0.0 5.1 %copy-start.4 = (bf16[256,256]{1,0:T(8,128)(2,1)S(1)}, bf16[256,256]{1,0:T(8,128)(2,1)}, u32[]{:S(2)}) copy-start(bf16[256,256]{1,0:T(8,128)(2,1)} %constant.42.clone.shuffle) | copy-start | bytes 393220
  0.0 4.0 %copy-start.5 = (f32[256,256]{1,0:T(8,128)S(1)}, f32[256,256]{1,0:T(8,128)}, u32[]{:S(2)}) copy-start(f32[256,256]{1,0:T(8,128)} %param.12) | copy-start | bytes 786436
  1.6 4.6 %collective-permute-start.6 = (s32[16]{0:T(128)S(1)}, s32[16]{0:T(128)S(1)}, u32[]{:S(2)}, u32[]{:S(2)}) collective-permute-start(s32[16]{0:T(128)S(1)} %pad_add_fusion.1), channel_id=1, source_target_pairs={{0,1},{1,2},{2,3},{3,4},{4,5},{5,6},{6,7},{7,8},{8,9},{9,10},{10,1... | collective-permute-start | bytes 200 | tf_op jit(solution)/shard_map/ppermute | solution.py:788
  8.0 7.7 %collective-permute-start = (f32[48,4,8,256]{3,2,1,0:T(8,128)S(1)}, f32[48,4,8,256]{3,2,1,0:T(8,128)S(1)}, u32[]{:S(2)}, u32[]{:S(2)}) collective-permute-start(f32[48,4,8,256]{3,2,1,0:T(8,128)S(1)} %get-tuple-element.313), channel_id=1, source_target_pairs={{0,1},{2,3},{4,5},{6,7},{8,9},{10,11},{12,13},{14,15},{1,0},{3,2},... | collective-permute-start | bytes 4718600 | tf_op jit(solution)/shard_map/while/body/ppermute | solution.py:710
  12.6 8.4 %collective-permute-start.2 = (f32[48,4,8,256]{3,2,1,0:T(8,128)S(1)}, f32[48,4,8,256]{3,2,1,0:T(8,128)S(1)}, u32[]{:S(2)}, u32[]{:S(2)}) collective-permute-start(f32[48,4,8,256]{3,2,1,0:T(8,128)S(1)} %get-tuple-element.316), channel_id=1, source_target_pairs={{1,2},{5,6},{9,10},{13,14},{2,1},{6,5},{10,9},{14,13},{17,18},{21,... | collective-permute-start | bytes 4718600 | tf_op jit(solution)/shard_map/while/body/ppermute | solution.py:710
  13.4 7.7 %collective-permute-start.3 = (f32[28,4,8,256]{3,2,1,0:T(8,128)S(1)}, f32[28,4,8,256]{3,2,1,0:T(8,128)S(1)}, u32[]{:S(2)}, u32[]{:S(2)}) collective-permute-start(f32[28,4,8,256]{3,2,1,0:T(8,128)S(1)} %get-tuple-element.317), channel_id=1, source_target_pairs={{3,4},{7,8},{11,12},{4,3},{8,7},{12,11},{19,20},{23,24},{27,28},{2... | collective-permute-start | bytes 2752520 | tf_op jit(solution)/shard_map/while/body/ppermute | solution.py:710
  18.7 2.0 %copy-start = (f32[4,4,256,256]{3,2,1,0:T(8,128)}, f32[4,4,256,256]{3,2,1,0:T(8,128)S(1)}, u32[]{:S(2)}) copy-start(f32[4,4,256,256]{3,2,1,0:T(8,128)S(1)} %get-tuple-element.315.tiles_in) | copy-start | bytes 12582916 | tf_op jit(solution)/shard_map/while
  20.7 105.6 %collective-permute-start.1 = (f32[48,4,8,256]{3,2,1,0:T(8,128)}, f32[48,4,8,256]{3,2,1,0:T(8,128)S(1)}, u32[]{:S(2)}, u32[]{:S(2)}) collective-permute-start(f32[48,4,8,256]{3,2,1,0:T(8,128)} %get-tuple-element.314), channel_id=1, source_target_pairs={{0,1},{2,3},{4,5},{6,7},{8,9},{10,11},{12,13},{14,15},{1,0},{3,2},... | collective-permute-start | bytes 4718600 | tf_op jit(solution)/shard_map/while/body/ppermute | solution.py:710
  24.5 2.0 %copy-start.2 = (f32[4,4,256,256]{3,2,1,0:T(8,128)}, f32[4,4,256,256]{3,2,1,0:T(8,128)S(1)}, u32[]{:S(2)}) copy-start(f32[4,4,256,256]{3,2,1,0:T(8,128)S(1)} %get-tuple-element.318.tiles_out) | copy-start | bytes 12582916 | tf_op jit(solution)/shard_map/while
  26.5 105.4 %collective-permute-start.4 = (f32[48,4,8,256]{3,2,1,0:T(8,128)}, f32[48,4,8,256]{3,2,1,0:T(8,128)S(1)}, u32[]{:S(2)}, u32[]{:S(2)}) collective-permute-start(f32[48,4,8,256]{3,2,1,0:T(8,128)} %get-tuple-element.319), channel_id=1, source_target_pairs={{1,2},{5,6},{9,10},{13,14},{2,1},{6,5},{10,9},{14,13},{17,18},{21,... | collective-permute-start | bytes 4718600 | tf_op jit(solution)/shard_map/while/body/ppermute | solution.py:710
  27.2 104.6 %collective-permute-start.5 = (f32[28,4,8,256]{3,2,1,0:T(8,128)}, f32[28,4,8,256]{3,2,1,0:T(8,128)}, u32[]{:S(2)}, u32[]{:S(2)}) collective-permute-start(f32[28,4,8,256]{3,2,1,0:T(8,128)} %get-tuple-element.320), channel_id=1, source_target_pairs={{3,4},{7,8},{11,12},{4,3},{8,7},{12,11},{19,20},{23,24},{27,28},{2... | collective-permute-start | bytes 2752520 | tf_op jit(solution)/shard_map/while/body/ppermute | solution.py:710
  126.3 2.2 %copy-start.1 = (f32[4,4,256,256]{3,2,1,0:T(8,128)S(1)}, f32[4,4,256,256]{3,2,1,0:T(8,128)}, u32[]{:S(2)}) copy-start(f32[4,4,256,256]{3,2,1,0:T(8,128)} %copy-done) | copy-start | bytes 12582916 | tf_op jit(solution)/shard_map/while
  128.5 2.2 %copy-start.3 = (f32[4,4,256,256]{3,2,1,0:T(8,128)S(1)}, f32[4,4,256,256]{3,2,1,0:T(8,128)}, u32[]{:S(2)}) copy-start(f32[4,4,256,256]{3,2,1,0:T(8,128)} %copy-done.2) | copy-start | bytes 12582916 | tf_op jit(solution)/shard_map/while
